TPU v7x, 32 devices: a whole 2x2x4 slice. The times are simulated.
32 devices in a mesh: ctx: 8 (over z, y), dp: 4 (over x, core).
Axes of the slice: x: 2, y: 2, z: 4, core: 2. Of those that a mesh axis runs over, the one named last changes fastest.
Arguments:
- queries: bfloat16 [4, 4096, 512], P('dp', 'ctx'), may hold values from -40 to 40
- keys: bfloat16 [4, 4096, 512], P('dp', 'ctx'), may hold values from -40 to 40
- values: bfloat16 [4, 4096, 512], P('dp', 'ctx'), may hold values from -6 to 6
- segment_ids: int32 [4, 4096], P('dp', 'ctx'), may hold values from 0 to 7, never falling along the last dimension, each value on 1 to 1024 neighbouring positions
- out_grad: bfloat16 [4, 4096, 2048], P('dp', 'ctx'), may hold values from -6 to 6
- out_weight: bfloat16 [512, 2048], replicated, may hold values from -0.25 to 0.25
Outputs:
- query_grad: bfloat16 [4, 4096, 512], P('dp', 'ctx')
- key_grad: bfloat16 [4, 4096, 512], P('dp', 'ctx')
- value_grad: bfloat16 [4, 4096, 512], P('dp', 'ctx')
- weight_grad: float32 [512, 2048], P('ctx', 'dp')
Inputs may be any that keep to these rules, and one draw needn't show every extreme that they name: `segment_ids`: segment numbers never fall along a sequence; every segment holds 1 to 1024 positions, and some segment exactly 1024.
All inputs are finite; a program needn't handle non-finite values.
Results may differ from a plain program's by a relative error of at most 0.0096.
Values may be sent and summed in bfloat16 or wider, within the bound.
No kernel may reach another device: no remote copies, remote signals or barrier semaphores. Data moves between devices by JAX's collectives and lax.ppermute only.
A program may use at most 128 MiB of HBM per device.

v0:
```python
import functools

import jax
import jax.numpy as jnp
from jax import lax
from jax.experimental import pallas as pl
from jax.experimental.pallas import tpu as pltpu
from jax.sharding import PartitionSpec as P

HEAD_DIM = 64
TILE = 256
LANES = 128
TAG_LANES = 64
PIECES = 3
MASKED_SCORE = -1e30
SCALE = HEAD_DIM ** (-0.5)
F32 = jnp.float32
BF16 = jnp.bfloat16
PARAMS = pltpu.CompilerParams(vmem_limit_bytes=20 << 20)


def shift(x, by):
    size = lax.axis_size("ctx")
    pairs = [(i, i + by) for i in range(size) if 0 <= i + by < size]
    return lax.ppermute(x, "ctx", pairs)


def dot_t(a, b):
    return lax.dot_general(a, b, (((1,), (1,)), ((), ())), preferred_element_type=F32)


def dot(a, b):
    return jnp.dot(a, b, preferred_element_type=F32)


def lane_of(rows):
    return lax.broadcasted_iota(jnp.int32, (rows, LANES), 1)


def one_hot(tag_row):
    count = tag_row.shape[1]
    tag = lax.broadcasted_iota(jnp.int32, (LANES, count), 0) + 1
    hit = (tag_row.astype(F32) == tag.astype(F32)) & (tag <= TAG_LANES)
    return jnp.where(hit, 1.0, 0.0).astype(F32).T


def key_extra(tag_row):
    hot = one_hot(tag_row)
    lane = lane_of(hot.shape[0])
    return jnp.where(lane < TAG_LANES, (1.0 - hot) * MASKED_SCORE, 1.0).astype(BF16)


def pieces(x):
    out = []
    for _ in range(PIECES):
        part = x.astype(BF16).astype(F32)
        out.append(part)
        x = x - part
    return out


def own(lane, half):
    return (lane >= half * HEAD_DIM) & (lane < (half + 1) * HEAD_DIM)


def query_extra(stats, head):
    lane = lane_of(stats.shape[0])
    first = TAG_LANES + 2 * PIECES * head
    none = jnp.zeros_like(stats)
    tag_lse = (lane < TAG_LANES) | ((lane >= first) & (lane < first + PIECES))
    delta = (lane >= first + PIECES) & (lane < first + 2 * PIECES)
    return jnp.where(tag_lse, stats, none), jnp.where(delta, stats, none)


def wide(features, extra):
    return jnp.concatenate([features, extra], axis=1)


def lower(shape, by_query):
    a = lax.broadcasted_iota(jnp.int32, shape, 0)
    b = lax.broadcasted_iota(jnp.int32, shape, 1)
    return (b <= a) if by_query else (a <= b)


def forward_kernel(first_pair, q_ref, g_ref, kc, vc, ka, va, kb, vb, tc, ta, tb, *rest):
    before = rest[0] if first_pair else None
    o_ref, st_ref, xc, xa, xb, tag, rowed = rest[1 if first_pair else 0 :]
    step = pl.program_id(0)
    rows = q_ref.shape[0]

    @pl.when(step == 0)
    def _():
        xc[...] = key_extra(tc[...])
        xa[...] = key_extra(ta[0:1, :])
        xb[...] = key_extra(tb[0:1, :])
        tag[...] = one_hot(tc[...]).astype(BF16)
        rowed[...] = jnp.zeros_like(rowed)

    lane = lane_of(TILE)
    vt = {id(v): v[...].T for v in (va, vb, vc)}
    gt = g_ref[...].T.astype(F32)
    for base in range(0, rows, TILE):
        end = base + TILE
        spans = [(ka, va, xa, base, rows), (kb, vb, xb, 0, rows)]
        spans += [(kc, vc, xc, 0, base)] if base else []
        spans += [(kc, vc, xc, base, end)]
        q = q_ref[base:end, :] * SCALE
        for half in range(2):
            feats = slice(half * HEAD_DIM, (half + 1) * HEAD_DIM)
            qx = wide(jnp.where(own(lane, half), q, jnp.zeros_like(q)), tag[base:end, :])
            scores = [dot_t(wide(k[lo:hi, :], x[lo:hi, :]), qx) for k, v, x, lo, hi in spans]
            scores[-1] = jnp.where(lower((TILE, TILE), False), scores[-1], MASKED_SCORE)
            peak = functools.reduce(
                jnp.maximum, [jnp.max(s, axis=0, keepdims=True) for s in scores]
            )
            total = jnp.zeros((1, TILE), F32)
            acc = jnp.zeros((HEAD_DIM, TILE), F32)
            for s, (k, v, x, lo, hi) in zip(scores, spans):
                e = jnp.exp(s - peak)
                total = total + jnp.sum(e, axis=0, keepdims=True)
                acc = acc + dot(vt[id(v)][feats, lo:hi], e.astype(BF16))
            acc = acc / total
            o_ref[feats, base:end] = acc.astype(BF16)
            delta = jnp.sum(acc * gt[feats, base:end], axis=0, keepdims=True)
            first = TAG_LANES + 2 * PIECES * (2 * (step + first_pair) + half)
            for i, part in enumerate(pieces(-(peak + jnp.log(total))) + pieces(-delta)):
                rowed[pl.ds(first + i, 1), base:end] = part

    @pl.when(step == pl.num_programs(0) - 1)
    def _():
        was = tag[...] if before is None else before[...]
        st_ref[...] = (was.astype(F32) + rowed[...].T).astype(BF16)


def query_kernel(first_pair, q_ref, g_ref, st_ref, kc, vc, ka, va, kb, vb, tc, ta, tb, *rest):
    dq_ref, xc, xa, xb, acc = rest[1 if first_pair else 0 :]
    step = pl.program_id(0)
    rows = q_ref.shape[0]

    @pl.when(step == 0)
    def _():
        xc[...] = key_extra(tc[...])
        xa[...] = key_extra(ta[0:1, :])
        xb[...] = key_extra(tb[0:1, :])

    lane = lane_of(rows)
    q = q_ref[...] * SCALE
    g = g_ref[...]
    for half in range(2):
        mine = own(lane, half)
        for_score, for_grad = query_extra(st_ref[...], 2 * (step + first_pair) + half)
        qx = wide(jnp.where(mine, q, jnp.zeros_like(q)), for_score)
        gx = wide(jnp.where(mine, g, jnp.zeros_like(g)), for_grad)
        acc[...] = jnp.zeros_like(acc)
        for k, v, x, near in ((ka, va, xa, 0), (kb, vb, xb, 1), (kc, vc, xc, 2)):
            for lo in range(0, rows, TILE):
                hi = lo + TILE
                top = lo if near == 2 else 0
                end = hi if near == 0 else rows
                p = jnp.exp(dot_t(qx[top:end], wide(k[lo:hi, :], x[lo:hi, :])))
                if near == 2:
                    p = jnp.where(lower((end - top, TILE), True), p, 0.0)
                dp = dot_t(gx[top:end], wide(v[lo:hi, :], x[lo:hi, :]))
                acc[top:end, :] += dot((p * dp).astype(BF16), k[lo:hi, :])
        if half == 0:
            dq_ref[...] = (acc[...] * SCALE).astype(BF16)
        else:
            dq_ref[...] = jnp.where(mine, (acc[...] * SCALE).astype(BF16), dq_ref[...])


def key_kernel(first_pair, k_ref, v_ref, t_ref, qc, gc, sc, qd, gd, sd, qe, ge, se, *rest):
    dk_ref, dv_ref, x_ref, dk, dv = rest[2 if first_pair else 0 :]
    step = pl.program_id(0)
    rows = k_ref.shape[0]

    @pl.when(step == 0)
    def _():
        x_ref[...] = key_extra(t_ref[...])

    lane = lane_of(TILE)
    kx = wide(k_ref[...], x_ref[...])
    vx = wide(v_ref[...], x_ref[...])
    for half in range(2):
        dk[...] = jnp.zeros_like(dk)
        dv[...] = jnp.zeros_like(dv)
        mine = own(lane, half)
        for q_ref, g_ref, s_ref, near in ((qc, gc, sc, 2), (qd, gd, sd, 1), (qe, ge, se, 0)):
            for lo in range(0, rows, TILE):
                hi = lo + TILE
                top = lo if near == 0 else 0
                end = hi if near == 2 else rows
                q = q_ref[lo:hi, :] * SCALE
                g = g_ref[lo:hi, :]
                for_score, for_grad = query_extra(s_ref[lo:hi, :], 2 * (step + first_pair) + half)
                qx = wide(jnp.where(mine, q, jnp.zeros_like(q)), for_score)
                gx = wide(jnp.where(mine, g, jnp.zeros_like(g)), for_grad)
                p = jnp.exp(dot_t(kx[top:end], qx))
                if near == 2:
                    row = lax.broadcasted_iota(jnp.int32, p.shape, 0)
                    col = lax.broadcasted_iota(jnp.int32, p.shape, 1) + lo
                    p = jnp.where(row <= col, p, 0.0)
                dp = dot_t(vx[top:end], gx)
                dv[top:end, :] += dot(p.astype(BF16), g)
                dk[top:end, :] += dot((p * dp).astype(BF16), q)
        if half == 0:
            dk_ref[...] = dk[...].astype(BF16)
            dv_ref[...] = dv[...].astype(BF16)
        else:
            keep = own(lane_of(rows), half)
            dk_ref[...] = jnp.where(keep, dk[...].astype(BF16), dk_ref[...])
            dv_ref[...] = jnp.where(keep, dv[...].astype(BF16), dv_ref[...])


def lasting(microseconds):
    return pl.CostEstimate(flops=0, transcendentals=0, bytes_accessed=int(microseconds * 3.5e6))


class Attention:
    def __init__(self, rows, width, chunk, chunks):
        pairs = width // LANES // chunks
        self.first = chunk * pairs
        block = lambda off: pl.BlockSpec((rows, LANES), lambda p: (0, p + off))
        fixed = lambda shape, row: pl.BlockSpec(shape, lambda p: (row, 0))
        here, whole = self.first, width // LANES
        own_tag, far_tag = fixed((1, rows), 0), fixed((16, rows), rows // 16)
        self.stat = stat = fixed((rows, LANES), 0)
        self.sent = sent = [block(here), block(whole + here)]
        self.window = [block(here)] * 2 + [block(0), block(pairs)] * 2 + [own_tag, far_tag, far_tag]
        self.local = [block(here)] * 2 + [own_tag]
        self.out = block(here)
        self.extra = pltpu.VMEM((rows, LANES), BF16)
        self.total = pltpu.VMEM((rows, LANES), F32)
        self.rows, self.width, self.pairs = rows, width, pairs

    def call(self, kernel, in_specs, args, out_specs, out_shape, scratch, before=(), aliased=True, last=8):
        before = list(before)
        spec = pl.BlockSpec(memory_space=pl.ANY) if aliased else self.stat
        aliases = {len(args) + i: i for i in range(len(before))} if aliased else {}
        return pl.pallas_call(
            functools.partial(kernel, self.first), grid=(self.pairs,),
            in_specs=in_specs + [spec] * len(before), out_specs=out_specs,
            out_shape=[jax.ShapeDtypeStruct(s, BF16) for s in out_shape],
            scratch_shapes=scratch, input_output_aliases=aliases,
            compiler_params=PARAMS, cost_estimate=lasting(last), name=kernel.__name__,
        )(*args, *before)

    def forward(self, sent, window, before):
        return self.call(
            forward_kernel, self.sent + self.window, [sent, sent, *window],
            [pl.BlockSpec((LANES, self.rows), lambda p: (p, 0)), self.stat],
            [(self.pairs * LANES, self.rows), (self.rows, LANES)],
            [self.extra] * 4 + [pltpu.VMEM((LANES, self.rows), F32)], before, False,
        )

    def query(self, sent, stats, window, before):
        return self.call(
            query_kernel, self.sent + [self.stat] + self.window, [sent, sent, stats, *window],
            [self.out], [(self.rows, self.width)], [self.extra] * 3 + [self.total], before,
        )

    def key(self, local, sources, before):
        return self.call(
            key_kernel, self.local + (self.sent + [self.stat]) * 3, local + sources,
            [self.out] * 2, [(self.rows, self.width)] * 2, [self.extra] + [self.total] * 2, before,
        )


def send_kernel(q_ref, g_ref, w_ref, out_ref):
    half = pl.num_programs(0) // 2
    step = pl.program_id(0)

    @pl.when(step < half)
    def _():
        out_ref[...] = q_ref[...]

    @pl.when(step >= half)
    def _():
        out_ref[...] = dot_t(g_ref[...], w_ref[...]).astype(BF16)


def queries_to_send(query_rows, grad_rows, out_weight):
    rows, width = query_rows.shape
    model = grad_rows.shape[1]
    blocks = width // TILE
    return pl.pallas_call(
        send_kernel, grid=(2 * blocks,),
        in_specs=[
            pl.BlockSpec((rows, TILE), lambda i: (0, jnp.minimum(i, blocks - 1))),
            pl.BlockSpec((rows, model), lambda i: (0, 0)),
            pl.BlockSpec((TILE, model), lambda i: (jnp.maximum(i - blocks, 0), 0)),
        ],
        out_specs=pl.BlockSpec((rows, TILE), lambda i: (0, i)),
        out_shape=jax.ShapeDtypeStruct((rows, 2 * width), BF16),
        compiler_params=PARAMS, cost_estimate=lasting(5), name="queries_to_send",
    )(query_rows, grad_rows, out_weight)


def weight_kernel(sel_ref, *refs):
    outs, g_ref, w_ref = refs[:2], refs[2], refs[-1]
    size = outs[0].shape[0]
    for i, o_ref in enumerate(outs):
        part = dot(o_ref[...], g_ref[...])
        if len(refs) == 5:
            part = part + refs[3][0, i * size : (i + 1) * size, :].astype(F32)
        w_ref[0, i * size : (i + 1) * size, :] = part.astype(w_ref.dtype)


def weight_term(attn, grad_rows, columns, parts, got, dtype):
    size, rows = attn[0].shape
    width = size * len(attn)
    cols = grad_rows.shape[1] // parts
    steps = 1 if got is not None else parts // 2
    column = lambda i, s: (0, s[0] + 2 * i)
    extra = [] if got is None else [pl.BlockSpec((1, width, cols), lambda i, s: (s[1], 0, 0))]
    return pl.pallas_call(
        weight_kernel,
        grid_spec=pltpu.PrefetchScalarGridSpec(
            num_scalar_prefetch=1, grid=(steps,),
            in_specs=[pl.BlockSpec((size, rows), lambda i, s: (0, 0))] * 2
            + [pl.BlockSpec((rows, cols), column)] + extra,
            out_specs=pl.BlockSpec((1, width, cols), lambda i, s: (i, 0, 0)),
        ),
        out_shape=jax.ShapeDtypeStruct((steps, width, cols), dtype),
        compiler_params=PARAMS, cost_estimate=lasting(3), name="weight_term",
    )(columns, *attn, grad_rows, *([] if got is None else [got]))


def swap(x, axis, bit):
    return lax.ppermute(x, axis, [(i, i ^ bit) for i in range(lax.axis_size(axis))])


def after(x, *others):
    return lax.optimization_barrier((x,) + others)[0]


def weight_by_dp(attn, grad_rows):
    parts = lax.axis_size("dp")
    me = lax.axis_index("dp").astype(jnp.int32)
    core, chip = me % 2, me // 2
    pick = lambda part, entry: jnp.stack([part, entry])
    sent = weight_term(attn, grad_rows, pick(1 - core, core), parts, None, BF16)
    got = swap(sent, "dp", 1)
    sent = weight_term(attn, grad_rows, pick(2 * (1 - chip) + core, 1 - chip), parts, got, BF16)
    moved = swap(sent, "dp", 2)
    kept = weight_term(attn, grad_rows, pick(me, chip), parts, got, F32)
    return kept[0], moved[0]


def halves(total, got, axis, bit):
    split = lambda x: x.reshape((x.shape[0] // 2, 2) + x.shape[1:])
    total, got = split(total), split(got)
    mine = (lax.axis_index(axis) // bit) % 2
    take = lambda which: lax.dynamic_index_in_dim(
        total, which, 1, keepdims=False
    ) + lax.dynamic_index_in_dim(got, which, 1, keepdims=False).astype(F32)
    return take(1 - mine).astype(BF16), take(mine)


def on_device(queries, keys, values, segment_ids, out_grad, out_weight):
    query_rows, key_rows, value_rows, grad_rows = queries[0], keys[0], values[0], out_grad[0]
    rows, width = query_rows.shape
    chunks = 2
    size = width // chunks
    tags = segment_ids + 1
    tag_rows = jnp.pad(tags.astype(BF16), ((0, 15), (0, 2 * size - rows)))
    odd = lax.axis_index("ctx") % 2 == 1
    mine, far = [], []
    for i in range(chunks):
        cut = slice(i * size, (i + 1) * size)
        mine.append(
            jnp.concatenate(
                [jnp.concatenate([key_rows[:, cut], value_rows[:, cut]], axis=1), tag_rows], axis=0
            )
        )
        far.append(shift(mine[i], 2))
    sent = queries_to_send(after(query_rows, *mine), grad_rows, out_weight)
    far_sent = shift(sent, -2)
    far[0] = after(far[0], sent)
    near = []
    for i in range(chunks):
        passed = jnp.where(odd, far[i], mine[i])
        near.append(swap(passed, "ctx", 1))
        if i + 1 < chunks:
            far[i + 1] = after(far[i + 1], passed)
    parts = [Attention(rows, width, i, chunks) for i in range(chunks)]
    window = lambda i: [key_rows, value_rows, far[i], far[i], near[i], near[i], tags, far[i], near[i]]
    attn, stats = [], []
    from_forward = sent
    for i in range(chunks):
        half, after_half = parts[i].forward(from_forward, window(i), stats)
        attn.append(half)
        stats = [after_half]
        if i == 0:
            passed = jnp.where(odd, sent, after(far_sent, half))
            near_sent = swap(passed, "ctx", 1)
            from_forward = after(sent, passed)
    stats = stats[0]
    kept, moved = weight_by_dp(attn, grad_rows)
    near_stats = shift(stats, -1)
    far_stats = shift(stats, -2)
    settled = [stats, after(stats, near_stats, far_stats)]
    query_grad = []
    for i in range(chunks):
        query_grad = parts[i].query(sent, settled[i], window(i), query_grad)
    query_grad = query_grad[0]
    by_ctx = lambda x: x.reshape(count, width // count, x.shape[-1])
    count = lax.axis_size("ctx")
    kept, moved = by_ctx(kept), by_ctx(moved)
    key_value = []
    sources = [sent, sent, stats, near_sent, near_sent, near_stats, far_sent, far_sent, far_stats]
    bit = 1
    chunk = 0
    moved = after(moved, query_grad)
    while bit < count:
        send, kept = halves(kept, moved, "ctx", bit)
        moved = swap(send, "ctx", bit)
        if chunk < chunks:
            tied, send = lax.optimization_barrier((stats, send))
            sources[2] = tied
            key_value = parts[chunk].key([key_rows, value_rows, tags], sources, key_value)
            moved = after(moved, *key_value)
            chunk += 1
        bit *= 2
    weight_grad = kept[0] + moved[0].astype(F32)
    key_grad, value_grad = key_value
    return query_grad[None], key_grad[None], value_grad[None], weight_grad


def solution(mesh):
    rows = P("dp", "ctx", None)
    return jax.shard_map(
        on_device,
        mesh=mesh,
        in_specs=(rows, rows, rows, P("dp", "ctx"), rows, P()),
        out_specs=(rows, rows, rows, P("ctx", "dp")),
        check_vma=False,
    )
```

profile of v0, /device:TPU:0, one launch (start us, length us, event | category | flops | bytes accessed | tf_op | source)
XLA Modules:
  0.0 127.5 jit_solution(2477099969045786429)
XLA Ops:
  0.6 0.7 broadcast_add_fusion
  1.3 1.4 %fusion.9 = (bf16[512,256]{1,0:T(8,128)(2,1)S(1)}, bf16[512,256]{1,0:T(8,128)(2,1)S(1)}, bf16[512,256]{1,0:T(8,128)(2,1)S(1)}, bf16[512,256]{1,0:T(8,128)(2,1)S(1)}) fusion(bf16[512,512]{1,0:T(8,128)(2,1)} %bitcast.38, bf16[512,512]{1,0:T(8,128)(2,1)} %bitcast.45), kind=kLoop, calls=%fused_computation.23 | loop fusion | bytes 2097152 | tf_op jit(solution)/shard_map/slice | solution.py:372
  2.7 0.0 copy-start.12
  2.7 0.0 copy-start.14
  2.8 0.0 copy-start.15
  2.8 0.0 copy-start
  2.8 1.1 fusion.2
  3.8 5.9 %collective-permute-start.1 = (bf16[528,512]{1,0:T(8,128)(2,1)}, bf16[528,512]{1,0:T(8,128)(2,1)}, u32[]{:S(2)}, u32[]{:S(2)}) collective-permute-start(bf16[528,512]{1,0:T(8,128)(2,1)} %get-tuple-element.53), channel_id=1, source_target_pairs={{0,8},{4,12},{8,16},{12,20},{16,24},{20,28},{1,9},{5,13},{9,17},{1... | collective-permute-start | bytes 1622024 | tf_op jit(solution)/shard_map/ppermute | solution.py:25
  9.8 0.0 copy-start.11
  9.8 1.0 copy-done.11
  10.8 1.8 %queries_to_send.1.q_ref.g_ref.qc.gc = bf16[512,1024]{1,0:T(8,128)(2,1)S(1)} custom-call(bf16[512,512]{1,0:T(8,128)(2,1)S(1)} %bitcast.53, bf16[512,2048]{1,0:T(8,128)(2,1)S(1)} %bitcast.34, bf16[512,2048]{1,0:T(8,128)(2,1)S(1)} %copy-done.10), custom_call_target="tpu_custom_call" | custom-call | bytes 17500000 | tf_op jit(solution)/shard_map/queries_to_send/pallas_call | solution.py:285
  12.6 1.3 %collective-permute-start = (bf16[512,1024]{1,0:T(8,128)(2,1)S(1)}, bf16[512,1024]{1,0:T(8,128)(2,1)}, u32[]{:S(2)}, u32[]{:S(2)}) collective-permute-start(bf16[512,1024]{1,0:T(8,128)(2,1)S(1)} %queries_to_send.1.q_ref.g_ref.qc.gc), channel_id=1, source_target_pairs={{8,0},{12,4},{16,8},{20,12},{24,16},{28,20},{9,1},{13,5},{17,9},{2... | collective-permute-start | bytes 3145736 | tf_op jit(solution)/shard_map/ppermute | solution.py:25
  13.9 5.4 %collective-permute-start.3 = (bf16[528,512]{1,0:T(8,128)(2,1)}, bf16[528,512]{1,0:T(8,128)(2,1)}, u32[]{:S(2)}, u32[]{:S(2)}) collective-permute-start(bf16[528,512]{1,0:T(8,128)(2,1)} %get-tuple-element.52), channel_id=1, source_target_pairs={{0,8},{4,12},{8,16},{12,20},{16,24},{20,28},{1,9},{5,13},{9,17},{1... | collective-permute-start | bytes 1622024 | tf_op jit(solution)/shard_map/ppermute | solution.py:25
  19.2 2.6 %collective-permute-done.1.ka.va.ta = bf16[528,512]{1,0:T(8,128)(2,1)} collective-permute-done((bf16[528,512]{1,0:T(8,128)(2,1)}, bf16[528,512]{1,0:T(8,128)(2,1)}, u32[]{:S(2)}, u32[]{:S(2)}) %collective-permute-start.1) | collective-permute-done | bytes 540704 | tf_op jit(solution)/shard_map/ppermute | solution.py:25
  21.9 2.0 %broadcast_select_fusion.2 = bf16[528,512]{1,0:T(8,128)(2,1)} fusion(bf16[528,512]{1,0:T(8,128)(2,1)} %collective-permute-done.1.ka.va.ta, pred[]{:T(512)S(6)} %eq.9, bf16[1,512]{1,0:T(2,128)(2,1)S(1)} %get-tuple-element.51, bf16[512,256]{1,0:T(8,128)(2,1)} %copy-done.15, bf16[512,256]{1,0:T(8,128)(2,1)} %copy-done.14), kind=kLoop, calls=%fused_computation.6 | loop fusion | flops 2433024 | bytes 1606657 | tf_op jit(solution)/shard_map/jit(_where)/select_n | solution.py:381
  23.9 1.7 %collective-permute-start.2 = (bf16[528,512]{1,0:T(8,128)(2,1)}, bf16[528,512]{1,0:T(8,128)(2,1)}, u32[]{:S(2)}, u32[]{:S(2)}) collective-permute-start(bf16[528,512]{1,0:T(8,128)(2,1)} %broadcast_select_fusion.2), channel_id=1, source_target_pairs={{0,4},{4,0},{8,12},{12,8},{16,20},{20,16},{24,28},{28,24},{1,5},{5... | collective-permute-start | bytes 1622024 | tf_op jit(solution)/shard_map/ppermute | solution.py:329
  25.5 6.8 %collective-permute-done.3.ka.va.ta = bf16[528,512]{1,0:T(8,128)(2,1)} collective-permute-done((bf16[528,512]{1,0:T(8,128)(2,1)}, bf16[528,512]{1,0:T(8,128)(2,1)}, u32[]{:S(2)}, u32[]{:S(2)}) %collective-permute-start.3) | collective-permute-done | bytes 540704 | tf_op jit(solution)/shard_map/ppermute | solution.py:25
  32.3 0.0 copy-done.13
  32.3 0.9 broadcast_select_fusion.1
  33.3 2.6 %collective-permute-start.4 = (bf16[528,512]{1,0:T(8,128)(2,1)}, bf16[528,512]{1,0:T(8,128)(2,1)}, u32[]{:S(2)}, u32[]{:S(2)}) collective-permute-start(bf16[528,512]{1,0:T(8,128)(2,1)} %broadcast_select_fusion.1), channel_id=1, source_target_pairs={{0,4},{4,0},{8,12},{12,8},{16,20},{20,16},{24,28},{28,24},{1,5},{5... | collective-permute-start | bytes 1622024 | tf_op jit(solution)/shard_map/ppermute | solution.py:329
  35.8 0.1 pad_add_fusion.1.sel_ref
  35.9 0.4 collective-permute-done.2.kb.vb.tb
  36.3 1.0 copy-done.1
  37.4 1.0 copy-done.4
  38.4 7.2 %forward_kernel.2 = (bf16[256,512]{1,0:T(8,128)(2,1)S(1)}, bf16[512,128]{1,0:T(8,128)(2,1)S(1)}) custom-call(bf16[512,1024]{1,0:T(8,128)(2,1)S(1)} %queries_to_send.1.q_ref.g_ref.qc.gc, bf16[512,1024]{1,0:T(8,128)(2,1)S(1)} %queries_to_send.1.q_ref.g_ref.qc.gc, bf16[512,512]{1,0:T(8,128)(2,1)S(1)} %bitcast.39, bf16[512,512]{1,0:T(8,128)(2,1)S(1)} %bitcast.46, ...), custom_call_target="tpu_custom_call" | custom-call | bytes 28000000 | tf_op jit(solution)/shard_map/forward_kernel/pallas_call | solution.py:239
  45.6 0.0 collective-permute-done.qe.ge
  45.6 2.3 %broadcast_select_fusion = bf16[512,1024]{1,0:T(8,128)(2,1)} fusion(bf16[512,1024]{1,0:T(8,128)(2,1)S(1)} %queries_to_send.1.q_ref.g_ref.qc.gc, bf16[512,1024]{1,0:T(8,128)(2,1)} %collective-permute-done.qe.ge, pred[]{:T(512)S(6)} %eq.9), kind=kLoop, calls=%fused_computation.2 | loop fusion | flops 524288 | bytes 3145729 | tf_op jit(solution)/shard_map/jit(_where)/select_n | solution.py:394
  47.9 0.0 collective-permute-done.4.kb.vb.tb
  47.9 7.2 %forward_kernel.3 = (bf16[256,512]{1,0:T(8,128)(2,1)S(1)}, bf16[512,128]{1,0:T(8,128)(2,1)S(1)}) custom-call(bf16[512,1024]{1,0:T(8,128)(2,1)S(1)} %queries_to_send.1.q_ref.g_ref.qc.gc, bf16[512,1024]{1,0:T(8,128)(2,1)S(1)} %queries_to_send.1.q_ref.g_ref.qc.gc, bf16[512,512]{1,0:T(8,128)(2,1)S(1)} %bitcast.40, bf16[512,512]{1,0:T(8,128)(2,1)S(1)} %bitcast.47, ...), custom_call_target="tpu_custom_call" | custom-call | bytes 28000000 | tf_op jit(solution)/shard_map/forward_kernel/pallas_call | solution.py:239
  55.1 0.0 copy-start.7
  55.1 2.4 %weight_term.3 = bf16[2,512,512]{2,1,0:T(8,128)(2,1)} custom-call(s32[2]{0:T(128)S(1)} %pad_add_fusion.1.sel_ref, bf16[256,512]{1,0:T(8,128)(2,1)S(1)} %get-tuple-element.25.refs_0_, bf16[256,512]{1,0:T(8,128)(2,1)S(1)} %get-tuple-element.32.refs_1_, bf16[512,2048]{1,0:T(8,128)(2,1)S(1)} %bitcast.35), custom_call_target="tpu_custom_call" | custom-call | bytes 10500000 | tf_op jit(solution)/shard_map/weight_term/pallas_call | solution.py:315
  57.5 0.0 collective-permute-start.7
  57.5 1.5 %collective-permute-start.10 = (bf16[512,1024]{1,0:T(8,128)(2,1)}, bf16[512,1024]{1,0:T(8,128)(2,1)}, u32[]{:S(2)}, u32[]{:S(2)}) collective-permute-start(bf16[512,1024]{1,0:T(8,128)(2,1)} %broadcast_select_fusion), channel_id=1, source_target_pairs={{0,4},{4,0},{8,12},{12,8},{16,20},{20,16},{24,28},{28,24},{1,5},{5... | collective-permute-start | bytes 3145736 | tf_op jit(solution)/shard_map/ppermute | solution.py:329
  59.0 0.1 pad_add_fusion
  59.1 1.4 %collective-permute-done.7.refs_3_ = bf16[2,512,512]{2,1,0:T(8,128)(2,1)} collective-permute-done((bf16[2,512,512]{2,1,0:T(8,128)(2,1)}, bf16[2,512,512]{2,1,0:T(8,128)(2,1)}, u32[]{:S(2)}, u32[]{:S(2)}) %collective-permute-start.7) | collective-permute-done | bytes 1048608 | tf_op jit(solution)/shard_map/ppermute | solution.py:329
  60.5 0.9 copy-done.8
  61.4 2.9 %weight_term.5 = bf16[1,512,512]{2,1,0:T(8,128)(2,1)} custom-call(s32[2]{0:T(128)S(1)} %get-tuple-element.57.sel_ref, bf16[256,512]{1,0:T(8,128)(2,1)S(1)} %get-tuple-element.25.refs_0_, bf16[256,512]{1,0:T(8,128)(2,1)S(1)} %copy-done.8, bf16[512,2048]{1,0:T(8,128)(2,1)S(1)} %bitcast.36, bf16[2,512,512]{2,1,0:T(8,128)(2,1)} %collective-permute-done.7.refs_3_), custom_call_target="tpu_custom_call" | custom-call | bytes 10500000 | tf_op jit(solution)/shard_map/weight_term/pallas_call | solution.py:315
  64.3 1.5 %collective-permute-start.8 = (bf16[1,512,512]{2,1,0:T(8,128)(2,1)}, bf16[1,512,512]{2,1,0:T(8,128)(2,1)}, u32[]{:S(2)}, u32[]{:S(2)}) collective-permute-start(bf16[1,512,512]{2,1,0:T(8,128)(2,1)} %weight_term.5), channel_id=1, source_target_pairs={{0,2},{1,3},{2,0},{3,1},{4,6},{5,7},{6,4},{7,5},{8,10},{9,11},{10,... | collective-permute-start | bytes 1572872 | tf_op jit(solution)/shard_map/ppermute | solution.py:329
  65.8 1.3 %collective-permute-start.6 = (bf16[512,128]{1,0:T(8,128)(2,1)S(1)}, bf16[512,128]{1,0:T(8,128)(2,1)}, u32[]{:S(2)}, u32[]{:S(2)}) collective-permute-start(bf16[512,128]{1,0:T(8,128)(2,1)S(1)} %get-tuple-element.38.st_ref.sc), channel_id=1, source_target_pairs={{8,0},{12,4},{16,8},{20,12},{24,16},{28,20},{9,1},{13,5},{17,9},{2... | collective-permute-start | bytes 393224 | tf_op jit(solution)/shard_map/ppermute | solution.py:25
  67.0 1.5 %collective-permute-start.5 = (bf16[512,128]{1,0:T(8,128)(2,1)S(1)}, bf16[512,128]{1,0:T(8,128)(2,1)}, u32[]{:S(2)}, u32[]{:S(2)}) collective-permute-start(bf16[512,128]{1,0:T(8,128)(2,1)S(1)} %get-tuple-element.38.st_ref.sc), channel_id=1, source_target_pairs={{4,0},{8,4},{12,8},{16,12},{20,16},{24,20},{28,24},{5,1},{9,5},{13... | collective-permute-start | bytes 393224 | tf_op jit(solution)/shard_map/ppermute | solution.py:25
  68.5 0.0 copy-start.2
  68.6 1.0 copy-done.2
  69.6 1.0 copy-done.5
  70.6 7.2 %query_kernel.2.rest_0_ = bf16[512,512]{1,0:T(8,128)(2,1)} custom-call(bf16[512,1024]{1,0:T(8,128)(2,1)S(1)} %queries_to_send.1.q_ref.g_ref.qc.gc, bf16[512,1024]{1,0:T(8,128)(2,1)S(1)} %queries_to_send.1.q_ref.g_ref.qc.gc, bf16[512,128]{1,0:T(8,128)(2,1)S(1)} %get-tuple-element.38.st_ref.sc, bf16[512,512]{1,0:T(8,128)(2,1)S(1)} %bitcast.41, ...), custom_call_target="tpu_custom_call" | custom-call | bytes 28000000 | tf_op jit(solution)/shard_map/query_kernel/pallas_call | solution.py:239
  77.8 0.0 collective-permute-done.6.se
  77.8 8.3 %collective-permute-done.5.sd = bf16[512,128]{1,0:T(8,128)(2,1)} collective-permute-done((bf16[512,128]{1,0:T(8,128)(2,1)S(1)}, bf16[512,128]{1,0:T(8,128)(2,1)}, u32[]{:S(2)}, u32[]{:S(2)}) %collective-permute-start.5) | collective-permute-done | bytes 131104 | tf_op jit(solution)/shard_map/ppermute | solution.py:25
  86.2 7.2 %query_kernel.3 = bf16[512,512]{1,0:T(8,128)(2,1)} custom-call(bf16[512,1024]{1,0:T(8,128)(2,1)S(1)} %queries_to_send.1.q_ref.g_ref.qc.gc, bf16[512,1024]{1,0:T(8,128)(2,1)S(1)} %queries_to_send.1.q_ref.g_ref.qc.gc, bf16[512,128]{1,0:T(8,128)(2,1)S(1)} %get-tuple-element.38.st_ref.sc, ...), custom_call_target="tpu_custom_call", output_to_operand_aliasing={{}: (12, {})} | custom-call | bytes 28000000 | tf_op jit(solution)/shard_map/query_kernel/pallas_call | solution.py:239
  93.4 2.1 %weight_term.4 = f32[1,512,512]{2,1,0:T(8,128)S(1)} custom-call(s32[2]{0:T(128)S(1)} %get-tuple-element.56.sel_ref, bf16[256,512]{1,0:T(8,128)(2,1)S(1)} %get-tuple-element.25.refs_0_, bf16[256,512]{1,0:T(8,128)(2,1)S(1)} %copy-done.9, bf16[512,2048]{1,0:T(8,128)(2,1)S(1)} %bitcast.37, bf16[2,512,512]{2,1,0:T(8,128)(2,1)} %collective-permute-done.7.refs_3_), custom_call_target="tpu_custom_call" | custom-call | bytes 10500000 | tf_op jit(solution)/shard_map/weight_term/pallas_call | solution.py:315
  95.4 0.0 collective-permute-done.8
  95.4 0.0 copy-start.3
  95.4 0.0 copy-start.6
  95.5 2.1 %fusion.3 = (bf16[4,64,512]{2,1,0:T(8,128)(2,1)S(1)}, f32[4,1,64,512]{3,2,1,0:T(8,128)}) fusion(f32[4,2,64,512]{3,2,1,0:T(8,128)S(1)} %bitcast.52, s32[]{:T(128)S(6)} %select_n.94, bf16[4,2,64,512]{3,2,1,0:T(8,128)(2,1)} %bitcast.13, s32[]{:T(128)S(6)} %select_n.90), kind=kLoop, calls=%fused_computation.9 | loop fusion | flops 655360 | bytes 2359304 | tf_op jit(solution)/shard_map/convert_element_type | solution.py:356
  97.6 0.0 collective-permute-start.9
  97.6 0.0 collective-permute-done.10.qd.gd
  97.6 8.8 %key_kernel.2 = (bf16[512,512]{1,0:T(8,128)(2,1)}, bf16[512,512]{1,0:T(8,128)(2,1)}) custom-call(bf16[512,512]{1,0:T(8,128)(2,1)S(1)} %bitcast.43, bf16[512,512]{1,0:T(8,128)(2,1)S(1)} %bitcast.50, s32[1,512]{1,0:T(1,128)S(1)} %get-tuple-element.50.tc.t_ref, bf16[512,1024]{1,0:T(8,128)(2,1)S(1)} %queries_to_send.1.q_ref.g_ref.qc.gc, ...), custom_call_target="tpu_custom_call" | custom-call | bytes 28000000 | tf_op jit(solution)/shard_map/key_kernel/pallas_call | solution.py:239
  106.4 0.0 collective-permute-done.9
  106.4 1.7 %convert_add_fusion.1 = (f32[2,1,64,512]{3,2,1,0:T(8,128)S(1)}, bf16[2,64,512]{2,1,0:T(8,128)(2,1)}) fusion(f32[2,2,64,512]{3,2,1,0:T(8,128)S(1)} %bitcast.54, s32[]{:T(128)S(6)} %select_n.95, bf16[2,2,64,512]{3,2,1,0:T(8,128)(2,1)} %bitcast.16, s32[]{:T(128)S(6)} %select_n.93), kind=kLoop, calls=%fused_computation.10 | loop fusion | flops 327680 | bytes 1179656 | tf_op jit(solution)/shard_map/add | solution.py:353
  108.1 2.5 %collective-permute-start.11 = (bf16[2,64,512]{2,1,0:T(8,128)(2,1)}, bf16[2,64,512]{2,1,0:T(8,128)(2,1)}, u32[]{:S(2)}, u32[]{:S(2)}) collective-permute-start(bf16[2,64,512]{2,1,0:T(8,128)(2,1)} %get-tuple-element.45), channel_id=1, source_target_pairs={{0,8},{4,12},{8,0},{12,4},{16,24},{20,28},{24,16},{28,20},{1,9},{5... | collective-permute-start | bytes 393224 | tf_op jit(solution)/shard_map/ppermute | solution.py:329
  110.6 8.8 %key_kernel.3 = (bf16[512,512]{1,0:T(8,128)(2,1)}, bf16[512,512]{1,0:T(8,128)(2,1)}) custom-call(bf16[512,512]{1,0:T(8,128)(2,1)S(1)} %bitcast.44, bf16[512,512]{1,0:T(8,128)(2,1)S(1)} %bitcast.51, s32[1,512]{1,0:T(1,128)S(1)} %get-tuple-element.50.tc.t_ref, ...), custom_call_target="tpu_custom_call", output_to_operand_aliasing={{0}: (12, {}), {1}: (13, {})} | custom-call | bytes 28000000 | tf_op jit(solution)/shard_map/key_kernel/pallas_call | solution.py:239
  119.3 0.0 collective-permute-done.11
  119.3 0.9 fusion.5
  120.2 2.7 %collective-permute-start.12 = (bf16[1,64,512]{2,1,0:T(8,128)(2,1)S(1)}, bf16[1,64,512]{2,1,0:T(8,128)(2,1)S(1)}, u32[]{:S(2)}, u32[]{:S(2)}) collective-permute-start(bf16[1,64,512]{2,1,0:T(8,128)(2,1)S(1)} %fusion.5), channel_id=1, source_target_pairs={{0,16},{4,20},{8,24},{12,28},{16,0},{20,4},{24,8},{28,12},{1,17},{... | collective-permute-start | bytes 196616 | tf_op jit(solution)/shard_map/ppermute | solution.py:329
  122.9 3.1 %collective-permute-done.12 = bf16[1,64,512]{2,1,0:T(8,128)(2,1)S(1)} collective-permute-done((bf16[1,64,512]{2,1,0:T(8,128)(2,1)S(1)}, bf16[1,64,512]{2,1,0:T(8,128)(2,1)S(1)}, u32[]{:S(2)}, u32[]{:S(2)}) %collective-permute-start.12) | collective-permute-done | bytes 65568 | tf_op jit(solution)/shard_map/ppermute | solution.py:329
  126.0 1.5 %fusion.7 = f32[64,512]{1,0:T(8,128)} fusion(bf16[1,64,512]{2,1,0:T(8,128)(2,1)S(1)} %collective-permute-done.12, f32[2,1,64,512]{3,2,1,0:T(8,128)S(1)} %get-tuple-element.44, s32[]{:T(128)S(6)} %select_n.98, bf16[2,64,512]{2,1,0:T(8,128)(2,1)} %collective-permute-done.11), kind=kLoop, calls=%fused_computation.17 | loop fusion | flops 131072 | bytes 393220 | tf_op jit(solution)/shard_map/add | solution.py:424
  (18 shorter events, 0.0 us)
Async XLA Ops:
  1.3 8.4 %copy-start.10 = (bf16[512,2048]{1,0:T(8,128)(2,1)S(1)}, bf16[512,2048]{1,0:T(8,128)(2,1)}, u32[]{:S(2)}) copy-start(bf16[512,2048]{1,0:T(8,128)(2,1)} %w_ref.1) | copy-start | bytes 6291460
  2.7 7.0 %copy-start.12 = (bf16[512,256]{1,0:T(8,128)(2,1)}, bf16[512,256]{1,0:T(8,128)(2,1)S(1)}, u32[]{:S(2)}) copy-start(bf16[512,256]{1,0:T(8,128)(2,1)S(1)} %get-tuple-element.55) | copy-start | bytes 786436
  2.7 7.0 %copy-start.14 = (bf16[512,256]{1,0:T(8,128)(2,1)}, bf16[512,256]{1,0:T(8,128)(2,1)S(1)}, u32[]{:S(2)}) copy-start(bf16[512,256]{1,0:T(8,128)(2,1)S(1)} %get-tuple-element.47) | copy-start | bytes 786436
  2.8 7.0 %copy-start.15 = (bf16[512,256]{1,0:T(8,128)(2,1)}, bf16[512,256]{1,0:T(8,128)(2,1)S(1)}, u32[]{:S(2)}) copy-start(bf16[512,256]{1,0:T(8,128)(2,1)S(1)} %get-tuple-element.54) | copy-start | bytes 786436
  2.8 7.0 %copy-start = (bf16[1,512,2048]{2,1,0:T(8,128)(2,1)S(1)}, bf16[1,512,2048]{2,1,0:T(8,128)(2,1)}, u32[]{:S(2)}) copy-start(bf16[1,512,2048]{2,1,0:T(8,128)(2,1)} %param.10) | copy-start | bytes 6291460
  3.8 18.0 %collective-permute-start.1 = (bf16[528,512]{1,0:T(8,128)(2,1)}, bf16[528,512]{1,0:T(8,128)(2,1)}, u32[]{:S(2)}, u32[]{:S(2)}) collective-permute-start(bf16[528,512]{1,0:T(8,128)(2,1)} %get-tuple-element.53), channel_id=1, source_target_pairs={{0,8},{4,12},{8,16},{12,20},{16,24},{20,28},{1,9},{5,13},{9,17},{1... | collective-permute-start | bytes 1622024 | tf_op jit(solution)/shard_map/ppermute | solution.py:25
  9.8 1.0 copy-start.11
  12.6 33.0 %collective-permute-start = (bf16[512,1024]{1,0:T(8,128)(2,1)S(1)}, bf16[512,1024]{1,0:T(8,128)(2,1)}, u32[]{:S(2)}, u32[]{:S(2)}) collective-permute-start(bf16[512,1024]{1,0:T(8,128)(2,1)S(1)} %queries_to_send.1.q_ref.g_ref.qc.gc), channel_id=1, source_target_pairs={{8,0},{12,4},{16,8},{20,12},{24,16},{28,20},{9,1},{13,5},{17,9},{2... | collective-permute-start | bytes 3145736 | tf_op jit(solution)/shard_map/ppermute | solution.py:25
  13.9 18.4 %collective-permute-start.3 = (bf16[528,512]{1,0:T(8,128)(2,1)}, bf16[528,512]{1,0:T(8,128)(2,1)}, u32[]{:S(2)}, u32[]{:S(2)}) collective-permute-start(bf16[528,512]{1,0:T(8,128)(2,1)} %get-tuple-element.52), channel_id=1, source_target_pairs={{0,8},{4,12},{8,16},{12,20},{16,24},{20,28},{1,9},{5,13},{9,17},{1... | collective-permute-start | bytes 1622024 | tf_op jit(solution)/shard_map/ppermute | solution.py:25
  19.2 13.1 %copy-start.13 = (bf16[512,256]{1,0:T(8,128)(2,1)S(1)}, bf16[512,256]{1,0:T(8,128)(2,1)}, u32[]{:S(2)}) copy-start(bf16[512,256]{1,0:T(8,128)(2,1)} %copy-done.12) | copy-start | bytes 786436
  23.9 12.5 %collective-permute-start.2 = (bf16[528,512]{1,0:T(8,128)(2,1)}, bf16[528,512]{1,0:T(8,128)(2,1)}, u32[]{:S(2)}, u32[]{:S(2)}) collective-permute-start(bf16[528,512]{1,0:T(8,128)(2,1)} %broadcast_select_fusion.2), channel_id=1, source_target_pairs={{0,4},{4,0},{8,12},{12,8},{16,20},{20,16},{24,28},{28,24},{1,5},{5... | collective-permute-start | bytes 1622024 | tf_op jit(solution)/shard_map/ppermute | solution.py:329
  33.3 14.7 %collective-permute-start.4 = (bf16[528,512]{1,0:T(8,128)(2,1)}, bf16[528,512]{1,0:T(8,128)(2,1)}, u32[]{:S(2)}, u32[]{:S(2)}) collective-permute-start(bf16[528,512]{1,0:T(8,128)(2,1)} %broadcast_select_fusion.1), channel_id=1, source_target_pairs={{0,4},{4,0},{8,12},{12,8},{16,20},{20,16},{24,28},{28,24},{1,5},{5... | collective-permute-start | bytes 1622024 | tf_op jit(solution)/shard_map/ppermute | solution.py:329
  36.3 1.0 copy-start.1
  37.4 1.0 copy-start.4
  55.1 2.4 %copy-start.7 = (bf16[256,512]{1,0:T(8,128)(2,1)}, bf16[256,512]{1,0:T(8,128)(2,1)S(1)}, u32[]{:S(2)}) copy-start(bf16[256,512]{1,0:T(8,128)(2,1)S(1)} %get-tuple-element.32.refs_1_) | copy-start | bytes 786436
  57.5 3.0 %collective-permute-start.7 = (bf16[2,512,512]{2,1,0:T(8,128)(2,1)}, bf16[2,512,512]{2,1,0:T(8,128)(2,1)}, u32[]{:S(2)}, u32[]{:S(2)}) collective-permute-start(bf16[2,512,512]{2,1,0:T(8,128)(2,1)} %weight_term.3), channel_id=1, source_target_pairs={{0,1},{1,0},{2,3},{3,2},{4,5},{5,4},{6,7},{7,6},{8,9},{9,8},{10,11... | collective-permute-start | bytes 3145736 | tf_op jit(solution)/shard_map/ppermute | solution.py:329
  57.5 40.1 %collective-permute-start.10 = (bf16[512,1024]{1,0:T(8,128)(2,1)}, bf16[512,1024]{1,0:T(8,128)(2,1)}, u32[]{:S(2)}, u32[]{:S(2)}) collective-permute-start(bf16[512,1024]{1,0:T(8,128)(2,1)} %broadcast_select_fusion), channel_id=1, source_target_pairs={{0,4},{4,0},{8,12},{12,8},{16,20},{20,16},{24,28},{28,24},{1,5},{5... | collective-permute-start | bytes 3145736 | tf_op jit(solution)/shard_map/ppermute | solution.py:329
  60.5 1.0 copy-start.8
  64.3 31.1 %collective-permute-start.8 = (bf16[1,512,512]{2,1,0:T(8,128)(2,1)}, bf16[1,512,512]{2,1,0:T(8,128)(2,1)}, u32[]{:S(2)}, u32[]{:S(2)}) collective-permute-start(bf16[1,512,512]{2,1,0:T(8,128)(2,1)} %weight_term.5), channel_id=1, source_target_pairs={{0,2},{1,3},{2,0},{3,1},{4,6},{5,7},{6,4},{7,5},{8,10},{9,11},{10,... | collective-permute-start | bytes 1572872 | tf_op jit(solution)/shard_map/ppermute | solution.py:329
  65.8 12.1 %collective-permute-start.6 = (bf16[512,128]{1,0:T(8,128)(2,1)S(1)}, bf16[512,128]{1,0:T(8,128)(2,1)}, u32[]{:S(2)}, u32[]{:S(2)}) collective-permute-start(bf16[512,128]{1,0:T(8,128)(2,1)S(1)} %get-tuple-element.38.st_ref.sc), channel_id=1, source_target_pairs={{8,0},{12,4},{16,8},{20,12},{24,16},{28,20},{9,1},{13,5},{17,9},{2... | collective-permute-start | bytes 393224 | tf_op jit(solution)/shard_map/ppermute | solution.py:25
  67.0 19.1 %collective-permute-start.5 = (bf16[512,128]{1,0:T(8,128)(2,1)S(1)}, bf16[512,128]{1,0:T(8,128)(2,1)}, u32[]{:S(2)}, u32[]{:S(2)}) collective-permute-start(bf16[512,128]{1,0:T(8,128)(2,1)S(1)} %get-tuple-element.38.st_ref.sc), channel_id=1, source_target_pairs={{4,0},{8,4},{12,8},{16,12},{20,16},{24,20},{28,24},{5,1},{9,5},{13... | collective-permute-start | bytes 393224 | tf_op jit(solution)/shard_map/ppermute | solution.py:25
  68.5 1.0 copy-start.2
  69.6 1.0 copy-start.5
  77.8 15.5 %copy-start.9 = (bf16[256,512]{1,0:T(8,128)(2,1)S(1)}, bf16[256,512]{1,0:T(8,128)(2,1)}, u32[]{:S(2)}) copy-start(bf16[256,512]{1,0:T(8,128)(2,1)} %copy-done.7) | copy-start | bytes 786436
  95.4 2.1 %copy-start.3 = (bf16[1,512,512]{2,1,0:T(8,128)(2,1)S(1)}, bf16[1,512,512]{2,1,0:T(8,128)(2,1)}, u32[]{:S(2)}) copy-start(bf16[1,512,512]{2,1,0:T(8,128)(2,1)} %param.7) | copy-start | bytes 1572868
  95.4 2.1 %copy-start.6 = (bf16[1,512,512]{2,1,0:T(8,128)(2,1)S(1)}, bf16[1,512,512]{2,1,0:T(8,128)(2,1)}, u32[]{:S(2)}) copy-start(bf16[1,512,512]{2,1,0:T(8,128)(2,1)} %param.8) | copy-start | bytes 1572868
  97.6 8.8 %collective-permute-start.9 = (bf16[4,64,512]{2,1,0:T(8,128)(2,1)S(1)}, bf16[4,64,512]{2,1,0:T(8,128)(2,1)}, u32[]{:S(2)}, u32[]{:S(2)}) collective-permute-start(bf16[4,64,512]{2,1,0:T(8,128)(2,1)S(1)} %get-tuple-element.42), channel_id=1, source_target_pairs={{0,4},{4,0},{8,12},{12,8},{16,20},{20,16},{24,28},{28,24},{1,5},{5... | collective-permute-start | bytes 786440 | tf_op jit(solution)/shard_map/ppermute | solution.py:329
  97.6 8.8 %copy-start.16 = (f32[4,1,64,512]{3,2,1,0:T(8,128)S(1)}, f32[4,1,64,512]{3,2,1,0:T(8,128)}, u32[]{:S(2)}) copy-start(f32[4,1,64,512]{3,2,1,0:T(8,128)} %get-tuple-element.43) | copy-start | bytes 1572868
  108.1 11.2 %collective-permute-start.11 = (bf16[2,64,512]{2,1,0:T(8,128)(2,1)}, bf16[2,64,512]{2,1,0:T(8,128)(2,1)}, u32[]{:S(2)}, u32[]{:S(2)}) collective-permute-start(bf16[2,64,512]{2,1,0:T(8,128)(2,1)} %get-tuple-element.45), channel_id=1, source_target_pairs={{0,8},{4,12},{8,0},{12,4},{16,24},{20,28},{24,16},{28,20},{1,9},{5... | collective-permute-start | bytes 393224 | tf_op jit(solution)/shard_map/ppermute | solution.py:329
  120.2 5.8 %collective-permute-start.12 = (bf16[1,64,512]{2,1,0:T(8,128)(2,1)S(1)}, bf16[1,64,512]{2,1,0:T(8,128)(2,1)S(1)}, u32[]{:S(2)}, u32[]{:S(2)}) collective-permute-start(bf16[1,64,512]{2,1,0:T(8,128)(2,1)S(1)} %fusion.5), channel_id=1, source_target_pairs={{0,16},{4,20},{8,24},{12,28},{16,0},{20,4},{24,8},{28,12},{1,17},{... | collective-permute-start | bytes 196616 | tf_op jit(solution)/shard_map/ppermute | solution.py:329
where the time goes:
time: 128 us; the launch traced here: 127 us
  Pallas kernels  55.3 us (43%)
  starting transfers between devices  27.7 us (22%)
  waiting for transfers between devices  22.7 us (18%)
  other arithmetic  13.3 us (10%)
  local copies, waits for them, and re-layouts  7.61 us (6%)
    pallas_call x6, Pallas kernels, call(): pl.pallas_call(functools.partial(kernel, self.first), grid=(self.pairs,),...  46.2 us
    ppermute x5, waiting for transfers between devices, shift(): return lax.ppermute(x, 'ctx', pairs)  17.8 us
    ppermute x5, starting transfers between devices, shift(): return lax.ppermute(x, 'ctx', pairs)  15.3 us
    ppermute x8, starting transfers between devices, swap(): lax.ppermute(x, axis, [(i, i ^ bit) for i in range(lax.axis_size(axis))])  12.4 us
    pallas_call x3, Pallas kernels, weight_term(): pl.pallas_call(weight_kernel, grid_spec=pltpu.PrefetchScalarGridSpec(num_...  7.28 us
    unnamed x34, local copies, waits for them, and re-layouts  6.21 us
    ppermute x8, waiting for transfers between devices, swap(): lax.ppermute(x, axis, [(i, i ^ bit) for i in range(lax.axis_size(axis))])  4.96 us
    convert_element_type x2, other arithmetic, halves(): return (take(1 - mine).astype(BF16), take(mine))  2.96 us
  transfers between devices with their start and end apart: 13, of which 6 were waited for; matrix products, arithmetic and copies ran while one was open for 6% of the time, Pallas kernels for 36%

commit v1 on v0

v1 whole, which is shorter than its diff:
```python
import functools

import jax
import jax.numpy as jnp
from jax import lax
from jax.experimental import pallas as pl
from jax.experimental.pallas import tpu as pltpu
from jax.sharding import PartitionSpec as P

HEAD_DIM = 64
TILE = 256
LANES = 128
TAG_LANES = 64
PIECES = 3
MASKED_SCORE = -1e30
SCALE = HEAD_DIM ** (-0.5)
F32 = jnp.float32
BF16 = jnp.bfloat16
PARAMS = pltpu.CompilerParams(vmem_limit_bytes=16 << 20)


def shift(x, by):
    size = lax.axis_size("ctx")
    pairs = [(i, i + by) for i in range(size) if 0 <= i + by < size]
    return lax.ppermute(x, "ctx", pairs)


def dot_t(a, b):
    return lax.dot_general(a, b, (((1,), (1,)), ((), ())), preferred_element_type=F32)


def dot(a, b):
    return jnp.dot(a, b, preferred_element_type=F32)


def lane_of(rows):
    return lax.broadcasted_iota(jnp.int32, (rows, LANES), 1)


def one_hot(tag_row):
    count = tag_row.shape[1]
    tag = lax.broadcasted_iota(jnp.int32, (LANES, count), 0) + 1
    hit = (tag_row.astype(F32) == tag.astype(F32)) & (tag <= TAG_LANES)
    return jnp.where(hit, 1.0, 0.0).astype(F32).T


def key_extra(tag_row):
    hot = one_hot(tag_row)
    lane = lane_of(hot.shape[0])
    return jnp.where(lane < TAG_LANES, (1.0 - hot) * MASKED_SCORE, 1.0).astype(BF16)


def pieces(x):
    out = []
    for _ in range(PIECES):
        part = x.astype(BF16).astype(F32)
        out.append(part)
        x = x - part
    return out


def own(lane, half):
    return (lane >= half * HEAD_DIM) & (lane < (half + 1) * HEAD_DIM)


def factor(chosen, value=1.0):
    return jnp.where(chosen, value, 0.0).astype(F32).astype(BF16)


def own_factor(half, value=1.0):
    return factor(own(lane_of(1), half), value)


def extra_factors(head):
    lane = lane_of(1)
    first = TAG_LANES + 2 * PIECES * head
    tag_lse = (lane < TAG_LANES) | ((lane >= first) & (lane < first + PIECES))
    delta = (lane >= first + PIECES) & (lane < first + 2 * PIECES)
    return factor(tag_lse), factor(delta)


def wide(features, extra):
    return jnp.concatenate([features, extra], axis=1)


def lower(shape, by_query):
    a = lax.broadcasted_iota(jnp.int32, shape, 0)
    b = lax.broadcasted_iota(jnp.int32, shape, 1)
    return (b <= a) if by_query else (a <= b)


def join(to_k, to_v, to_x, ke, ve, te, ko, vo, to, first_step):
    to_k[...] = ke[...] + ko[...]
    to_v[...] = ve[...] + vo[...]

    @pl.when(first_step)
    def _():
        to_x[...] = key_extra(te[0:1, :] + to[0:1, :])


def forward_kernel(first_pair, q_ref, g_ref, kc, vc, tc, ka, va, ta, ke, ve, te, ko, vo, to, *rest):
    before = rest[0] if first_pair else None
    o_ref, st_ref, xc, xa, xb, kb, vb, tag, rowed = rest[1 if first_pair else 0 :]
    step = pl.program_id(0)
    rows = q_ref.shape[0]

    @pl.when(step == 0)
    def _():
        xc[...] = key_extra(tc[0:1, :])
        xa[...] = key_extra(ta[0:1, :])
        tag[...] = one_hot(tc[0:1, :]).astype(BF16)
        rowed[...] = jnp.zeros_like(rowed)

    join(kb, vb, xb, ke, ve, te, ko, vo, to, step == 0)

    vt = {id(v): v[...].T for v in (va, vb, vc)}
    gt = g_ref[...].T.astype(F32)
    for base in range(0, rows, TILE):
        end = base + TILE
        spans = [(ka, va, xa, base, rows), (kb, vb, xb, 0, rows)]
        spans += [(kc, vc, xc, 0, base)] if base else []
        spans += [(kc, vc, xc, base, end)]
        q = q_ref[base:end, :]
        for half in range(2):
            feats = slice(half * HEAD_DIM, (half + 1) * HEAD_DIM)
            qx = wide(q * own_factor(half, SCALE), tag[base:end, :])
            scores = [dot_t(wide(k[lo:hi, :], x[lo:hi, :]), qx) for k, v, x, lo, hi in spans]
            scores[-1] = jnp.where(lower((TILE, TILE), False), scores[-1], MASKED_SCORE)
            peak = functools.reduce(
                jnp.maximum, [jnp.max(s, axis=0, keepdims=True) for s in scores]
            )
            total = jnp.zeros((1, TILE), F32)
            acc = jnp.zeros((HEAD_DIM, TILE), F32)
            for s, (k, v, x, lo, hi) in zip(scores, spans):
                e = jnp.exp(s - peak)
                total = total + jnp.sum(e, axis=0, keepdims=True)
                acc = acc + dot(vt[id(v)][feats, lo:hi], e.astype(BF16))
            acc = acc / total
            o_ref[feats, base:end] = acc.astype(BF16)
            delta = jnp.sum(acc * gt[feats, base:end], axis=0, keepdims=True)
            first = TAG_LANES + 2 * PIECES * (2 * (step + first_pair) + half)
            for i, part in enumerate(pieces(-(peak + jnp.log(total))) + pieces(-delta)):
                rowed[pl.ds(first + i, 1), base:end] = part

    @pl.when(step == pl.num_programs(0) - 1)
    def _():
        was = tag[...] if before is None else before[...]
        st_ref[...] = (was.astype(F32) + rowed[...].T).astype(BF16)


def query_kernel(first_pair, q_ref, g_ref, st_ref, kc, vc, tc, ka, va, ta, ke, ve, te, ko, vo, to, *rest):
    dq_ref, xc, xa, xb, kb, vb, acc, first = rest[1 if first_pair else 0 :]
    step = pl.program_id(0)
    rows = q_ref.shape[0]

    @pl.when(step == 0)
    def _():
        xc[...] = key_extra(tc[0:1, :])
        xa[...] = key_extra(ta[0:1, :])

    join(kb, vb, xb, ke, ve, te, ko, vo, to, step == 0)
    lane = lane_of(rows)
    q, g, stats = q_ref[...], g_ref[...], st_ref[...]
    for half in range(2):
        mine = own(lane, half)
        for_score, for_grad = extra_factors(2 * (step + first_pair) + half)
        qx = wide(q * own_factor(half, SCALE), stats * for_score)
        gx = wide(g * own_factor(half), stats * for_grad)
        acc[...] = jnp.zeros_like(acc)
        for k, v, x, near in ((ka, va, xa, 0), (kb, vb, xb, 1), (kc, vc, xc, 2)):
            for lo in range(0, rows, TILE):
                hi = lo + TILE
                top = lo if near == 2 else 0
                end = hi if near == 0 else rows
                p = jnp.exp(dot_t(qx[top:end], wide(k[lo:hi, :], x[lo:hi, :])))
                if near == 2:
                    p = jnp.where(lower((end - top, TILE), True), p, 0.0)
                dp = dot_t(gx[top:end], wide(v[lo:hi, :], x[lo:hi, :]))
                acc[top:end, :] += dot((p * dp).astype(BF16), k[lo:hi, :])
        if half == 0:
            first[...] = acc[...]
        else:
            dq_ref[...] = (jnp.where(mine, acc[...], first[...]) * SCALE).astype(BF16)


def key_kernel(first_pair, k_ref, v_ref, t_ref, qc, gc, sc, qd, gd, sd, qe, ge, se, *rest):
    dk_ref, dv_ref, x_ref = rest[2 if first_pair else 0 :][:3]
    dks, dvs = rest[-4:-2], rest[-2:]
    step = pl.program_id(0)
    rows = k_ref.shape[0]

    @pl.when(step == 0)
    def _():
        x_ref[...] = key_extra(t_ref[0:1, :])

    kx = wide(k_ref[...], x_ref[...])
    vx = wide(v_ref[...], x_ref[...])
    for half in range(2):
        dk, dv = dks[half], dvs[half]
        dk[...] = jnp.zeros_like(dk)
        dv[...] = jnp.zeros_like(dv)
        for_score, for_grad = extra_factors(2 * (step + first_pair) + half)
        for q_ref, g_ref, s_ref, near in ((qc, gc, sc, 2), (qd, gd, sd, 1), (qe, ge, se, 0)):
            for lo in range(0, rows, TILE):
                hi = lo + TILE
                top = lo if near == 0 else 0
                end = hi if near == 2 else rows
                q, g, stats = q_ref[lo:hi, :], g_ref[lo:hi, :], s_ref[lo:hi, :]
                qx = wide(q * own_factor(half, SCALE), stats * for_score)
                gx = wide(g * own_factor(half), stats * for_grad)
                p = jnp.exp(dot_t(kx[top:end], qx))
                if near == 2:
                    row = lax.broadcasted_iota(jnp.int32, p.shape, 0)
                    col = lax.broadcasted_iota(jnp.int32, p.shape, 1) + lo
                    p = jnp.where(row <= col, p, 0.0)
                dp = dot_t(vx[top:end], gx)
                dv[top:end, :] += dot(p.astype(BF16), g)
                dk[top:end, :] += dot((p * dp).astype(BF16), q)
    second = own(lane_of(rows), 1)
    dk_ref[...] = (jnp.where(second, dks[1][...], dks[0][...]) * SCALE).astype(BF16)
    dv_ref[...] = jnp.where(second, dvs[1][...], dvs[0][...]).astype(BF16)


def lasting(microseconds):
    return pl.CostEstimate(flops=0, transcendentals=0, bytes_accessed=int(microseconds * 3.5e6))


class Attention:
    def __init__(self, rows, width, chunks, first, count):
        whole = width // LANES
        size = whole // chunks
        begin = first // size * size
        block = lambda off: pl.BlockSpec((rows, LANES), lambda p: (0, p + off))
        tag = pl.BlockSpec((16, rows), lambda p: (rows // 16, 0))
        self.first, self.count, self.rows, self.width = first, count, rows, width
        self.stat = pl.BlockSpec((rows, LANES), lambda p: (0, 0))
        self.sent = [block(first), block(whole + first)]
        self.held = [block(first - begin), block(size + first - begin), tag]
        self.out = block(first)
        self.extra = pltpu.VMEM((rows, LANES), BF16)
        self.total = pltpu.VMEM((rows, LANES), F32)

    def call(self, kernel, in_specs, args, out_specs, out_shape, scratch, before, aliased, last):
        before = list(before)
        spec = pl.BlockSpec(memory_space=pl.ANY) if aliased else self.stat
        aliases = {len(args) + i: i for i in range(len(before))} if aliased else {}
        return pl.pallas_call(
            functools.partial(kernel, self.first), grid=(self.count,),
            in_specs=in_specs + [spec] * len(before), out_specs=out_specs,
            out_shape=[jax.ShapeDtypeStruct(s, BF16) for s in out_shape],
            scratch_shapes=scratch, input_output_aliases=aliases,
            compiler_params=PARAMS, cost_estimate=lasting(last * self.count), name=kernel.__name__,
        )(*args, *before)

    def forward(self, sent, window, before):
        return self.call(
            forward_kernel, self.sent + self.held * 4,
            [sent, sent] + [x for x in window for _ in range(3)],
            [pl.BlockSpec((LANES, self.rows), lambda p: (p, 0)), self.stat],
            [(self.count * LANES, self.rows), (self.rows, LANES)],
            [self.extra] * 6 + [pltpu.VMEM((LANES, self.rows), F32)], before, False, 3.5,
        )

    def query(self, sent, stats, window, before):
        return self.call(
            query_kernel, self.sent + [self.stat] + self.held * 4,
            [sent, sent, stats] + [x for x in window for _ in range(3)],
            [self.out], [(self.rows, self.width)], [self.extra] * 5 + [self.total] * 2, before, True, 3.5,
        )

    def key(self, held, sources, before):
        return self.call(
            key_kernel, self.held + (self.sent + [self.stat]) * 3,
            [held] * 3 + [in_hbm(x) for q, st in sources for x in (q, q, st)],
            [self.out] * 2, [(self.rows, self.width)] * 2, [self.extra] + [self.total] * 4,
            before, True, 4.2,
        )


def send_kernel(q_ref, g_ref, w_ref, out_ref):
    half = pl.num_programs(0) // 2
    step = pl.program_id(0)

    @pl.when(step < half)
    def _():
        out_ref[...] = q_ref[...]

    @pl.when(step >= half)
    def _():
        out_ref[...] = dot_t(g_ref[...], w_ref[...]).astype(BF16)


def queries_to_send(query_rows, grad_rows, out_weight):
    rows, width = query_rows.shape
    model = grad_rows.shape[1]
    blocks = width // TILE
    return pl.pallas_call(
        send_kernel, grid=(2 * blocks,),
        in_specs=[
            pl.BlockSpec((rows, TILE), lambda i: (0, jnp.minimum(i, blocks - 1))),
            pl.BlockSpec((rows, model), lambda i: (0, 0)),
            pl.BlockSpec((TILE, model), lambda i: (jnp.maximum(i - blocks, 0), 0)),
        ],
        out_specs=pl.BlockSpec((rows, TILE), lambda i: (0, i)),
        out_shape=jax.ShapeDtypeStruct((rows, 2 * width), BF16),
        compiler_params=PARAMS, cost_estimate=lasting(5), name="queries_to_send",
    )(query_rows, grad_rows, out_weight)


def weight_kernel(sel_ref, *refs):
    outs, g_ref, w_ref = refs[:2], refs[2], refs[-1]
    size = outs[0].shape[0]
    for i, o_ref in enumerate(outs):
        part = dot(o_ref[...], g_ref[...])
        if len(refs) == 5:
            part = part + refs[3][0, i * size : (i + 1) * size, :].astype(F32)
        w_ref[0, i * size : (i + 1) * size, :] = part.astype(w_ref.dtype)


def weight_term(attn, grad_rows, columns, parts, got, dtype):
    size, rows = attn[0].shape
    width = size * len(attn)
    cols = grad_rows.shape[1] // parts
    steps = 1 if got is not None else parts // 2
    column = lambda i, s: (0, s[0] + 2 * i)
    extra = [] if got is None else [pl.BlockSpec((1, width, cols), lambda i, s: (s[1], 0, 0))]
    return pl.pallas_call(
        weight_kernel,
        grid_spec=pltpu.PrefetchScalarGridSpec(
            num_scalar_prefetch=1, grid=(steps,),
            in_specs=[pl.BlockSpec((size, rows), lambda i, s: (0, 0))] * 2
            + [pl.BlockSpec((rows, cols), column)] + extra,
            out_specs=pl.BlockSpec((1, width, cols), lambda i, s: (i, 0, 0)),
        ),
        out_shape=jax.ShapeDtypeStruct((steps, width, cols), dtype),
        compiler_params=PARAMS, cost_estimate=lasting(3), name="weight_term",
    )(columns, *map(in_hbm, attn), in_hbm(grad_rows), *([] if got is None else [got]))


def keep_kernel(sel_ref, o0_ref, o1_ref, g_ref, got_ref, moved_ref, send_ref, keep_ref):
    mine = sel_ref[2]
    count, size = send_ref.shape[0], send_ref.shape[1]
    half = o0_ref.shape[0]
    for i, o_ref in enumerate((o0_ref, o1_ref)):
        cut = slice(i * half, (i + 1) * half)
        part = dot(o_ref[...], g_ref[...]) + got_ref[0, cut, :].astype(F32) + moved_ref[0, cut, :].astype(F32)
        part = part.reshape(count // 2, 2, size, part.shape[1])
        low, high = part[:, 0], part[:, 1]
        out = slice(i * count // 2, (i + 1) * count // 2)
        send_ref[out] = jnp.where(mine == 0, high, low).astype(BF16)
        keep_ref[out] = jnp.where(mine == 0, low, high)


def keep_term(attn, grad_rows, columns, parts, got, moved, blocks):
    size, rows = attn[0].shape
    width = size * len(attn)
    cols = grad_rows.shape[1] // parts
    shape = (blocks // 2, width // blocks, cols)
    fixed = lambda shape: pl.BlockSpec(shape, lambda i, s: (0,) * len(shape))
    return pl.pallas_call(
        keep_kernel,
        grid_spec=pltpu.PrefetchScalarGridSpec(
            num_scalar_prefetch=1, grid=(1,),
            in_specs=[fixed((size, rows))] * 2 + [
                pl.BlockSpec((rows, cols), lambda i, s: (0, s[0])),
                pl.BlockSpec((1, width, cols), lambda i, s: (s[1], 0, 0)),
                fixed((1, width, cols)),
            ],
            out_specs=[fixed(shape)] * 2,
        ),
        out_shape=[jax.ShapeDtypeStruct(shape, BF16), jax.ShapeDtypeStruct(shape, F32)],
        compiler_params=PARAMS, cost_estimate=lasting(3), name="keep_term",
    )(columns, *map(in_hbm, attn), in_hbm(grad_rows), got, moved)


def swap(x, axis, bit):
    return lax.ppermute(x, axis, [(i, i ^ bit) for i in range(lax.axis_size(axis))])


def within_pair(x, to_odd):
    size = lax.axis_size("ctx")
    return lax.ppermute(x, "ctx", [(i, i + 1) if to_odd else (i + 1, i) for i in range(0, size, 2)])


def in_hbm(x):
    return pltpu.with_memory_space_constraint(x, pltpu.HBM)


def after(x, *others):
    return lax.optimization_barrier((x,) + others)[0]


def whole_of(x):
    return pl.BlockSpec(x.shape, lambda i, s: (0,) * x.ndim)


def stage_kernel(sel_ref, total_ref, got_ref, send_ref, keep_ref):
    mine = sel_ref[0]
    total = total_ref[...] + got_ref[...].astype(F32)
    total = total.reshape((send_ref.shape[0], 2) + send_ref.shape[1:])
    low, high = total[:, 0], total[:, 1]
    send_ref[...] = jnp.where(mine == 0, high, low).astype(BF16)
    keep_ref[...] = jnp.where(mine == 0, low, high)


def halves(total, got, axis, bit):
    mine = ((lax.axis_index(axis) // bit) % 2).astype(jnp.int32).reshape(1)
    out = lambda dtype: jax.ShapeDtypeStruct((total.shape[0] // 2,) + total.shape[1:], dtype)
    return pl.pallas_call(
        stage_kernel,
        grid_spec=pltpu.PrefetchScalarGridSpec(
            num_scalar_prefetch=1, grid=(1,), in_specs=[whole_of(total), whole_of(got)],
            out_specs=[whole_of(out(F32))] * 2,
        ),
        out_shape=[out(BF16), out(F32)],
        compiler_params=PARAMS, cost_estimate=lasting(1), name="stage",
    )(mine, total, got)


def last_kernel(total_ref, got_ref, out_ref):
    out_ref[...] = total_ref[...] + got_ref[...].astype(F32)


def last_sum(total, got):
    return pl.pallas_call(
        last_kernel, out_shape=jax.ShapeDtypeStruct(total.shape, F32),
        compiler_params=PARAMS, cost_estimate=lasting(1), name="last_sum",
    )(total, got)


def on_device(queries, keys, values, segment_ids, out_grad, out_weight):
    query_rows, key_rows, value_rows, grad_rows = queries[0], keys[0], values[0], out_grad[0]
    rows, width = query_rows.shape
    pairs = width // LANES
    chunks = 2
    size = width // chunks
    tag_rows = jnp.pad((segment_ids + 1).astype(BF16), ((0, 15), (0, 2 * size - rows)))
    odd = lax.axis_index("ctx") % 2 == 1
    mine, far, paired, passed = [], [], [], []
    for i in range(chunks):
        cut = slice(i * size, (i + 1) * size)
        mine.append(
            jnp.concatenate(
                [jnp.concatenate([key_rows[:, cut], value_rows[:, cut]], axis=1), tag_rows], axis=0
            )
        )
        far.append(shift(mine[i], 2))
    sent = queries_to_send(after(query_rows, *mine), grad_rows, out_weight)
    far[0] = after(far[0], sent)
    for i in range(chunks):
        paired.append(within_pair(mine[i], True))
        passed.append(within_pair(far[i], False))
    far_sent = shift(sent, -2)
    parts = [Attention(rows, width, chunks, i * pairs // chunks, pairs // chunks) for i in range(chunks)]
    window = lambda i: [mine[i], far[i], paired[i], passed[i]]
    attn, stats = [], []
    from_forward = sent
    for i in range(chunks):
        half, after_half = parts[i].forward(from_forward, window(i), stats)
        attn.append(half)
        stats = [after_half]
        if i == 0:
            relayed = jnp.where(odd, sent, after(far_sent, half))
            near_sent = swap(relayed, "ctx", 1)
            from_forward = after(sent, relayed)
    stats = stats[0]
    near_stats = shift(stats, -1)
    far_stats = shift(stats, -2)

    shares = lax.axis_size("dp")
    count = lax.axis_size("ctx")
    me = lax.axis_index("dp").astype(jnp.int32)
    core, chip = me % 2, me // 2
    low = lax.axis_index("ctx").astype(jnp.int32) % 2
    pick = lambda part, entry: jnp.stack([part, entry, low])
    got = swap(weight_term(attn, grad_rows, pick(1 - core, core), shares, None, BF16), "dp", 1)
    to_chip = weight_term(attn, grad_rows, pick(2 * (1 - chip) + core, 1 - chip), shares, got, BF16)
    moved = swap(to_chip, "dp", 2)
    query_grad = []
    for i in range(chunks):
        query_grad = parts[i].query(sent, stats, window(i), query_grad)
    query_grad = query_grad[0]
    moved = after(moved, query_grad, near_stats, far_stats)
    send, kept = keep_term(attn, grad_rows, pick(me, chip), shares, got, moved, count)

    pieces_of_keys = [(0, 2), (2, 1), (3, 1)]
    key_value = []
    stage = 0
    bit = 1
    while bit < count:
        moved = swap(send, "ctx", bit)
        if stage < len(pieces_of_keys):
            first, some = pieces_of_keys[stage]
            tied, send = lax.optimization_barrier((stats, send))
            sources = [(sent, tied), (near_sent, near_stats), (far_sent, far_stats)]
            held = mine[first * chunks // pairs]
            key_value = Attention(rows, width, chunks, first, some).key(held, sources, key_value)
            moved = after(moved, *key_value)
            stage += 1
        bit *= 2
        if bit < count:
            send, kept = halves(kept, moved, "ctx", bit)
    weight_grad = last_sum(kept[0], moved[0])
    key_grad, value_grad = key_value
    return query_grad[None], key_grad[None], value_grad[None], weight_grad


def solution(mesh):
    rows = P("dp", "ctx", None)
    return jax.shard_map(
        on_device,
        mesh=mesh,
        in_specs=(rows, rows, rows, P("dp", "ctx"), rows, P()),
        out_specs=(rows, rows, rows, P("ctx", "dp")),
        check_vma=False,
    )
```

time: 128 us -> 116 us (0.906)
  other arithmetic: 13.3 us -> 3.33 us
  waiting for transfers between devices: 22.7 us -> 14.7 us
  starting transfers between devices: 27.7 us -> 33.3 us
  Pallas kernels: 55.3 us -> 59.9 us
  local copies, waits for them, and re-layouts: 7.61 us -> 3.17 us
    ppermute x0 -> x4, starting transfers between devices: none -> 13 us  [within_pair(): lax.ppermute(x, 'ctx', [(i, i + 1) if to_odd else (i + 1, i) for i in ran...]
    ppermute x5, waiting for transfers between devices: 17.8 us -> 6.51 us  [shift(): return lax.ppermute(x, 'ctx', pairs)]
    pallas_call x6 -> x11, Pallas kernels: 46.2 us -> 52.3 us  [the longest x7 49.2 us: call(): pl.pallas_call(functools.partial(kernel, self.first), grid=(self.count,),...]
    ppermute x8 -> x6, starting transfers between devices: 12.4 us -> 6.5 us  [swap(): lax.ppermute(x, axis, [(i, i ^ bit) for i in range(lax.axis_size(axis))])]
    ppermute x0 -> x4, waiting for transfers between devices: none -> 5.25 us  [within_pair(): lax.ppermute(x, 'ctx', [(i, i + 1) if to_odd else (i + 1, i) for i in ran...]
    unnamed x34 -> x18, local copies, waits for them, and re-layouts: 6.21 us -> 1.77 us
    add x3 -> x0, other arithmetic: 3.91 us -> none  [the longest x1 1.7 us: halves(): lax.dynamic_index_in_dim(total, which, 1, keepdims=False)]
    select_n x3 -> x1, other arithmetic: 5.24 us -> 2.41 us  [on_device(): relayed = jnp.where(odd, sent, after(far_sent, half))]
  transfers between devices with their start and end apart: 13 -> 15, of which waited for: 6 -> 6; matrix products, arithmetic and copies ran while one was open for 6% -> 2% of each run, Pallas kernels for 36% -> 42%
where the time goes in v1:
time: 116 us; the launch traced here: 115 us
  Pallas kernels  59.9 us (52%)
  starting transfers between devices  33.3 us (29%)
  waiting for transfers between devices  14.7 us (13%)
  other arithmetic  3.33 us (3%)
  local copies, waits for them, and re-layouts  3.17 us (3%)
    pallas_call x7, Pallas kernels, call(): pl.pallas_call(functools.partial(kernel, self.first), grid=(self.count,),...  49.2 us
    ppermute x5, starting transfers between devices, shift(): return lax.ppermute(x, 'ctx', pairs)  13.7 us
    ppermute x4, starting transfers between devices, within_pair(): lax.ppermute(x, 'ctx', [(i, i + 1) if to_odd else (i + 1, i) for i in ran...  13 us
    ppermute x5, waiting for transfers between devices, shift(): return lax.ppermute(x, 'ctx', pairs)  6.51 us
    ppermute x6, starting transfers between devices, swap(): lax.ppermute(x, axis, [(i, i ^ bit) for i in range(lax.axis_size(axis))])  6.5 us
    pallas_call x2, Pallas kernels, weight_term(): pl.pallas_call(weight_kernel, grid_spec=pltpu.PrefetchScalarGridSpec(num_...  5.8 us
    ppermute x4, waiting for transfers between devices, within_pair(): lax.ppermute(x, 'ctx', [(i, i + 1) if to_odd else (i + 1, i) for i in ran...  5.25 us
    ppermute x6, waiting for transfers between devices, swap(): lax.ppermute(x, axis, [(i, i ^ bit) for i in range(lax.axis_size(axis))])  2.91 us
  transfers between devices with their start and end apart: 15, of which 6 were waited for; matrix products, arithmetic and copies ran while one was open for 2% of the time, Pallas kernels for 42%

profile of v1, /device:TPU:0, one launch (start us, length us, event | category | flops | bytes accessed | tf_op | source)
XLA Modules:
  0.0 115.3 jit_solution(11227026961805898166)
XLA Ops:
  0.6 0.7 add_convert_fusion
  1.3 0.0 copy-start.5
  1.3 1.4 %fusion.3 = (bf16[512,256]{1,0:T(8,128)(2,1)S(1)}, bf16[512,256]{1,0:T(8,128)(2,1)S(1)}, bf16[512,256]{1,0:T(8,128)(2,1)S(1)}, bf16[512,256]{1,0:T(8,128)(2,1)S(1)}) fusion(bf16[512,512]{1,0:T(8,128)(2,1)} %bitcast.28, bf16[512,512]{1,0:T(8,128)(2,1)} %bitcast.29), kind=kLoop, calls=%fused_computation.9 | loop fusion | bytes 2097152 | tf_op jit(solution)/shard_map/slice | solution.py:444
  2.7 0.0 copy-start.1
  2.7 0.1 fusion.2
  2.8 5.1 %collective-permute-start.1 = (bf16[528,512]{1,0:T(8,128)(2,1)S(1)}, bf16[528,512]{1,0:T(8,128)(2,1)S(1)}, u32[]{:S(2)}, u32[]{:S(2)}) collective-permute-start(bf16[528,512]{1,0:T(8,128)(2,1)S(1)} %get-tuple-element.63.kc.vc.tc.k_ref.v_ref.t_ref), channel_id=1, source_target_pairs={{0,8},{4,12},{8,16},{12,20},{16,24},{20,28},{1,9},{5,13},{9,17},{1... | collective-permute-start | bytes 1622024 | tf_op jit(solution)/shard_map/ppermute | solution.py:25
  7.9 0.0 copy-done.5
  7.9 0.0 copy-done.1
  7.9 0.0 copy-start.6
  8.0 1.0 copy-done.6
  9.0 1.8 %queries_to_send.1.q_ref.g_ref.qc.gc = bf16[512,1024]{1,0:T(8,128)(2,1)S(1)} custom-call(bf16[512,512]{1,0:T(8,128)(2,1)S(1)} %bitcast.22, bf16[512,2048]{1,0:T(8,128)(2,1)S(1)} %bitcast.21, bf16[512,2048]{1,0:T(8,128)(2,1)S(1)} %copy-done.5), custom_call_target="tpu_custom_call" | custom-call | bytes 17500000 | tf_op jit(solution)/shard_map/queries_to_send/pallas_call | solution.py:297
  10.8 0.0 copy-start
  10.8 1.3 %collective-permute-start = (bf16[512,1024]{1,0:T(8,128)(2,1)S(1)}, bf16[512,1024]{1,0:T(8,128)(2,1)}, u32[]{:S(2)}, u32[]{:S(2)}) collective-permute-start(bf16[512,1024]{1,0:T(8,128)(2,1)S(1)} %queries_to_send.1.q_ref.g_ref.qc.gc), channel_id=1, source_target_pairs={{8,0},{12,4},{16,8},{20,12},{24,16},{28,20},{9,1},{13,5},{17,9},{2... | collective-permute-start | bytes 3145736 | tf_op jit(solution)/shard_map/ppermute | solution.py:25
  12.1 4.6 %collective-permute-start.4 = (bf16[528,512]{1,0:T(8,128)(2,1)S(1)}, bf16[528,512]{1,0:T(8,128)(2,1)S(1)}, u32[]{:S(2)}, u32[]{:S(2)}) collective-permute-start(bf16[528,512]{1,0:T(8,128)(2,1)S(1)} %get-tuple-element.62.kc.vc.tc.k_ref.v_ref.t_ref), channel_id=1, source_target_pairs={{0,8},{4,12},{8,16},{12,20},{16,24},{20,28},{1,9},{5,13},{9,17},{1... | collective-permute-start | bytes 1622024 | tf_op jit(solution)/shard_map/ppermute | solution.py:25
  16.7 4.3 %collective-permute-start.2 = (bf16[528,512]{1,0:T(8,128)(2,1)S(1)}, bf16[528,512]{1,0:T(8,128)(2,1)}, u32[]{:S(2)}, u32[]{:S(2)}) collective-permute-start(bf16[528,512]{1,0:T(8,128)(2,1)S(1)} %get-tuple-element.63.kc.vc.tc.k_ref.v_ref.t_ref), channel_id=1, source_target_pairs={{0,4},{8,12},{16,20},{24,28},{1,5},{9,13},{17,21},{25,29},{2,6},{1... | collective-permute-start | bytes 1622024 | tf_op jit(solution)/shard_map/ppermute | solution.py:382
  21.0 0.0 collective-permute-done.1.ka.va.ta
  21.0 1.3 %collective-permute-start.3 = (bf16[528,512]{1,0:T(8,128)(2,1)S(1)}, bf16[528,512]{1,0:T(8,128)(2,1)}, u32[]{:S(2)}, u32[]{:S(2)}) collective-permute-start(bf16[528,512]{1,0:T(8,128)(2,1)S(1)} %collective-permute-done.1.ka.va.ta), channel_id=1, source_target_pairs={{4,0},{12,8},{20,16},{28,24},{5,1},{13,9},{21,17},{29,25},{6,2},{1... | collective-permute-start | bytes 1622024 | tf_op jit(solution)/shard_map/ppermute | solution.py:382
  22.3 6.2 %collective-permute-start.5 = (bf16[528,512]{1,0:T(8,128)(2,1)S(1)}, bf16[528,512]{1,0:T(8,128)(2,1)}, u32[]{:S(2)}, u32[]{:S(2)}) collective-permute-start(bf16[528,512]{1,0:T(8,128)(2,1)S(1)} %get-tuple-element.62.kc.vc.tc.k_ref.v_ref.t_ref), channel_id=1, source_target_pairs={{0,4},{8,12},{16,20},{24,28},{1,5},{9,13},{17,21},{25,29},{2,6},{1... | collective-permute-start | bytes 1622024 | tf_op jit(solution)/shard_map/ppermute | solution.py:382
  28.5 2.5 %collective-permute-done.4.ka.va.ta = bf16[528,512]{1,0:T(8,128)(2,1)S(1)} collective-permute-done((bf16[528,512]{1,0:T(8,128)(2,1)S(1)}, bf16[528,512]{1,0:T(8,128)(2,1)S(1)}, u32[]{:S(2)}, u32[]{:S(2)}) %collective-permute-start.4) | collective-permute-done | bytes 540704 | tf_op jit(solution)/shard_map/ppermute | solution.py:25
  31.0 1.3 %collective-permute-start.6 = (bf16[528,512]{1,0:T(8,128)(2,1)S(1)}, bf16[528,512]{1,0:T(8,128)(2,1)}, u32[]{:S(2)}, u32[]{:S(2)}) collective-permute-start(bf16[528,512]{1,0:T(8,128)(2,1)S(1)} %collective-permute-done.4.ka.va.ta), channel_id=1, source_target_pairs={{4,0},{12,8},{20,16},{28,24},{5,1},{13,9},{21,17},{29,25},{6,2},{1... | collective-permute-start | bytes 1622024 | tf_op jit(solution)/shard_map/ppermute | solution.py:382
  32.3 0.1 add_add_fusion.1.sel_ref
  32.4 0.5 collective-permute-done.2.ke.ve.te
  32.8 4.3 %collective-permute-done.3.ko.vo.to = bf16[528,512]{1,0:T(8,128)(2,1)} collective-permute-done((bf16[528,512]{1,0:T(8,128)(2,1)S(1)}, bf16[528,512]{1,0:T(8,128)(2,1)}, u32[]{:S(2)}, u32[]{:S(2)}) %collective-permute-start.3) | collective-permute-done | bytes 540704 | tf_op jit(solution)/shard_map/ppermute | solution.py:382
  37.1 7.4 %forward_kernel.2 = (bf16[256,512]{1,0:T(8,128)(2,1)S(1)}, bf16[512,128]{1,0:T(8,128)(2,1)S(1)}) custom-call(bf16[512,1024]{1,0:T(8,128)(2,1)S(1)} %queries_to_send.1.q_ref.g_ref.qc.gc, bf16[512,1024]{1,0:T(8,128)(2,1)S(1)} %queries_to_send.1.q_ref.g_ref.qc.gc, bf16[528,512]{1,0:T(8,128)(2,1)S(1)} %get-tuple-element.63.kc.vc.tc.k_ref.v_ref.t_ref, ...), custom_call_target="tpu_custom_call" | custom-call | bytes 24500000 | tf_op jit(solution)/shard_map/forward_kernel/pallas_call | solution.py:247
  44.5 0.0 copy-start.3
  44.5 0.0 collective-permute-done.qe.ge
  44.5 2.4 %broadcast_select_fusion = bf16[512,1024]{1,0:T(8,128)(2,1)} fusion(bf16[512,1024]{1,0:T(8,128)(2,1)S(1)} %queries_to_send.1.q_ref.g_ref.qc.gc, bf16[512,1024]{1,0:T(8,128)(2,1)} %collective-permute-done.qe.ge, pred[]{:T(512)S(6)} %eq.9), kind=kLoop, calls=%fused_computation.2 | loop fusion | flops 524288 | bytes 3145729 | tf_op jit(solution)/shard_map/jit(_where)/select_n | solution.py:463
  46.9 0.0 copy-done.3
  46.9 0.0 collective-permute-done.5.ke.ve.te
  46.9 0.5 collective-permute-done.6.ko.vo.to
  47.5 7.4 %forward_kernel.3 = (bf16[256,512]{1,0:T(8,128)(2,1)S(1)}, bf16[512,128]{1,0:T(8,128)(2,1)S(1)}) custom-call(bf16[512,1024]{1,0:T(8,128)(2,1)S(1)} %queries_to_send.1.q_ref.g_ref.qc.gc, bf16[512,1024]{1,0:T(8,128)(2,1)S(1)} %queries_to_send.1.q_ref.g_ref.qc.gc, bf16[528,512]{1,0:T(8,128)(2,1)S(1)} %get-tuple-element.62.kc.vc.tc.k_ref.v_ref.t_ref, ...), custom_call_target="tpu_custom_call" | custom-call | bytes 24500000 | tf_op jit(solution)/shard_map/forward_kernel/pallas_call | solution.py:247
  54.8 0.0 copy-start.4
  54.8 0.7 copy-done.4
  55.5 3.5 %weight_term.2 = bf16[2,512,512]{2,1,0:T(8,128)(2,1)} custom-call(s32[3]{0:T(128)S(1)} %add_add_fusion.1.sel_ref, bf16[256,512]{1,0:T(8,128)(2,1)} %copy-done.3, bf16[256,512]{1,0:T(8,128)(2,1)} %copy-done.4, bf16[512,2048]{1,0:T(8,128)(2,1)} %bitcast.18), custom_call_target="tpu_custom_call" | custom-call | bytes 10500000 | tf_op jit(solution)/shard_map/weight_term/pallas_call | solution.py:327
  59.0 0.0 collective-permute-start.7
  59.0 0.0 collective-permute-start.12
  59.0 0.1 add_add_fusion
  59.1 2.9 %collective-permute-done.7.refs_3_.got_ref = bf16[2,512,512]{2,1,0:T(8,128)(2,1)} collective-permute-done((bf16[2,512,512]{2,1,0:T(8,128)(2,1)}, bf16[2,512,512]{2,1,0:T(8,128)(2,1)}, u32[]{:S(2)}, u32[]{:S(2)}) %collective-permute-start.7) | collective-permute-done | bytes 1048608 | tf_op jit(solution)/shard_map/ppermute | solution.py:377
  62.0 2.3 %weight_term.3 = bf16[1,512,512]{2,1,0:T(8,128)(2,1)S(1)} custom-call(s32[3]{0:T(128)S(1)} %get-tuple-element.67.sel_ref, bf16[256,512]{1,0:T(8,128)(2,1)} %copy-done.3, bf16[256,512]{1,0:T(8,128)(2,1)} %copy-done.4, bf16[512,2048]{1,0:T(8,128)(2,1)} %bitcast.19, bf16[2,512,512]{2,1,0:T(8,128)(2,1)} %collective-permute-done.7.refs_3_.got_ref), custom_call_target="tpu_custom_call" | custom-call | bytes 10500000 | tf_op jit(solution)/shard_map/weight_term/pallas_call | solution.py:327
  64.4 1.6 %collective-permute-start.8 = (bf16[1,512,512]{2,1,0:T(8,128)(2,1)S(1)}, bf16[1,512,512]{2,1,0:T(8,128)(2,1)S(1)}, u32[]{:S(2)}, u32[]{:S(2)}) collective-permute-start(bf16[1,512,512]{2,1,0:T(8,128)(2,1)S(1)} %weight_term.3), channel_id=1, source_target_pairs={{0,2},{1,3},{2,0},{3,1},{4,6},{5,7},{6,4},{7,5},{8,10},{9,11},{10,... | collective-permute-start | bytes 1572872 | tf_op jit(solution)/shard_map/ppermute | solution.py:377
  65.9 1.3 %collective-permute-start.10 = (bf16[512,128]{1,0:T(8,128)(2,1)S(1)}, bf16[512,128]{1,0:T(8,128)(2,1)S(1)}, u32[]{:S(2)}, u32[]{:S(2)}) collective-permute-start(bf16[512,128]{1,0:T(8,128)(2,1)S(1)} %get-tuple-element.53.st_ref.sc), channel_id=1, source_target_pairs={{8,0},{12,4},{16,8},{20,12},{24,16},{28,20},{9,1},{13,5},{17,9},{2... | collective-permute-start | bytes 393224 | tf_op jit(solution)/shard_map/ppermute | solution.py:25
  67.2 1.5 %collective-permute-start.9 = (bf16[512,128]{1,0:T(8,128)(2,1)S(1)}, bf16[512,128]{1,0:T(8,128)(2,1)S(1)}, u32[]{:S(2)}, u32[]{:S(2)}) collective-permute-start(bf16[512,128]{1,0:T(8,128)(2,1)S(1)} %get-tuple-element.53.st_ref.sc), channel_id=1, source_target_pairs={{4,0},{8,4},{12,8},{16,12},{20,16},{24,20},{28,24},{5,1},{9,5},{13... | collective-permute-start | bytes 393224 | tf_op jit(solution)/shard_map/ppermute | solution.py:25
  68.7 7.5 %query_kernel.2.rest_0_ = bf16[512,512]{1,0:T(8,128)(2,1)} custom-call(bf16[512,1024]{1,0:T(8,128)(2,1)S(1)} %queries_to_send.1.q_ref.g_ref.qc.gc, bf16[512,1024]{1,0:T(8,128)(2,1)S(1)} %queries_to_send.1.q_ref.g_ref.qc.gc, bf16[512,128]{1,0:T(8,128)(2,1)S(1)} %get-tuple-element.53.st_ref.sc, ...), custom_call_target="tpu_custom_call" | custom-call | bytes 24500000 | tf_op jit(solution)/shard_map/query_kernel/pallas_call | solution.py:247
  76.1 0.0 copy-done
  76.1 0.0 copy-done.2
  76.1 7.5 %query_kernel.3 = bf16[512,512]{1,0:T(8,128)(2,1)} custom-call(bf16[512,1024]{1,0:T(8,128)(2,1)S(1)} %queries_to_send.1.q_ref.g_ref.qc.gc, bf16[512,1024]{1,0:T(8,128)(2,1)S(1)} %queries_to_send.1.q_ref.g_ref.qc.gc, bf16[512,128]{1,0:T(8,128)(2,1)S(1)} %get-tuple-element.53.st_ref.sc, ...), custom_call_target="tpu_custom_call", output_to_operand_aliasing={{}: (15, {})} | custom-call | bytes 24500000 | tf_op jit(solution)/shard_map/query_kernel/pallas_call | solution.py:247
  83.6 0.0 collective-permute-done.10.se
  83.6 4.0 %collective-permute-done.9.sd = bf16[512,128]{1,0:T(8,128)(2,1)S(1)} collective-permute-done((bf16[512,128]{1,0:T(8,128)(2,1)S(1)}, bf16[512,128]{1,0:T(8,128)(2,1)S(1)}, u32[]{:S(2)}, u32[]{:S(2)}) %collective-permute-start.9) | collective-permute-done | bytes 131104 | tf_op jit(solution)/shard_map/ppermute | solution.py:25
  87.6 0.0 collective-permute-done.8.moved_ref
  87.6 2.4 %keep_term.1 = (bf16[4,64,512]{2,1,0:T(8,128)(2,1)S(1)}, f32[4,64,512]{2,1,0:T(8,128)S(1)}) custom-call(s32[3]{0:T(128)S(1)} %get-tuple-element.66.sel_ref, bf16[256,512]{1,0:T(8,128)(2,1)} %copy-done.3, bf16[256,512]{1,0:T(8,128)(2,1)} %copy-done.4, bf16[512,2048]{1,0:T(8,128)(2,1)} %bitcast.20, ...), custom_call_target="tpu_custom_call" | custom-call | bytes 10500000 | tf_op jit(solution)/shard_map/keep_term/pallas_call | solution.py:360
  90.0 0.0 copy-done.7
  90.0 0.0 copy-done.8
  90.0 0.1 collective-permute-start.11
  90.1 0.0 collective-permute-done.12.qd.gd
  90.1 8.9 %key_kernel.3 = (bf16[512,512]{1,0:T(8,128)(2,1)}, bf16[512,512]{1,0:T(8,128)(2,1)}) custom-call(bf16[528,512]{1,0:T(8,128)(2,1)S(1)} %get-tuple-element.63.kc.vc.tc.k_ref.v_ref.t_ref, bf16[528,512]{1,0:T(8,128)(2,1)S(1)} %get-tuple-element.63.kc.vc.tc.k_ref.v_ref.t_ref, bf16[528,512]{1,0:T(8,128)(2,1)S(1)} %get-tuple-element.63.kc.vc.tc.k_ref.v_ref.t_ref, ...), custom_call_target="tpu_custom_call" | custom-call | bytes 29400000 | tf_op jit(solution)/shard_map/key_kernel/pallas_call | solution.py:247
  99.0 0.0 collective-permute-done.11.got_ref
  99.0 0.1 stage.2
  99.1 1.6 %collective-permute-start.13 = (bf16[2,64,512]{2,1,0:T(8,128)(2,1)S(1)}, bf16[2,64,512]{2,1,0:T(8,128)(2,1)S(1)}, u32[]{:S(2)}, u32[]{:S(2)}) collective-permute-start(bf16[2,64,512]{2,1,0:T(8,128)(2,1)S(1)} %get-tuple-element.47), channel_id=1, source_target_pairs={{0,8},{4,12},{8,0},{12,4},{16,24},{20,28},{24,16},{28,20},{1,9},{5... | collective-permute-start | bytes 393224 | tf_op jit(solution)/shard_map/ppermute | solution.py:377
  100.7 5.3 %key_kernel.4 = (bf16[512,512]{1,0:T(8,128)(2,1)}, bf16[512,512]{1,0:T(8,128)(2,1)}) custom-call(bf16[528,512]{1,0:T(8,128)(2,1)S(1)} %get-tuple-element.62.kc.vc.tc.k_ref.v_ref.t_ref, bf16[528,512]{1,0:T(8,128)(2,1)S(1)} %get-tuple-element.62.kc.vc.tc.k_ref.v_ref.t_ref, ...), custom_call_target="tpu_custom_call", output_to_operand_aliasing={{0}: (12, {}), {1}: (13, {})} | custom-call | bytes 14700000 | tf_op jit(solution)/shard_map/key_kernel/pallas_call | solution.py:247
  106.0 0.0 collective-permute-done.13.got_ref
  106.0 3.3 %collective-permute-start.14 = (bf16[1,64,512]{2,1,0:T(8,128)(2,1)S(1)}, bf16[1,64,512]{2,1,0:T(8,128)(2,1)S(1)}, u32[]{:S(2)}, u32[]{:S(2)}) collective-permute-start(bf16[1,64,512]{2,1,0:T(8,128)(2,1)S(1)} %get-tuple-element.52), channel_id=1, source_target_pairs={{0,16},{4,20},{8,24},{12,28},{16,0},{20,4},{24,8},{28,12},{1,17},{... | collective-permute-start | bytes 196616 | tf_op jit(solution)/shard_map/ppermute | solution.py:377
  109.3 5.3 %key_kernel.5 = (bf16[512,512]{1,0:T(8,128)(2,1)}, bf16[512,512]{1,0:T(8,128)(2,1)}) custom-call(bf16[528,512]{1,0:T(8,128)(2,1)S(1)} %get-tuple-element.62.kc.vc.tc.k_ref.v_ref.t_ref, bf16[528,512]{1,0:T(8,128)(2,1)S(1)} %get-tuple-element.62.kc.vc.tc.k_ref.v_ref.t_ref, ...), custom_call_target="tpu_custom_call", output_to_operand_aliasing={{0}: (12, {}), {1}: (13, {})} | custom-call | bytes 14700000 | tf_op jit(solution)/shard_map/key_kernel/pallas_call | solution.py:247
  114.6 0.0 collective-permute-done.14
  114.6 0.7 last_sum.1
  (4 shorter events, 0.0 us)
Async XLA Ops:
  1.3 6.6 %copy-start.5 = (bf16[512,2048]{1,0:T(8,128)(2,1)S(1)}, bf16[512,2048]{1,0:T(8,128)(2,1)}, u32[]{:S(2)}) copy-start(bf16[512,2048]{1,0:T(8,128)(2,1)} %w_ref.1) | copy-start | bytes 6291460
  2.7 5.2 %copy-start.1 = (bf16[1,512,2048]{2,1,0:T(8,128)(2,1)S(1)}, bf16[1,512,2048]{2,1,0:T(8,128)(2,1)}, u32[]{:S(2)}) copy-start(bf16[1,512,2048]{2,1,0:T(8,128)(2,1)} %param.10) | copy-start | bytes 6291460
  2.8 18.2 %collective-permute-start.1 = (bf16[528,512]{1,0:T(8,128)(2,1)S(1)}, bf16[528,512]{1,0:T(8,128)(2,1)S(1)}, u32[]{:S(2)}, u32[]{:S(2)}) collective-permute-start(bf16[528,512]{1,0:T(8,128)(2,1)S(1)} %get-tuple-element.63.kc.vc.tc.k_ref.v_ref.t_ref), channel_id=1, source_target_pairs={{0,8},{4,12},{8,16},{12,20},{16,24},{20,28},{1,9},{5,13},{9,17},{1... | collective-permute-start | bytes 1622024 | tf_op jit(solution)/shard_map/ppermute | solution.py:25
  7.9 1.0 copy-start.6
  10.8 65.3 %copy-start = (bf16[512,1024]{1,0:T(8,128)(2,1)}, bf16[512,1024]{1,0:T(8,128)(2,1)S(1)}, u32[]{:S(2)}) copy-start(bf16[512,1024]{1,0:T(8,128)(2,1)S(1)} %queries_to_send.1.q_ref.g_ref.qc.gc) | copy-start | bytes 3145732
  10.8 33.7 %collective-permute-start = (bf16[512,1024]{1,0:T(8,128)(2,1)S(1)}, bf16[512,1024]{1,0:T(8,128)(2,1)}, u32[]{:S(2)}, u32[]{:S(2)}) collective-permute-start(bf16[512,1024]{1,0:T(8,128)(2,1)S(1)} %queries_to_send.1.q_ref.g_ref.qc.gc), channel_id=1, source_target_pairs={{8,0},{12,4},{16,8},{20,12},{24,16},{28,20},{9,1},{13,5},{17,9},{2... | collective-permute-start | bytes 3145736 | tf_op jit(solution)/shard_map/ppermute | solution.py:25
  12.1 18.9 %collective-permute-start.4 = (bf16[528,512]{1,0:T(8,128)(2,1)S(1)}, bf16[528,512]{1,0:T(8,128)(2,1)S(1)}, u32[]{:S(2)}, u32[]{:S(2)}) collective-permute-start(bf16[528,512]{1,0:T(8,128)(2,1)S(1)} %get-tuple-element.62.kc.vc.tc.k_ref.v_ref.t_ref), channel_id=1, source_target_pairs={{0,8},{4,12},{8,16},{12,20},{16,24},{20,28},{1,9},{5,13},{9,17},{1... | collective-permute-start | bytes 1622024 | tf_op jit(solution)/shard_map/ppermute | solution.py:25
  16.7 16.1 %collective-permute-start.2 = (bf16[528,512]{1,0:T(8,128)(2,1)S(1)}, bf16[528,512]{1,0:T(8,128)(2,1)}, u32[]{:S(2)}, u32[]{:S(2)}) collective-permute-start(bf16[528,512]{1,0:T(8,128)(2,1)S(1)} %get-tuple-element.63.kc.vc.tc.k_ref.v_ref.t_ref), channel_id=1, source_target_pairs={{0,4},{8,12},{16,20},{24,28},{1,5},{9,13},{17,21},{25,29},{2,6},{1... | collective-permute-start | bytes 1622024 | tf_op jit(solution)/shard_map/ppermute | solution.py:382
  21.0 16.1 %collective-permute-start.3 = (bf16[528,512]{1,0:T(8,128)(2,1)S(1)}, bf16[528,512]{1,0:T(8,128)(2,1)}, u32[]{:S(2)}, u32[]{:S(2)}) collective-permute-start(bf16[528,512]{1,0:T(8,128)(2,1)S(1)} %collective-permute-done.1.ka.va.ta), channel_id=1, source_target_pairs={{4,0},{12,8},{20,16},{28,24},{5,1},{13,9},{21,17},{29,25},{6,2},{1... | collective-permute-start | bytes 1622024 | tf_op jit(solution)/shard_map/ppermute | solution.py:382
  22.3 24.7 %collective-permute-start.5 = (bf16[528,512]{1,0:T(8,128)(2,1)S(1)}, bf16[528,512]{1,0:T(8,128)(2,1)}, u32[]{:S(2)}, u32[]{:S(2)}) collective-permute-start(bf16[528,512]{1,0:T(8,128)(2,1)S(1)} %get-tuple-element.62.kc.vc.tc.k_ref.v_ref.t_ref), channel_id=1, source_target_pairs={{0,4},{8,12},{16,20},{24,28},{1,5},{9,13},{17,21},{25,29},{2,6},{1... | collective-permute-start | bytes 1622024 | tf_op jit(solution)/shard_map/ppermute | solution.py:382
  31.0 16.5 %collective-permute-start.6 = (bf16[528,512]{1,0:T(8,128)(2,1)S(1)}, bf16[528,512]{1,0:T(8,128)(2,1)}, u32[]{:S(2)}, u32[]{:S(2)}) collective-permute-start(bf16[528,512]{1,0:T(8,128)(2,1)S(1)} %collective-permute-done.4.ka.va.ta), channel_id=1, source_target_pairs={{4,0},{12,8},{20,16},{28,24},{5,1},{13,9},{21,17},{29,25},{6,2},{1... | collective-permute-start | bytes 1622024 | tf_op jit(solution)/shard_map/ppermute | solution.py:382
  44.5 2.4 %copy-start.3 = (bf16[256,512]{1,0:T(8,128)(2,1)}, bf16[256,512]{1,0:T(8,128)(2,1)S(1)}, u32[]{:S(2)}) copy-start(bf16[256,512]{1,0:T(8,128)(2,1)S(1)} %get-tuple-element.33.refs_0_.o0_ref) | copy-start | bytes 786436
  54.8 0.7 copy-start.4
  55.5 20.6 %copy-start.2 = (bf16[512,128]{1,0:T(8,128)(2,1)}, bf16[512,128]{1,0:T(8,128)(2,1)S(1)}, u32[]{:S(2)}) copy-start(bf16[512,128]{1,0:T(8,128)(2,1)S(1)} %get-tuple-element.53.st_ref.sc) | copy-start | bytes 393220
  59.0 3.0 %collective-permute-start.7 = (bf16[2,512,512]{2,1,0:T(8,128)(2,1)}, bf16[2,512,512]{2,1,0:T(8,128)(2,1)}, u32[]{:S(2)}, u32[]{:S(2)}) collective-permute-start(bf16[2,512,512]{2,1,0:T(8,128)(2,1)} %weight_term.2), channel_id=1, source_target_pairs={{0,1},{1,0},{2,3},{3,2},{4,5},{5,4},{6,7},{7,6},{8,9},{9,8},{10,11... | collective-permute-start | bytes 3145736 | tf_op jit(solution)/shard_map/ppermute | solution.py:377
  59.0 31.1 %collective-permute-start.12 = (bf16[512,1024]{1,0:T(8,128)(2,1)}, bf16[512,1024]{1,0:T(8,128)(2,1)}, u32[]{:S(2)}, u32[]{:S(2)}) collective-permute-start(bf16[512,1024]{1,0:T(8,128)(2,1)} %broadcast_select_fusion), channel_id=1, source_target_pairs={{0,4},{4,0},{8,12},{12,8},{16,20},{20,16},{24,28},{28,24},{1,5},{5... | collective-permute-start | bytes 3145736 | tf_op jit(solution)/shard_map/ppermute | solution.py:377
  64.4 23.2 %collective-permute-start.8 = (bf16[1,512,512]{2,1,0:T(8,128)(2,1)S(1)}, bf16[1,512,512]{2,1,0:T(8,128)(2,1)S(1)}, u32[]{:S(2)}, u32[]{:S(2)}) collective-permute-start(bf16[1,512,512]{2,1,0:T(8,128)(2,1)S(1)} %weight_term.3), channel_id=1, source_target_pairs={{0,2},{1,3},{2,0},{3,1},{4,6},{5,7},{6,4},{7,5},{8,10},{9,11},{10,... | collective-permute-start | bytes 1572872 | tf_op jit(solution)/shard_map/ppermute | solution.py:377
  65.9 17.7 %collective-permute-start.10 = (bf16[512,128]{1,0:T(8,128)(2,1)S(1)}, bf16[512,128]{1,0:T(8,128)(2,1)S(1)}, u32[]{:S(2)}, u32[]{:S(2)}) collective-permute-start(bf16[512,128]{1,0:T(8,128)(2,1)S(1)} %get-tuple-element.53.st_ref.sc), channel_id=1, source_target_pairs={{8,0},{12,4},{16,8},{20,12},{24,16},{28,20},{9,1},{13,5},{17,9},{2... | collective-permute-start | bytes 393224 | tf_op jit(solution)/shard_map/ppermute | solution.py:25
  67.2 20.4 %collective-permute-start.9 = (bf16[512,128]{1,0:T(8,128)(2,1)S(1)}, bf16[512,128]{1,0:T(8,128)(2,1)S(1)}, u32[]{:S(2)}, u32[]{:S(2)}) collective-permute-start(bf16[512,128]{1,0:T(8,128)(2,1)S(1)} %get-tuple-element.53.st_ref.sc), channel_id=1, source_target_pairs={{4,0},{8,4},{12,8},{16,12},{20,16},{24,20},{28,24},{5,1},{9,5},{13... | collective-permute-start | bytes 393224 | tf_op jit(solution)/shard_map/ppermute | solution.py:25
  83.6 6.4 %copy-start.7 = (bf16[512,128]{1,0:T(8,128)(2,1)}, bf16[512,128]{1,0:T(8,128)(2,1)S(1)}, u32[]{:S(2)}) copy-start(bf16[512,128]{1,0:T(8,128)(2,1)S(1)} %collective-permute-done.10.se) | copy-start | bytes 393220
  87.6 2.4 %copy-start.8 = (bf16[512,128]{1,0:T(8,128)(2,1)}, bf16[512,128]{1,0:T(8,128)(2,1)S(1)}, u32[]{:S(2)}) copy-start(bf16[512,128]{1,0:T(8,128)(2,1)S(1)} %collective-permute-done.9.sd) | copy-start | bytes 393220
  90.0 9.0 %collective-permute-start.11 = (bf16[4,64,512]{2,1,0:T(8,128)(2,1)S(1)}, bf16[4,64,512]{2,1,0:T(8,128)(2,1)S(1)}, u32[]{:S(2)}, u32[]{:S(2)}) collective-permute-start(bf16[4,64,512]{2,1,0:T(8,128)(2,1)S(1)} %get-tuple-element.41), channel_id=1, source_target_pairs={{0,4},{4,0},{8,12},{12,8},{16,20},{20,16},{24,28},{28,24},{1,5},{5... | collective-permute-start | bytes 786440 | tf_op jit(solution)/shard_map/ppermute | solution.py:377
  99.1 6.9 %collective-permute-start.13 = (bf16[2,64,512]{2,1,0:T(8,128)(2,1)S(1)}, bf16[2,64,512]{2,1,0:T(8,128)(2,1)S(1)}, u32[]{:S(2)}, u32[]{:S(2)}) collective-permute-start(bf16[2,64,512]{2,1,0:T(8,128)(2,1)S(1)} %get-tuple-element.47), channel_id=1, source_target_pairs={{0,8},{4,12},{8,0},{12,4},{16,24},{20,28},{24,16},{28,20},{1,9},{5... | collective-permute-start | bytes 393224 | tf_op jit(solution)/shard_map/ppermute | solution.py:377
  106.0 8.6 %collective-permute-start.14 = (bf16[1,64,512]{2,1,0:T(8,128)(2,1)S(1)}, bf16[1,64,512]{2,1,0:T(8,128)(2,1)S(1)}, u32[]{:S(2)}, u32[]{:S(2)}) collective-permute-start(bf16[1,64,512]{2,1,0:T(8,128)(2,1)S(1)} %get-tuple-element.52), channel_id=1, source_target_pairs={{0,16},{4,20},{8,24},{12,28},{16,0},{20,4},{24,8},{28,12},{1,17},{... | collective-permute-start | bytes 196616 | tf_op jit(solution)/shard_map/ppermute | solution.py:377

commit v2 on v1

--- a/solution.py
+++ b/solution.py
@@ -113,32 +113,49 @@
 
     join(kb, vb, xb, ke, ve, te, ko, vo, to, step == 0)
 
-    vt = {id(v): v[...].T for v in (va, vb, vc)}
-    gt = g_ref[...].T.astype(F32)
-    for base in range(0, rows, TILE):
+    lane = lane_of(TILE)
+    fold = lambda op, arrays: functools.reduce(
+        op, [x[:, i : i + LANES] for x in arrays for i in range(0, x.shape[1], LANES)]
+    )
+    def score(base, half):
         end = base + TILE
         spans = [(ka, va, xa, base, rows), (kb, vb, xb, 0, rows)]
         spans += [(kc, vc, xc, 0, base)] if base else []
         spans += [(kc, vc, xc, base, end)]
-        q = q_ref[base:end, :]
-        for half in range(2):
-            feats = slice(half * HEAD_DIM, (half + 1) * HEAD_DIM)
-            qx = wide(q * own_factor(half, SCALE), tag[base:end, :])
-            scores = [dot_t(wide(k[lo:hi, :], x[lo:hi, :]), qx) for k, v, x, lo, hi in spans]
-            scores[-1] = jnp.where(lower((TILE, TILE), False), scores[-1], MASKED_SCORE)
-            peak = functools.reduce(
-                jnp.maximum, [jnp.max(s, axis=0, keepdims=True) for s in scores]
-            )
-            total = jnp.zeros((1, TILE), F32)
-            acc = jnp.zeros((HEAD_DIM, TILE), F32)
-            for s, (k, v, x, lo, hi) in zip(scores, spans):
-                e = jnp.exp(s - peak)
-                total = total + jnp.sum(e, axis=0, keepdims=True)
-                acc = acc + dot(vt[id(v)][feats, lo:hi], e.astype(BF16))
-            acc = acc / total
-            o_ref[feats, base:end] = acc.astype(BF16)
-            delta = jnp.sum(acc * gt[feats, base:end], axis=0, keepdims=True)
-            first = TAG_LANES + 2 * PIECES * (2 * (step + first_pair) + half)
+        qx = wide(q_ref[base:end, :] * own_factor(half, SCALE), tag[base:end, :])
+        scores = [dot_t(qx, wide(k[lo:hi, :], x[lo:hi, :])) for k, v, x, lo, hi in spans]
+        scores[-1] = jnp.where(lower((TILE, TILE), True), scores[-1], MASKED_SCORE)
+        return scores, spans
+
+    turns = [(base, half) for base in range(0, rows, TILE) for half in range(2)]
+    ahead = score(*turns[0])
+    outs = []
+    for turn, (base, half) in enumerate(turns):
+        end = base + TILE
+        scores, spans = ahead
+        if turn + 1 < len(turns):
+            ahead = score(*turns[turn + 1])
+        mine = own(lane, half)
+        peak = jnp.max(fold(jnp.maximum, scores), axis=1, keepdims=True)
+        es = [jnp.exp(s - peak) for s in scores]
+        total = jnp.sum(fold(jnp.add, es), axis=1, keepdims=True)
+        acc = jnp.zeros((TILE, LANES), F32)
+        for e, (k, v, x, lo, hi) in zip(es, spans):
+            acc = acc + dot(e.astype(BF16), v[lo:hi, :])
+        acc = acc * (1.0 / total)
+        g = g_ref[base:end, :].astype(F32)
+        delta = jnp.sum(jnp.where(mine, acc * g, 0.0), axis=1, keepdims=True)
+        raw = raw if half else jnp.zeros((TILE, LANES), F32)
+        for i, column in enumerate((peak, total, delta)):
+            raw = jnp.where(lane == 3 * half + i, column, raw)
+        outs.append(acc)
+        if half == 0:
+            continue
+        o_ref[:, base:end] = jnp.where(own(lane, 0), outs[-2], outs[-1]).T.astype(BF16)
+        turned = raw.T
+        for side in range(2):
+            peak, total, delta = (turned[3 * side + i : 3 * side + i + 1, :] for i in range(3))
+            first = TAG_LANES + 2 * PIECES * (2 * (step + first_pair) + side)
             for i, part in enumerate(pieces(-(peak + jnp.log(total))) + pieces(-delta)):
                 rowed[pl.ds(first + i, 1), base:end] = part
 
@@ -167,16 +184,28 @@
         qx = wide(q * own_factor(half, SCALE), stats * for_score)
         gx = wide(g * own_factor(half), stats * for_grad)
         acc[...] = jnp.zeros_like(acc)
-        for k, v, x, near in ((ka, va, xa, 0), (kb, vb, xb, 1), (kc, vc, xc, 2)):
-            for lo in range(0, rows, TILE):
-                hi = lo + TILE
-                top = lo if near == 2 else 0
-                end = hi if near == 0 else rows
-                p = jnp.exp(dot_t(qx[top:end], wide(k[lo:hi, :], x[lo:hi, :])))
-                if near == 2:
-                    p = jnp.where(lower((end - top, TILE), True), p, 0.0)
-                dp = dot_t(gx[top:end], wide(v[lo:hi, :], x[lo:hi, :]))
-                acc[top:end, :] += dot((p * dp).astype(BF16), k[lo:hi, :])
+        turns = [
+            (k, v, x, near, lo)
+            for k, v, x, near in ((ka, va, xa, 0), (kb, vb, xb, 1), (kc, vc, xc, 2))
+            for lo in range(0, rows, TILE)
+        ]
+
+        def products(k, v, x, near, lo):
+            hi = lo + TILE
+            top = lo if near == 2 else 0
+            end = hi if near == 0 else rows
+            s = dot_t(qx[top:end], wide(k[lo:hi, :], x[lo:hi, :]))
+            return s, dot_t(gx[top:end], wide(v[lo:hi, :], x[lo:hi, :])), top, end
+
+        ahead = products(*turns[0])
+        for turn, (k, v, x, near, lo) in enumerate(turns):
+            s, dp, top, end = ahead
+            if turn + 1 < len(turns):
+                ahead = products(*turns[turn + 1])
+            p = jnp.exp(s)
+            if near == 2:
+                p = jnp.where(lower((end - top, TILE), True), p, 0.0)
+            acc[top:end, :] += dot((p * dp).astype(BF16), k[lo : lo + TILE, :])
         if half == 0:
             first[...] = acc[...]
         else:
@@ -200,22 +229,33 @@
         dk[...] = jnp.zeros_like(dk)
         dv[...] = jnp.zeros_like(dv)
         for_score, for_grad = extra_factors(2 * (step + first_pair) + half)
-        for q_ref, g_ref, s_ref, near in ((qc, gc, sc, 2), (qd, gd, sd, 1), (qe, ge, se, 0)):
-            for lo in range(0, rows, TILE):
-                hi = lo + TILE
-                top = lo if near == 0 else 0
-                end = hi if near == 2 else rows
-                q, g, stats = q_ref[lo:hi, :], g_ref[lo:hi, :], s_ref[lo:hi, :]
-                qx = wide(q * own_factor(half, SCALE), stats * for_score)
-                gx = wide(g * own_factor(half), stats * for_grad)
-                p = jnp.exp(dot_t(kx[top:end], qx))
-                if near == 2:
-                    row = lax.broadcasted_iota(jnp.int32, p.shape, 0)
-                    col = lax.broadcasted_iota(jnp.int32, p.shape, 1) + lo
-                    p = jnp.where(row <= col, p, 0.0)
-                dp = dot_t(vx[top:end], gx)
-                dv[top:end, :] += dot(p.astype(BF16), g)
-                dk[top:end, :] += dot((p * dp).astype(BF16), q)
+        turns = [
+            (q_ref, g_ref, s_ref, near, lo)
+            for q_ref, g_ref, s_ref, near in ((qc, gc, sc, 2), (qd, gd, sd, 1), (qe, ge, se, 0))
+            for lo in range(0, rows, TILE)
+        ]
+
+        def products(q_ref, g_ref, s_ref, near, lo):
+            hi = lo + TILE
+            top = lo if near == 0 else 0
+            end = hi if near == 2 else rows
+            q, g, stats = q_ref[lo:hi, :], g_ref[lo:hi, :], s_ref[lo:hi, :]
+            qx = wide(q * own_factor(half, SCALE), stats * for_score)
+            gx = wide(g * own_factor(half), stats * for_grad)
+            return dot_t(kx[top:end], qx), dot_t(vx[top:end], gx), q, g, top, end
+
+        ahead = products(*turns[0])
+        for turn, (q_ref, g_ref, s_ref, near, lo) in enumerate(turns):
+            s, dp, q, g, top, end = ahead
+            if turn + 1 < len(turns):
+                ahead = products(*turns[turn + 1])
+            p = jnp.exp(s)
+            if near == 2:
+                row = lax.broadcasted_iota(jnp.int32, p.shape, 0)
+                col = lax.broadcasted_iota(jnp.int32, p.shape, 1) + lo
+                p = jnp.where(row <= col, p, 0.0)
+            dv[top:end, :] += dot(p.astype(BF16), g)
+            dk[top:end, :] += dot((p * dp).astype(BF16), q)
     second = own(lane_of(rows), 1)
     dk_ref[...] = (jnp.where(second, dks[1][...], dks[0][...]) * SCALE).astype(BF16)
     dv_ref[...] = jnp.where(second, dvs[1][...], dvs[0][...]).astype(BF16)
@@ -439,9 +479,10 @@
     mine, far, paired, passed = [], [], [], []
     for i in range(chunks):
         cut = slice(i * size, (i + 1) * size)
+        tagged = after(tag_rows, *mine)
         mine.append(
             jnp.concatenate(
-                [jnp.concatenate([key_rows[:, cut], value_rows[:, cut]], axis=1), tag_rows], axis=0
+                [jnp.concatenate([key_rows[:, cut], value_rows[:, cut]], axis=1), tagged], axis=0
             )
         )
         far.append(shift(mine[i], 2))

time: 116 us -> 113 us (0.974)
  Pallas kernels: 59.9 us -> 55.8 us
  waiting for transfers between devices: 14.7 us -> 16.4 us
    pallas_call x7, Pallas kernels: 49.2 us -> 45.1 us  [call(): pl.pallas_call(functools.partial(kernel, self.first), grid=(self.count,),...]
    ppermute x4, waiting for transfers between devices: 5.25 us -> 6.45 us  [within_pair(): lax.ppermute(x, 'ctx', [(i, i + 1) if to_odd else (i + 1, i) for i in ran...]
  transfers between devices with their start and end apart: 15 -> 15, of which waited for: 6 -> 6; matrix products, arithmetic and copies ran while one was open for 2% -> 2% of each run, Pallas kernels for 42% -> 40%
where the time goes in v2:
time: 113 us; the launch traced here: 112 us
  Pallas kernels  55.8 us (49%)
  starting transfers between devices  32.7 us (29%)
  waiting for transfers between devices  16.4 us (15%)
  other arithmetic  3.31 us (3%)
  local copies, waits for them, and re-layouts  3.18 us (3%)
    pallas_call x7, Pallas kernels, call(): pl.pallas_call(functools.partial(kernel, self.first), grid=(self.count,),...  45.1 us
    ppermute x5, starting transfers between devices, shift(): return lax.ppermute(x, 'ctx', pairs)  13.7 us
    ppermute x4, starting transfers between devices, within_pair(): lax.ppermute(x, 'ctx', [(i, i + 1) if to_odd else (i + 1, i) for i in ran...  13 us
    ppermute x5, waiting for transfers between devices, shift(): return lax.ppermute(x, 'ctx', pairs)  7.09 us
    ppermute x4, waiting for transfers between devices, within_pair(): lax.ppermute(x, 'ctx', [(i, i + 1) if to_odd else (i + 1, i) for i in ran...  6.45 us
    ppermute x6, starting transfers between devices, swap(): lax.ppermute(x, axis, [(i, i ^ bit) for i in range(lax.axis_size(axis))])  5.93 us
    pallas_call x2, Pallas kernels, weight_term(): pl.pallas_call(weight_kernel, grid_spec=pltpu.PrefetchScalarGridSpec(num_...  5.8 us
    ppermute x6, waiting for transfers between devices, swap(): lax.ppermute(x, axis, [(i, i ^ bit) for i in range(lax.axis_size(axis))])  2.91 us
  transfers between devices with their start and end apart: 15, of which 6 were waited for; matrix products, arithmetic and copies ran while one was open for 2% of the time, Pallas kernels for 40%

profile of v2, /device:TPU:0, one launch (start us, length us, event | category | flops | bytes accessed | tf_op | source)
XLA Modules:
  0.0 112.4 jit_solution(10266972825993164143)
XLA Ops:
  0.6 0.7 add_convert_fusion
  1.3 0.0 copy-start.5
  1.3 1.4 %fusion = (bf16[512,256]{1,0:T(8,128)(2,1)S(1)}, bf16[512,256]{1,0:T(8,128)(2,1)S(1)}, bf16[512,256]{1,0:T(8,128)(2,1)S(1)}, bf16[512,256]{1,0:T(8,128)(2,1)S(1)}) fusion(bf16[512,512]{1,0:T(8,128)(2,1)} %bitcast.28, bf16[512,512]{1,0:T(8,128)(2,1)} %bitcast.29), kind=kLoop, calls=%fused_computation.7 | loop fusion | bytes 2097152 | tf_op jit(solution)/shard_map/slice | solution.py:485
  2.7 0.0 copy-start.1
  2.8 5.1 %collective-permute-start.1 = (bf16[528,512]{1,0:T(8,128)(2,1)S(1)}, bf16[528,512]{1,0:T(8,128)(2,1)S(1)}, u32[]{:S(2)}, u32[]{:S(2)}) collective-permute-start(bf16[528,512]{1,0:T(8,128)(2,1)S(1)} %pad_maximum_fusion.kc.vc.tc.k_ref.v_ref.t_ref), channel_id=1, source_target_pairs={{0,8},{4,12},{8,16},{12,20},{16,24},{20,28},{1,9},{5,13},{9,17},{1... | collective-permute-start | bytes 1622024 | tf_op jit(solution)/shard_map/ppermute | solution.py:25
  8.0 0.0 copy-done.5
  8.0 0.0 copy-done.1
  8.0 0.0 copy-start.6
  8.0 1.0 copy-done.6
  9.0 1.8 %queries_to_send.1.q_ref.g_ref.qc.gc = bf16[512,1024]{1,0:T(8,128)(2,1)S(1)} custom-call(bf16[512,512]{1,0:T(8,128)(2,1)S(1)} %bitcast.22, bf16[512,2048]{1,0:T(8,128)(2,1)S(1)} %bitcast.21, bf16[512,2048]{1,0:T(8,128)(2,1)S(1)} %copy-done.5), custom_call_target="tpu_custom_call" | custom-call | bytes 17500000 | tf_op jit(solution)/shard_map/queries_to_send/pallas_call | solution.py:337
  10.8 0.0 copy-start
  10.8 1.3 %collective-permute-start = (bf16[512,1024]{1,0:T(8,128)(2,1)S(1)}, bf16[512,1024]{1,0:T(8,128)(2,1)}, u32[]{:S(2)}, u32[]{:S(2)}) collective-permute-start(bf16[512,1024]{1,0:T(8,128)(2,1)S(1)} %queries_to_send.1.q_ref.g_ref.qc.gc), channel_id=1, source_target_pairs={{8,0},{12,4},{16,8},{20,12},{24,16},{28,20},{9,1},{13,5},{17,9},{2... | collective-permute-start | bytes 3145736 | tf_op jit(solution)/shard_map/ppermute | solution.py:25
  12.1 4.6 %collective-permute-start.4 = (bf16[528,512]{1,0:T(8,128)(2,1)S(1)}, bf16[528,512]{1,0:T(8,128)(2,1)S(1)}, u32[]{:S(2)}, u32[]{:S(2)}) collective-permute-start(bf16[528,512]{1,0:T(8,128)(2,1)S(1)} %pad_maximum_fusion.1.kc.vc.tc.k_ref.v_ref.t_ref), channel_id=1, source_target_pairs={{0,8},{4,12},{8,16},{12,20},{16,24},{20,28},{1,9},{5,13},{9,17},{1... | collective-permute-start | bytes 1622024 | tf_op jit(solution)/shard_map/ppermute | solution.py:25
  16.7 4.3 %collective-permute-start.2 = (bf16[528,512]{1,0:T(8,128)(2,1)S(1)}, bf16[528,512]{1,0:T(8,128)(2,1)}, u32[]{:S(2)}, u32[]{:S(2)}) collective-permute-start(bf16[528,512]{1,0:T(8,128)(2,1)S(1)} %pad_maximum_fusion.kc.vc.tc.k_ref.v_ref.t_ref), channel_id=1, source_target_pairs={{0,4},{8,12},{16,20},{24,28},{1,5},{9,13},{17,21},{25,29},{2,6},{1... | collective-permute-start | bytes 1622024 | tf_op jit(solution)/shard_map/ppermute | solution.py:422
  21.0 0.0 collective-permute-done.1.ka.va.ta
  21.0 1.3 %collective-permute-start.3 = (bf16[528,512]{1,0:T(8,128)(2,1)S(1)}, bf16[528,512]{1,0:T(8,128)(2,1)}, u32[]{:S(2)}, u32[]{:S(2)}) collective-permute-start(bf16[528,512]{1,0:T(8,128)(2,1)S(1)} %collective-permute-done.1.ka.va.ta), channel_id=1, source_target_pairs={{4,0},{12,8},{20,16},{28,24},{5,1},{13,9},{21,17},{29,25},{6,2},{1... | collective-permute-start | bytes 1622024 | tf_op jit(solution)/shard_map/ppermute | solution.py:422
  22.3 6.2 %collective-permute-start.5 = (bf16[528,512]{1,0:T(8,128)(2,1)S(1)}, bf16[528,512]{1,0:T(8,128)(2,1)}, u32[]{:S(2)}, u32[]{:S(2)}) collective-permute-start(bf16[528,512]{1,0:T(8,128)(2,1)S(1)} %pad_maximum_fusion.1.kc.vc.tc.k_ref.v_ref.t_ref), channel_id=1, source_target_pairs={{0,4},{8,12},{16,20},{24,28},{1,5},{9,13},{17,21},{25,29},{2,6},{1... | collective-permute-start | bytes 1622024 | tf_op jit(solution)/shard_map/ppermute | solution.py:422
  28.5 2.5 %collective-permute-done.4.ka.va.ta = bf16[528,512]{1,0:T(8,128)(2,1)S(1)} collective-permute-done((bf16[528,512]{1,0:T(8,128)(2,1)S(1)}, bf16[528,512]{1,0:T(8,128)(2,1)S(1)}, u32[]{:S(2)}, u32[]{:S(2)}) %collective-permute-start.4) | collective-permute-done | bytes 540704 | tf_op jit(solution)/shard_map/ppermute | solution.py:25
  31.0 1.3 %collective-permute-start.6 = (bf16[528,512]{1,0:T(8,128)(2,1)S(1)}, bf16[528,512]{1,0:T(8,128)(2,1)}, u32[]{:S(2)}, u32[]{:S(2)}) collective-permute-start(bf16[528,512]{1,0:T(8,128)(2,1)S(1)} %collective-permute-done.4.ka.va.ta), channel_id=1, source_target_pairs={{4,0},{12,8},{20,16},{28,24},{5,1},{13,9},{21,17},{29,25},{6,2},{1... | collective-permute-start | bytes 1622024 | tf_op jit(solution)/shard_map/ppermute | solution.py:422
  32.3 0.1 add_add_fusion.1.sel_ref
  32.4 0.5 collective-permute-done.2.ke.ve.te
  32.8 4.3 %collective-permute-done.3.ko.vo.to = bf16[528,512]{1,0:T(8,128)(2,1)} collective-permute-done((bf16[528,512]{1,0:T(8,128)(2,1)S(1)}, bf16[528,512]{1,0:T(8,128)(2,1)}, u32[]{:S(2)}, u32[]{:S(2)}) %collective-permute-start.3) | collective-permute-done | bytes 540704 | tf_op jit(solution)/shard_map/ppermute | solution.py:422
  37.1 6.2 %forward_kernel.2 = (bf16[256,512]{1,0:T(8,128)(2,1)S(1)}, bf16[512,128]{1,0:T(8,128)(2,1)S(1)}) custom-call(bf16[512,1024]{1,0:T(8,128)(2,1)S(1)} %queries_to_send.1.q_ref.g_ref.qc.gc, bf16[512,1024]{1,0:T(8,128)(2,1)S(1)} %queries_to_send.1.q_ref.g_ref.qc.gc, bf16[528,512]{1,0:T(8,128)(2,1)S(1)} %pad_maximum_fusion.kc.vc.tc.k_ref.v_ref.t_ref, ...), custom_call_target="tpu_custom_call" | custom-call | bytes 24500000 | tf_op jit(solution)/shard_map/forward_kernel/pallas_call | solution.py:287
  43.3 0.0 copy-start.3
  43.3 0.0 collective-permute-done.qe.ge
  43.4 2.4 %broadcast_select_fusion = bf16[512,1024]{1,0:T(8,128)(2,1)} fusion(bf16[512,1024]{1,0:T(8,128)(2,1)S(1)} %queries_to_send.1.q_ref.g_ref.qc.gc, bf16[512,1024]{1,0:T(8,128)(2,1)} %collective-permute-done.qe.ge, pred[]{:T(512)S(6)} %eq.9), kind=kLoop, calls=%fused_computation | loop fusion | flops 524288 | bytes 3145729 | tf_op jit(solution)/shard_map/jit(_where)/select_n | solution.py:504
  45.7 0.0 copy-done.3
  45.8 0.0 collective-permute-done.5.ke.ve.te
  45.8 1.7 %collective-permute-done.6.ko.vo.to = bf16[528,512]{1,0:T(8,128)(2,1)} collective-permute-done((bf16[528,512]{1,0:T(8,128)(2,1)S(1)}, bf16[528,512]{1,0:T(8,128)(2,1)}, u32[]{:S(2)}, u32[]{:S(2)}) %collective-permute-start.6) | collective-permute-done | bytes 540704 | tf_op jit(solution)/shard_map/ppermute | solution.py:422
  47.4 6.2 %forward_kernel.3 = (bf16[256,512]{1,0:T(8,128)(2,1)S(1)}, bf16[512,128]{1,0:T(8,128)(2,1)S(1)}) custom-call(bf16[512,1024]{1,0:T(8,128)(2,1)S(1)} %queries_to_send.1.q_ref.g_ref.qc.gc, bf16[512,1024]{1,0:T(8,128)(2,1)S(1)} %queries_to_send.1.q_ref.g_ref.qc.gc, bf16[528,512]{1,0:T(8,128)(2,1)S(1)} %pad_maximum_fusion.1.kc.vc.tc.k_ref.v_ref.t_ref, ...), custom_call_target="tpu_custom_call" | custom-call | bytes 24500000 | tf_op jit(solution)/shard_map/forward_kernel/pallas_call | solution.py:287
  53.6 0.0 copy-start.4
  53.7 0.7 copy-done.4
  54.4 0.0 copy-start.2
  54.4 3.5 %weight_term.2 = bf16[2,512,512]{2,1,0:T(8,128)(2,1)} custom-call(s32[3]{0:T(128)S(1)} %add_add_fusion.1.sel_ref, bf16[256,512]{1,0:T(8,128)(2,1)} %copy-done.3, bf16[256,512]{1,0:T(8,128)(2,1)} %copy-done.4, bf16[512,2048]{1,0:T(8,128)(2,1)} %bitcast.18), custom_call_target="tpu_custom_call" | custom-call | bytes 10500000 | tf_op jit(solution)/shard_map/weight_term/pallas_call | solution.py:367
  57.8 0.0 collective-permute-start.7
  57.8 0.0 collective-permute-start.12
  57.8 0.1 add_add_fusion
  57.9 2.9 %collective-permute-done.7.refs_3_.got_ref = bf16[2,512,512]{2,1,0:T(8,128)(2,1)} collective-permute-done((bf16[2,512,512]{2,1,0:T(8,128)(2,1)}, bf16[2,512,512]{2,1,0:T(8,128)(2,1)}, u32[]{:S(2)}, u32[]{:S(2)}) %collective-permute-start.7) | collective-permute-done | bytes 1048608 | tf_op jit(solution)/shard_map/ppermute | solution.py:417
  60.8 2.3 %weight_term.3 = bf16[1,512,512]{2,1,0:T(8,128)(2,1)S(1)} custom-call(s32[3]{0:T(128)S(1)} %get-tuple-element.67.sel_ref, bf16[256,512]{1,0:T(8,128)(2,1)} %copy-done.3, bf16[256,512]{1,0:T(8,128)(2,1)} %copy-done.4, bf16[512,2048]{1,0:T(8,128)(2,1)} %bitcast.19, bf16[2,512,512]{2,1,0:T(8,128)(2,1)} %collective-permute-done.7.refs_3_.got_ref), custom_call_target="tpu_custom_call" | custom-call | bytes 10500000 | tf_op jit(solution)/shard_map/weight_term/pallas_call | solution.py:367
  63.2 1.6 %collective-permute-start.8 = (bf16[1,512,512]{2,1,0:T(8,128)(2,1)S(1)}, bf16[1,512,512]{2,1,0:T(8,128)(2,1)S(1)}, u32[]{:S(2)}, u32[]{:S(2)}) collective-permute-start(bf16[1,512,512]{2,1,0:T(8,128)(2,1)S(1)} %weight_term.3), channel_id=1, source_target_pairs={{0,2},{1,3},{2,0},{3,1},{4,6},{5,7},{6,4},{7,5},{8,10},{9,11},{10,... | collective-permute-start | bytes 1572872 | tf_op jit(solution)/shard_map/ppermute | solution.py:417
  64.7 1.3 %collective-permute-start.10 = (bf16[512,128]{1,0:T(8,128)(2,1)S(1)}, bf16[512,128]{1,0:T(8,128)(2,1)S(1)}, u32[]{:S(2)}, u32[]{:S(2)}) collective-permute-start(bf16[512,128]{1,0:T(8,128)(2,1)S(1)} %get-tuple-element.55.st_ref.sc), channel_id=1, source_target_pairs={{8,0},{12,4},{16,8},{20,12},{24,16},{28,20},{9,1},{13,5},{17,9},{2... | collective-permute-start | bytes 393224 | tf_op jit(solution)/shard_map/ppermute | solution.py:25
  66.0 1.5 %collective-permute-start.9 = (bf16[512,128]{1,0:T(8,128)(2,1)S(1)}, bf16[512,128]{1,0:T(8,128)(2,1)S(1)}, u32[]{:S(2)}, u32[]{:S(2)}) collective-permute-start(bf16[512,128]{1,0:T(8,128)(2,1)S(1)} %get-tuple-element.55.st_ref.sc), channel_id=1, source_target_pairs={{4,0},{8,4},{12,8},{16,12},{20,16},{24,20},{28,24},{5,1},{9,5},{13... | collective-permute-start | bytes 393224 | tf_op jit(solution)/shard_map/ppermute | solution.py:25
  67.5 7.2 %query_kernel.2.rest_0_ = bf16[512,512]{1,0:T(8,128)(2,1)} custom-call(bf16[512,1024]{1,0:T(8,128)(2,1)S(1)} %queries_to_send.1.q_ref.g_ref.qc.gc, bf16[512,1024]{1,0:T(8,128)(2,1)S(1)} %queries_to_send.1.q_ref.g_ref.qc.gc, bf16[512,128]{1,0:T(8,128)(2,1)S(1)} %get-tuple-element.55.st_ref.sc, ...), custom_call_target="tpu_custom_call" | custom-call | bytes 24500000 | tf_op jit(solution)/shard_map/query_kernel/pallas_call | solution.py:287
  74.7 0.0 copy-done
  74.7 0.0 copy-done.2
  74.7 7.2 %query_kernel.3 = bf16[512,512]{1,0:T(8,128)(2,1)} custom-call(bf16[512,1024]{1,0:T(8,128)(2,1)S(1)} %queries_to_send.1.q_ref.g_ref.qc.gc, bf16[512,1024]{1,0:T(8,128)(2,1)S(1)} %queries_to_send.1.q_ref.g_ref.qc.gc, bf16[512,128]{1,0:T(8,128)(2,1)S(1)} %get-tuple-element.55.st_ref.sc, ...), custom_call_target="tpu_custom_call", output_to_operand_aliasing={{}: (15, {})} | custom-call | bytes 24500000 | tf_op jit(solution)/shard_map/query_kernel/pallas_call | solution.py:287
  81.8 0.0 collective-permute-done.10.se
  81.8 4.6 %collective-permute-done.9.sd = bf16[512,128]{1,0:T(8,128)(2,1)S(1)} collective-permute-done((bf16[512,128]{1,0:T(8,128)(2,1)S(1)}, bf16[512,128]{1,0:T(8,128)(2,1)S(1)}, u32[]{:S(2)}, u32[]{:S(2)}) %collective-permute-start.9) | collective-permute-done | bytes 131104 | tf_op jit(solution)/shard_map/ppermute | solution.py:25
  86.4 0.0 collective-permute-done.8.moved_ref
  86.4 2.4 %keep_term.1 = (bf16[4,64,512]{2,1,0:T(8,128)(2,1)S(1)}, f32[4,64,512]{2,1,0:T(8,128)S(1)}) custom-call(s32[3]{0:T(128)S(1)} %get-tuple-element.66.sel_ref, bf16[256,512]{1,0:T(8,128)(2,1)} %copy-done.3, bf16[256,512]{1,0:T(8,128)(2,1)} %copy-done.4, bf16[512,2048]{1,0:T(8,128)(2,1)} %bitcast.20, ...), custom_call_target="tpu_custom_call" | custom-call | bytes 10500000 | tf_op jit(solution)/shard_map/keep_term/pallas_call | solution.py:400
  88.8 0.0 copy-done.7
  88.8 0.0 copy-done.8
  88.8 0.1 collective-permute-start.11
  88.9 0.0 collective-permute-done.12.qd.gd
  88.9 8.3 %key_kernel.3 = (bf16[512,512]{1,0:T(8,128)(2,1)}, bf16[512,512]{1,0:T(8,128)(2,1)}) custom-call(bf16[528,512]{1,0:T(8,128)(2,1)S(1)} %pad_maximum_fusion.kc.vc.tc.k_ref.v_ref.t_ref, bf16[528,512]{1,0:T(8,128)(2,1)S(1)} %pad_maximum_fusion.kc.vc.tc.k_ref.v_ref.t_ref, bf16[528,512]{1,0:T(8,128)(2,1)S(1)} %pad_maximum_fusion.kc.vc.tc.k_ref.v_ref.t_ref, ...), custom_call_target="tpu_custom_call" | custom-call | bytes 29400000 | tf_op jit(solution)/shard_map/key_kernel/pallas_call | solution.py:287
  97.2 0.0 collective-permute-done.11.got_ref
  97.2 0.1 stage.2
  97.3 1.6 %collective-permute-start.13 = (bf16[2,64,512]{2,1,0:T(8,128)(2,1)S(1)}, bf16[2,64,512]{2,1,0:T(8,128)(2,1)S(1)}, u32[]{:S(2)}, u32[]{:S(2)}) collective-permute-start(bf16[2,64,512]{2,1,0:T(8,128)(2,1)S(1)} %get-tuple-element.49), channel_id=1, source_target_pairs={{0,8},{4,12},{8,0},{12,4},{16,24},{20,28},{24,16},{28,20},{1,9},{5... | collective-permute-start | bytes 393224 | tf_op jit(solution)/shard_map/ppermute | solution.py:417
  98.9 5.0 %key_kernel.4 = (bf16[512,512]{1,0:T(8,128)(2,1)}, bf16[512,512]{1,0:T(8,128)(2,1)}) custom-call(bf16[528,512]{1,0:T(8,128)(2,1)S(1)} %pad_maximum_fusion.1.kc.vc.tc.k_ref.v_ref.t_ref, bf16[528,512]{1,0:T(8,128)(2,1)S(1)} %pad_maximum_fusion.1.kc.vc.tc.k_ref.v_ref.t_ref, ...), custom_call_target="tpu_custom_call", output_to_operand_aliasing={{0}: (12, {}), {1}: (13, {})} | custom-call | bytes 14700000 | tf_op jit(solution)/shard_map/key_kernel/pallas_call | solution.py:287
  103.9 0.0 collective-permute-done.13.got_ref
  104.0 2.7 %collective-permute-start.14 = (bf16[1,64,512]{2,1,0:T(8,128)(2,1)S(1)}, bf16[1,64,512]{2,1,0:T(8,128)(2,1)S(1)}, u32[]{:S(2)}, u32[]{:S(2)}) collective-permute-start(bf16[1,64,512]{2,1,0:T(8,128)(2,1)S(1)} %get-tuple-element.54), channel_id=1, source_target_pairs={{0,16},{4,20},{8,24},{12,28},{16,0},{20,4},{24,8},{28,12},{1,17},{... | collective-permute-start | bytes 196616 | tf_op jit(solution)/shard_map/ppermute | solution.py:417
  106.7 5.0 %key_kernel.5 = (bf16[512,512]{1,0:T(8,128)(2,1)}, bf16[512,512]{1,0:T(8,128)(2,1)}) custom-call(bf16[528,512]{1,0:T(8,128)(2,1)S(1)} %pad_maximum_fusion.1.kc.vc.tc.k_ref.v_ref.t_ref, bf16[528,512]{1,0:T(8,128)(2,1)S(1)} %pad_maximum_fusion.1.kc.vc.tc.k_ref.v_ref.t_ref, ...), custom_call_target="tpu_custom_call", output_to_operand_aliasing={{0}: (12, {}), {1}: (13, {})} | custom-call | bytes 14700000 | tf_op jit(solution)/shard_map/key_kernel/pallas_call | solution.py:287
  111.7 0.0 collective-permute-done.14
  111.7 0.7 last_sum.1
  (6 shorter events, 0.1 us)
Async XLA Ops:
  1.3 6.6 %copy-start.5 = (bf16[512,2048]{1,0:T(8,128)(2,1)S(1)}, bf16[512,2048]{1,0:T(8,128)(2,1)}, u32[]{:S(2)}) copy-start(bf16[512,2048]{1,0:T(8,128)(2,1)} %w_ref.1) | copy-start | bytes 6291460
  2.7 5.2 %copy-start.1 = (bf16[1,512,2048]{2,1,0:T(8,128)(2,1)S(1)}, bf16[1,512,2048]{2,1,0:T(8,128)(2,1)}, u32[]{:S(2)}) copy-start(bf16[1,512,2048]{2,1,0:T(8,128)(2,1)} %param.10) | copy-start | bytes 6291460
  2.8 18.2 %collective-permute-start.1 = (bf16[528,512]{1,0:T(8,128)(2,1)S(1)}, bf16[528,512]{1,0:T(8,128)(2,1)S(1)}, u32[]{:S(2)}, u32[]{:S(2)}) collective-permute-start(bf16[528,512]{1,0:T(8,128)(2,1)S(1)} %pad_maximum_fusion.kc.vc.tc.k_ref.v_ref.t_ref), channel_id=1, source_target_pairs={{0,8},{4,12},{8,16},{12,20},{16,24},{20,28},{1,9},{5,13},{9,17},{1... | collective-permute-start | bytes 1622024 | tf_op jit(solution)/shard_map/ppermute | solution.py:25
  8.0 1.0 copy-start.6
  10.8 63.9 %copy-start = (bf16[512,1024]{1,0:T(8,128)(2,1)}, bf16[512,1024]{1,0:T(8,128)(2,1)S(1)}, u32[]{:S(2)}) copy-start(bf16[512,1024]{1,0:T(8,128)(2,1)S(1)} %queries_to_send.1.q_ref.g_ref.qc.gc) | copy-start | bytes 3145732
  10.8 32.5 %collective-permute-start = (bf16[512,1024]{1,0:T(8,128)(2,1)S(1)}, bf16[512,1024]{1,0:T(8,128)(2,1)}, u32[]{:S(2)}, u32[]{:S(2)}) collective-permute-start(bf16[512,1024]{1,0:T(8,128)(2,1)S(1)} %queries_to_send.1.q_ref.g_ref.qc.gc), channel_id=1, source_target_pairs={{8,0},{12,4},{16,8},{20,12},{24,16},{28,20},{9,1},{13,5},{17,9},{2... | collective-permute-start | bytes 3145736 | tf_op jit(solution)/shard_map/ppermute | solution.py:25
  12.1 18.9 %collective-permute-start.4 = (bf16[528,512]{1,0:T(8,128)(2,1)S(1)}, bf16[528,512]{1,0:T(8,128)(2,1)S(1)}, u32[]{:S(2)}, u32[]{:S(2)}) collective-permute-start(bf16[528,512]{1,0:T(8,128)(2,1)S(1)} %pad_maximum_fusion.1.kc.vc.tc.k_ref.v_ref.t_ref), channel_id=1, source_target_pairs={{0,8},{4,12},{8,16},{12,20},{16,24},{20,28},{1,9},{5,13},{9,17},{1... | collective-permute-start | bytes 1622024 | tf_op jit(solution)/shard_map/ppermute | solution.py:25
  16.7 16.1 %collective-permute-start.2 = (bf16[528,512]{1,0:T(8,128)(2,1)S(1)}, bf16[528,512]{1,0:T(8,128)(2,1)}, u32[]{:S(2)}, u32[]{:S(2)}) collective-permute-start(bf16[528,512]{1,0:T(8,128)(2,1)S(1)} %pad_maximum_fusion.kc.vc.tc.k_ref.v_ref.t_ref), channel_id=1, source_target_pairs={{0,4},{8,12},{16,20},{24,28},{1,5},{9,13},{17,21},{25,29},{2,6},{1... | collective-permute-start | bytes 1622024 | tf_op jit(solution)/shard_map/ppermute | solution.py:422
  21.0 16.2 %collective-permute-start.3 = (bf16[528,512]{1,0:T(8,128)(2,1)S(1)}, bf16[528,512]{1,0:T(8,128)(2,1)}, u32[]{:S(2)}, u32[]{:S(2)}) collective-permute-start(bf16[528,512]{1,0:T(8,128)(2,1)S(1)} %collective-permute-done.1.ka.va.ta), channel_id=1, source_target_pairs={{4,0},{12,8},{20,16},{28,24},{5,1},{13,9},{21,17},{29,25},{6,2},{1... | collective-permute-start | bytes 1622024 | tf_op jit(solution)/shard_map/ppermute | solution.py:422
  22.3 23.5 %collective-permute-start.5 = (bf16[528,512]{1,0:T(8,128)(2,1)S(1)}, bf16[528,512]{1,0:T(8,128)(2,1)}, u32[]{:S(2)}, u32[]{:S(2)}) collective-permute-start(bf16[528,512]{1,0:T(8,128)(2,1)S(1)} %pad_maximum_fusion.1.kc.vc.tc.k_ref.v_ref.t_ref), channel_id=1, source_target_pairs={{0,4},{8,12},{16,20},{24,28},{1,5},{9,13},{17,21},{25,29},{2,6},{1... | collective-permute-start | bytes 1622024 | tf_op jit(solution)/shard_map/ppermute | solution.py:422
  31.0 16.5 %collective-permute-start.6 = (bf16[528,512]{1,0:T(8,128)(2,1)S(1)}, bf16[528,512]{1,0:T(8,128)(2,1)}, u32[]{:S(2)}, u32[]{:S(2)}) collective-permute-start(bf16[528,512]{1,0:T(8,128)(2,1)S(1)} %collective-permute-done.4.ka.va.ta), channel_id=1, source_target_pairs={{4,0},{12,8},{20,16},{28,24},{5,1},{13,9},{21,17},{29,25},{6,2},{1... | collective-permute-start | bytes 1622024 | tf_op jit(solution)/shard_map/ppermute | solution.py:422
  43.3 2.4 %copy-start.3 = (bf16[256,512]{1,0:T(8,128)(2,1)}, bf16[256,512]{1,0:T(8,128)(2,1)S(1)}, u32[]{:S(2)}) copy-start(bf16[256,512]{1,0:T(8,128)(2,1)S(1)} %get-tuple-element.35.refs_0_.o0_ref) | copy-start | bytes 786436
  53.6 0.7 copy-start.4
  54.4 20.3 %copy-start.2 = (bf16[512,128]{1,0:T(8,128)(2,1)}, bf16[512,128]{1,0:T(8,128)(2,1)S(1)}, u32[]{:S(2)}) copy-start(bf16[512,128]{1,0:T(8,128)(2,1)S(1)} %get-tuple-element.55.st_ref.sc) | copy-start | bytes 393220
  57.8 3.0 %collective-permute-start.7 = (bf16[2,512,512]{2,1,0:T(8,128)(2,1)}, bf16[2,512,512]{2,1,0:T(8,128)(2,1)}, u32[]{:S(2)}, u32[]{:S(2)}) collective-permute-start(bf16[2,512,512]{2,1,0:T(8,128)(2,1)} %weight_term.2), channel_id=1, source_target_pairs={{0,1},{1,0},{2,3},{3,2},{4,5},{5,4},{6,7},{7,6},{8,9},{9,8},{10,11... | collective-permute-start | bytes 3145736 | tf_op jit(solution)/shard_map/ppermute | solution.py:417
  57.8 31.1 %collective-permute-start.12 = (bf16[512,1024]{1,0:T(8,128)(2,1)}, bf16[512,1024]{1,0:T(8,128)(2,1)}, u32[]{:S(2)}, u32[]{:S(2)}) collective-permute-start(bf16[512,1024]{1,0:T(8,128)(2,1)} %broadcast_select_fusion), channel_id=1, source_target_pairs={{0,4},{4,0},{8,12},{12,8},{16,20},{20,16},{24,28},{28,24},{1,5},{5... | collective-permute-start | bytes 3145736 | tf_op jit(solution)/shard_map/ppermute | solution.py:417
  63.2 23.2 %collective-permute-start.8 = (bf16[1,512,512]{2,1,0:T(8,128)(2,1)S(1)}, bf16[1,512,512]{2,1,0:T(8,128)(2,1)S(1)}, u32[]{:S(2)}, u32[]{:S(2)}) collective-permute-start(bf16[1,512,512]{2,1,0:T(8,128)(2,1)S(1)} %weight_term.3), channel_id=1, source_target_pairs={{0,2},{1,3},{2,0},{3,1},{4,6},{5,7},{6,4},{7,5},{8,10},{9,11},{10,... | collective-permute-start | bytes 1572872 | tf_op jit(solution)/shard_map/ppermute | solution.py:417
  64.7 17.1 %collective-permute-start.10 = (bf16[512,128]{1,0:T(8,128)(2,1)S(1)}, bf16[512,128]{1,0:T(8,128)(2,1)S(1)}, u32[]{:S(2)}, u32[]{:S(2)}) collective-permute-start(bf16[512,128]{1,0:T(8,128)(2,1)S(1)} %get-tuple-element.55.st_ref.sc), channel_id=1, source_target_pairs={{8,0},{12,4},{16,8},{20,12},{24,16},{28,20},{9,1},{13,5},{17,9},{2... | collective-permute-start | bytes 393224 | tf_op jit(solution)/shard_map/ppermute | solution.py:25
  66.0 20.4 %collective-permute-start.9 = (bf16[512,128]{1,0:T(8,128)(2,1)S(1)}, bf16[512,128]{1,0:T(8,128)(2,1)S(1)}, u32[]{:S(2)}, u32[]{:S(2)}) collective-permute-start(bf16[512,128]{1,0:T(8,128)(2,1)S(1)} %get-tuple-element.55.st_ref.sc), channel_id=1, source_target_pairs={{4,0},{8,4},{12,8},{16,12},{20,16},{24,20},{28,24},{5,1},{9,5},{13... | collective-permute-start | bytes 393224 | tf_op jit(solution)/shard_map/ppermute | solution.py:25
  81.8 7.0 %copy-start.7 = (bf16[512,128]{1,0:T(8,128)(2,1)}, bf16[512,128]{1,0:T(8,128)(2,1)S(1)}, u32[]{:S(2)}) copy-start(bf16[512,128]{1,0:T(8,128)(2,1)S(1)} %collective-permute-done.10.se) | copy-start | bytes 393220
  86.4 2.4 %copy-start.8 = (bf16[512,128]{1,0:T(8,128)(2,1)}, bf16[512,128]{1,0:T(8,128)(2,1)S(1)}, u32[]{:S(2)}) copy-start(bf16[512,128]{1,0:T(8,128)(2,1)S(1)} %collective-permute-done.9.sd) | copy-start | bytes 393220
  88.8 8.4 %collective-permute-start.11 = (bf16[4,64,512]{2,1,0:T(8,128)(2,1)S(1)}, bf16[4,64,512]{2,1,0:T(8,128)(2,1)S(1)}, u32[]{:S(2)}, u32[]{:S(2)}) collective-permute-start(bf16[4,64,512]{2,1,0:T(8,128)(2,1)S(1)} %get-tuple-element.43), channel_id=1, source_target_pairs={{0,4},{4,0},{8,12},{12,8},{16,20},{20,16},{24,28},{28,24},{1,5},{5... | collective-permute-start | bytes 786440 | tf_op jit(solution)/shard_map/ppermute | solution.py:417
  97.3 6.6 %collective-permute-start.13 = (bf16[2,64,512]{2,1,0:T(8,128)(2,1)S(1)}, bf16[2,64,512]{2,1,0:T(8,128)(2,1)S(1)}, u32[]{:S(2)}, u32[]{:S(2)}) collective-permute-start(bf16[2,64,512]{2,1,0:T(8,128)(2,1)S(1)} %get-tuple-element.49), channel_id=1, source_target_pairs={{0,8},{4,12},{8,0},{12,4},{16,24},{20,28},{24,16},{28,20},{1,9},{5... | collective-permute-start | bytes 393224 | tf_op jit(solution)/shard_map/ppermute | solution.py:417
  104.0 7.8 %collective-permute-start.14 = (bf16[1,64,512]{2,1,0:T(8,128)(2,1)S(1)}, bf16[1,64,512]{2,1,0:T(8,128)(2,1)S(1)}, u32[]{:S(2)}, u32[]{:S(2)}) collective-permute-start(bf16[1,64,512]{2,1,0:T(8,128)(2,1)S(1)} %get-tuple-element.54), channel_id=1, source_target_pairs={{0,16},{4,20},{8,24},{12,28},{16,0},{20,4},{24,8},{28,12},{1,17},{... | collective-permute-start | bytes 196616 | tf_op jit(solution)/shard_map/ppermute | solution.py:417

commit v3 on v2

--- a/solution.py
+++ b/solution.py
@@ -377,6 +377,30 @@
     )(columns, *map(in_hbm, attn), in_hbm(grad_rows), *([] if got is None else [got]))
 
 
+def first_kernel(sel_ref, o_ref, g_ref, *rest):
+    w_ref = rest[-1]
+    w_ref[0] = dot(o_ref[...], g_ref[...]).astype(w_ref.dtype)
+
+
+def first_term(attn, chunk, chunks, grad_rows, columns, parts, before):
+    size, rows = attn.shape
+    cols = grad_rows.shape[1] // parts
+    return pl.pallas_call(
+        first_kernel,
+        grid_spec=pltpu.PrefetchScalarGridSpec(
+            num_scalar_prefetch=1, grid=(parts // 2,),
+            in_specs=[
+                pl.BlockSpec((size, rows), lambda i, s: (0, 0)),
+                pl.BlockSpec((rows, cols), lambda i, s: (0, s[0] + 2 * i)),
+            ] + [pl.BlockSpec(memory_space=pl.ANY)] * len(before),
+            out_specs=pl.BlockSpec((1, size, cols), lambda i, s: (i, chunk, 0)),
+        ),
+        out_shape=jax.ShapeDtypeStruct((parts // 2, size * chunks, cols), BF16),
+        input_output_aliases={3: 0} if before else {},
+        compiler_params=PARAMS, cost_estimate=lasting(2), name="first_term",
+    )(columns, attn, in_hbm(grad_rows), *before)
+
+
 def keep_kernel(sel_ref, o0_ref, o1_ref, g_ref, got_ref, moved_ref, send_ref, keep_ref):
     mine = sel_ref[2]
     count, size = send_ref.shape[0], send_ref.shape[1]
@@ -494,27 +518,28 @@
     far_sent = shift(sent, -2)
     parts = [Attention(rows, width, chunks, i * pairs // chunks, pairs // chunks) for i in range(chunks)]
     window = lambda i: [mine[i], far[i], paired[i], passed[i]]
-    attn, stats = [], []
-    from_forward = sent
-    for i in range(chunks):
-        half, after_half = parts[i].forward(from_forward, window(i), stats)
-        attn.append(half)
-        stats = [after_half]
-        if i == 0:
-            relayed = jnp.where(odd, sent, after(far_sent, half))
-            near_sent = swap(relayed, "ctx", 1)
-            from_forward = after(sent, relayed)
-    stats = stats[0]
-    near_stats = shift(stats, -1)
-    far_stats = shift(stats, -2)
-
     shares = lax.axis_size("dp")
     count = lax.axis_size("ctx")
     me = lax.axis_index("dp").astype(jnp.int32)
     core, chip = me % 2, me // 2
     low = lax.axis_index("ctx").astype(jnp.int32) % 2
     pick = lambda part, entry: jnp.stack([part, entry, low])
-    got = swap(weight_term(attn, grad_rows, pick(1 - core, core), shares, None, BF16), "dp", 1)
+    attn, stats, to_core = [], [], []
+    from_forward = sent
+    for i in range(chunks):
+        half, after_half = parts[i].forward(from_forward, window(i), stats)
+        attn.append(half)
+        stats = [after_half]
+        to_core = [first_term(half, i, chunks, grad_rows, pick(1 - core, core), shares, to_core)]
+        if i == 0:
+            relayed = jnp.where(odd, sent, after(far_sent, half))
+            near_sent = swap(relayed, "ctx", 1)
+            from_forward = after(sent, relayed, *to_core)
+    stats = stats[0]
+    near_stats = shift(stats, -1)
+    far_stats = shift(stats, -2)
+
+    got = swap(to_core[0], "dp", 1)
     to_chip = weight_term(attn, grad_rows, pick(2 * (1 - chip) + core, 1 - chip), shares, got, BF16)
     moved = swap(to_chip, "dp", 2)
     query_grad = []

time: 113 us -> 113 us (level)
  Pallas kernels: 55.8 us -> 58.2 us
  waiting for transfers between devices: 16.4 us -> 14.8 us
    pallas_call x0 -> x2, Pallas kernels: none -> 5.85 us  [first_term(): pl.pallas_call(first_kernel, grid_spec=pltpu.PrefetchScalarGridSpec(num_s...]
    pallas_call x2 -> x1, Pallas kernels: 5.8 us -> 2.34 us  [weight_term(): pl.pallas_call(weight_kernel, grid_spec=pltpu.PrefetchScalarGridSpec(num_...]
    ppermute x4, waiting for transfers between devices: 6.45 us -> 4.76 us  [within_pair(): lax.ppermute(x, 'ctx', [(i, i + 1) if to_odd else (i + 1, i) for i in ran...]
  transfers between devices with their start and end apart: 15 -> 15, of which waited for: 6 -> 5; matrix products, arithmetic and copies ran while one was open for 2% -> 2% of each run, Pallas kernels for 40% -> 43%
where the time goes in v3:
time: 113 us; the launch traced here: 112 us
  Pallas kernels  58.2 us (52%)
  starting transfers between devices  32.6 us (29%)
  waiting for transfers between devices  14.8 us (13%)
  other arithmetic  3.22 us (3%)
  local copies, waits for them, and re-layouts  2.49 us (2%)
    pallas_call x7, Pallas kernels, call(): pl.pallas_call(functools.partial(kernel, self.first), grid=(self.count,),...  45.1 us
    ppermute x5, starting transfers between devices, shift(): return lax.ppermute(x, 'ctx', pairs)  13.7 us
    ppermute x4, starting transfers between devices, within_pair(): lax.ppermute(x, 'ctx', [(i, i + 1) if to_odd else (i + 1, i) for i in ran...  13 us
    ppermute x5, waiting for transfers between devices, shift(): return lax.ppermute(x, 'ctx', pairs)  7.09 us
    pallas_call x2, Pallas kernels, first_term(): pl.pallas_call(first_kernel, grid_spec=pltpu.PrefetchScalarGridSpec(num_s...  5.85 us
    ppermute x6, starting transfers between devices, swap(): lax.ppermute(x, axis, [(i, i ^ bit) for i in range(lax.axis_size(axis))])  5.82 us
    ppermute x4, waiting for transfers between devices, within_pair(): lax.ppermute(x, 'ctx', [(i, i + 1) if to_odd else (i + 1, i) for i in ran...  4.76 us
    ppermute x6, waiting for transfers between devices, swap(): lax.ppermute(x, axis, [(i, i ^ bit) for i in range(lax.axis_size(axis))])  2.91 us
  transfers between devices with their start and end apart: 15, of which 5 were waited for; matrix products, arithmetic and copies ran while one was open for 2% of the time, Pallas kernels for 43%

profile of v3, /device:TPU:0, one launch (start us, length us, event | category | flops | bytes accessed | tf_op | source)
XLA Modules:
  0.0 112.2 jit_solution(12650857697502485405)
XLA Ops:
  0.6 0.7 add_convert_fusion
  1.3 0.0 copy-start.5
  1.3 1.4 %fusion = (bf16[512,256]{1,0:T(8,128)(2,1)S(1)}, bf16[512,256]{1,0:T(8,128)(2,1)S(1)}, bf16[512,256]{1,0:T(8,128)(2,1)S(1)}, bf16[512,256]{1,0:T(8,128)(2,1)S(1)}) fusion(bf16[512,512]{1,0:T(8,128)(2,1)} %bitcast.29, bf16[512,512]{1,0:T(8,128)(2,1)} %bitcast.30), kind=kLoop, calls=%fused_computation.7 | loop fusion | bytes 2097152 | tf_op jit(solution)/shard_map/slice | solution.py:509
  2.7 0.0 copy-start.1
  2.8 5.1 %collective-permute-start.1 = (bf16[528,512]{1,0:T(8,128)(2,1)S(1)}, bf16[528,512]{1,0:T(8,128)(2,1)S(1)}, u32[]{:S(2)}, u32[]{:S(2)}) collective-permute-start(bf16[528,512]{1,0:T(8,128)(2,1)S(1)} %pad_maximum_fusion.kc.vc.tc.k_ref.v_ref.t_ref), channel_id=1, source_target_pairs={{0,8},{4,12},{8,16},{12,20},{16,24},{20,28},{1,9},{5,13},{9,17},{1... | collective-permute-start | bytes 1622024 | tf_op jit(solution)/shard_map/ppermute | solution.py:25
  8.0 0.0 copy-done.5
  8.0 0.0 copy-done.1
  8.0 0.0 copy-start.6
  8.0 1.0 copy-done.6
  9.0 1.8 %queries_to_send.1.q_ref.g_ref.qc.gc = bf16[512,1024]{1,0:T(8,128)(2,1)S(1)} custom-call(bf16[512,512]{1,0:T(8,128)(2,1)S(1)} %bitcast.23, bf16[512,2048]{1,0:T(8,128)(2,1)S(1)} %bitcast.22, bf16[512,2048]{1,0:T(8,128)(2,1)S(1)} %copy-done.5), custom_call_target="tpu_custom_call" | custom-call | bytes 17500000 | tf_op jit(solution)/shard_map/queries_to_send/pallas_call | solution.py:337
  10.8 0.0 copy-start
  10.8 1.3 %collective-permute-start = (bf16[512,1024]{1,0:T(8,128)(2,1)S(1)}, bf16[512,1024]{1,0:T(8,128)(2,1)}, u32[]{:S(2)}, u32[]{:S(2)}) collective-permute-start(bf16[512,1024]{1,0:T(8,128)(2,1)S(1)} %queries_to_send.1.q_ref.g_ref.qc.gc), channel_id=1, source_target_pairs={{8,0},{12,4},{16,8},{20,12},{24,16},{28,20},{9,1},{13,5},{17,9},{2... | collective-permute-start | bytes 3145736 | tf_op jit(solution)/shard_map/ppermute | solution.py:25
  12.1 4.6 %collective-permute-start.4 = (bf16[528,512]{1,0:T(8,128)(2,1)S(1)}, bf16[528,512]{1,0:T(8,128)(2,1)S(1)}, u32[]{:S(2)}, u32[]{:S(2)}) collective-permute-start(bf16[528,512]{1,0:T(8,128)(2,1)S(1)} %pad_maximum_fusion.1.kc.vc.tc.k_ref.v_ref.t_ref), channel_id=1, source_target_pairs={{0,8},{4,12},{8,16},{12,20},{16,24},{20,28},{1,9},{5,13},{9,17},{1... | collective-permute-start | bytes 1622024 | tf_op jit(solution)/shard_map/ppermute | solution.py:25
  16.7 4.3 %collective-permute-start.2 = (bf16[528,512]{1,0:T(8,128)(2,1)S(1)}, bf16[528,512]{1,0:T(8,128)(2,1)}, u32[]{:S(2)}, u32[]{:S(2)}) collective-permute-start(bf16[528,512]{1,0:T(8,128)(2,1)S(1)} %pad_maximum_fusion.kc.vc.tc.k_ref.v_ref.t_ref), channel_id=1, source_target_pairs={{0,4},{8,12},{16,20},{24,28},{1,5},{9,13},{17,21},{25,29},{2,6},{1... | collective-permute-start | bytes 1622024 | tf_op jit(solution)/shard_map/ppermute | solution.py:446
  21.0 0.0 collective-permute-done.1.ka.va.ta
  21.0 1.3 %collective-permute-start.3 = (bf16[528,512]{1,0:T(8,128)(2,1)S(1)}, bf16[528,512]{1,0:T(8,128)(2,1)}, u32[]{:S(2)}, u32[]{:S(2)}) collective-permute-start(bf16[528,512]{1,0:T(8,128)(2,1)S(1)} %collective-permute-done.1.ka.va.ta), channel_id=1, source_target_pairs={{4,0},{12,8},{20,16},{28,24},{5,1},{13,9},{21,17},{29,25},{6,2},{1... | collective-permute-start | bytes 1622024 | tf_op jit(solution)/shard_map/ppermute | solution.py:446
  22.3 6.2 %collective-permute-start.5 = (bf16[528,512]{1,0:T(8,128)(2,1)S(1)}, bf16[528,512]{1,0:T(8,128)(2,1)}, u32[]{:S(2)}, u32[]{:S(2)}) collective-permute-start(bf16[528,512]{1,0:T(8,128)(2,1)S(1)} %pad_maximum_fusion.1.kc.vc.tc.k_ref.v_ref.t_ref), channel_id=1, source_target_pairs={{0,4},{8,12},{16,20},{24,28},{1,5},{9,13},{17,21},{25,29},{2,6},{1... | collective-permute-start | bytes 1622024 | tf_op jit(solution)/shard_map/ppermute | solution.py:446
  28.5 2.5 %collective-permute-done.4.ka.va.ta = bf16[528,512]{1,0:T(8,128)(2,1)S(1)} collective-permute-done((bf16[528,512]{1,0:T(8,128)(2,1)S(1)}, bf16[528,512]{1,0:T(8,128)(2,1)S(1)}, u32[]{:S(2)}, u32[]{:S(2)}) %collective-permute-start.4) | collective-permute-done | bytes 540704 | tf_op jit(solution)/shard_map/ppermute | solution.py:25
  31.0 1.3 %collective-permute-start.6 = (bf16[528,512]{1,0:T(8,128)(2,1)S(1)}, bf16[528,512]{1,0:T(8,128)(2,1)}, u32[]{:S(2)}, u32[]{:S(2)}) collective-permute-start(bf16[528,512]{1,0:T(8,128)(2,1)S(1)} %collective-permute-done.4.ka.va.ta), channel_id=1, source_target_pairs={{4,0},{12,8},{20,16},{28,24},{5,1},{13,9},{21,17},{29,25},{6,2},{1... | collective-permute-start | bytes 1622024 | tf_op jit(solution)/shard_map/ppermute | solution.py:446
  32.3 0.1 add_add_fusion.sel_ref
  32.4 0.5 collective-permute-done.2.ke.ve.te
  32.8 4.3 %collective-permute-done.3.ko.vo.to = bf16[528,512]{1,0:T(8,128)(2,1)} collective-permute-done((bf16[528,512]{1,0:T(8,128)(2,1)S(1)}, bf16[528,512]{1,0:T(8,128)(2,1)}, u32[]{:S(2)}, u32[]{:S(2)}) %collective-permute-start.3) | collective-permute-done | bytes 540704 | tf_op jit(solution)/shard_map/ppermute | solution.py:446
  37.1 6.2 %forward_kernel.2 = (bf16[256,512]{1,0:T(8,128)(2,1)S(1)}, bf16[512,128]{1,0:T(8,128)(2,1)S(1)}) custom-call(bf16[512,1024]{1,0:T(8,128)(2,1)S(1)} %queries_to_send.1.q_ref.g_ref.qc.gc, bf16[512,1024]{1,0:T(8,128)(2,1)S(1)} %queries_to_send.1.q_ref.g_ref.qc.gc, bf16[528,512]{1,0:T(8,128)(2,1)S(1)} %pad_maximum_fusion.kc.vc.tc.k_ref.v_ref.t_ref, ...), custom_call_target="tpu_custom_call" | custom-call | bytes 24500000 | tf_op jit(solution)/shard_map/forward_kernel/pallas_call | solution.py:287
  43.3 0.0 copy-start.3
  43.3 2.9 %first_term.2.rest_0_ = bf16[2,512,512]{2,1,0:T(8,128)(2,1)} custom-call(s32[3]{0:T(128)S(1)} %add_add_fusion.sel_ref, bf16[256,512]{1,0:T(8,128)(2,1)S(1)} %get-tuple-element.35.o_ref.refs_0_.o0_ref, bf16[512,2048]{1,0:T(8,128)(2,1)} %bitcast.18), custom_call_target="tpu_custom_call" | custom-call | bytes 7000000 | tf_op jit(solution)/shard_map/first_term/pallas_call | solution.py:388
  46.3 0.0 copy-done.3
  46.3 0.0 collective-permute-done.qe.ge
  46.3 2.3 %broadcast_select_fusion = bf16[512,1024]{1,0:T(8,128)(2,1)} fusion(bf16[512,1024]{1,0:T(8,128)(2,1)S(1)} %queries_to_send.1.q_ref.g_ref.qc.gc, bf16[512,1024]{1,0:T(8,128)(2,1)} %collective-permute-done.qe.ge, pred[]{:T(512)S(6)} %eq.9), kind=kLoop, calls=%fused_computation | loop fusion | flops 524288 | bytes 3145729 | tf_op jit(solution)/shard_map/jit(_where)/select_n | solution.py:535
  48.6 0.0 collective-permute-done.5.ke.ve.te
  48.6 0.0 collective-permute-done.6.ko.vo.to
  48.6 6.2 %forward_kernel.3 = (bf16[256,512]{1,0:T(8,128)(2,1)S(1)}, bf16[512,128]{1,0:T(8,128)(2,1)S(1)}) custom-call(bf16[512,1024]{1,0:T(8,128)(2,1)S(1)} %queries_to_send.1.q_ref.g_ref.qc.gc, bf16[512,1024]{1,0:T(8,128)(2,1)S(1)} %queries_to_send.1.q_ref.g_ref.qc.gc, bf16[528,512]{1,0:T(8,128)(2,1)S(1)} %pad_maximum_fusion.1.kc.vc.tc.k_ref.v_ref.t_ref, ...), custom_call_target="tpu_custom_call" | custom-call | bytes 24500000 | tf_op jit(solution)/shard_map/forward_kernel/pallas_call | solution.py:287
  54.8 0.0 copy-start.4
  54.8 0.0 copy-start.2
  54.8 2.9 %first_term.3 = bf16[2,512,512]{2,1,0:T(8,128)(2,1)} custom-call(s32[3]{0:T(128)S(1)} %add_add_fusion.sel_ref, bf16[256,512]{1,0:T(8,128)(2,1)S(1)} %get-tuple-element.40.o_ref.refs_1_.o1_ref, bf16[512,2048]{1,0:T(8,128)(2,1)} %bitcast.19, bf16[2,512,512]{2,1,0:T(8,128)(2,1)} %first_term.2.rest_0_), custom_call_target="tpu_custom_call", output_to_operand_aliasing={{}: (3, {})} | custom-call | bytes 7000000 | tf_op jit(solution)/shard_map/first_term/pallas_call | solution.py:388
  57.8 0.0 copy-done.4
  57.8 0.0 collective-permute-start.7
  57.8 0.0 collective-permute-start.12
  57.8 0.1 add_add_fusion.1
  57.9 2.9 %collective-permute-done.7.refs_3_.got_ref = bf16[2,512,512]{2,1,0:T(8,128)(2,1)} collective-permute-done((bf16[2,512,512]{2,1,0:T(8,128)(2,1)}, bf16[2,512,512]{2,1,0:T(8,128)(2,1)}, u32[]{:S(2)}, u32[]{:S(2)}) %collective-permute-start.7) | collective-permute-done | bytes 1048608 | tf_op jit(solution)/shard_map/ppermute | solution.py:441
  60.8 2.3 %weight_term.1 = bf16[1,512,512]{2,1,0:T(8,128)(2,1)S(1)} custom-call(s32[3]{0:T(128)S(1)} %get-tuple-element.67.sel_ref, bf16[256,512]{1,0:T(8,128)(2,1)} %copy-done.3, bf16[256,512]{1,0:T(8,128)(2,1)} %copy-done.4, bf16[512,2048]{1,0:T(8,128)(2,1)} %bitcast.20, bf16[2,512,512]{2,1,0:T(8,128)(2,1)} %collective-permute-done.7.refs_3_.got_ref), custom_call_target="tpu_custom_call" | custom-call | bytes 10500000 | tf_op jit(solution)/shard_map/weight_term/pallas_call | solution.py:367
  63.1 1.6 %collective-permute-start.8 = (bf16[1,512,512]{2,1,0:T(8,128)(2,1)S(1)}, bf16[1,512,512]{2,1,0:T(8,128)(2,1)S(1)}, u32[]{:S(2)}, u32[]{:S(2)}) collective-permute-start(bf16[1,512,512]{2,1,0:T(8,128)(2,1)S(1)} %weight_term.1), channel_id=1, source_target_pairs={{0,2},{1,3},{2,0},{3,1},{4,6},{5,7},{6,4},{7,5},{8,10},{9,11},{10,... | collective-permute-start | bytes 1572872 | tf_op jit(solution)/shard_map/ppermute | solution.py:441
  64.7 1.3 %collective-permute-start.10 = (bf16[512,128]{1,0:T(8,128)(2,1)S(1)}, bf16[512,128]{1,0:T(8,128)(2,1)S(1)}, u32[]{:S(2)}, u32[]{:S(2)}) collective-permute-start(bf16[512,128]{1,0:T(8,128)(2,1)S(1)} %get-tuple-element.55.st_ref.sc), channel_id=1, source_target_pairs={{8,0},{12,4},{16,8},{20,12},{24,16},{28,20},{9,1},{13,5},{17,9},{2... | collective-permute-start | bytes 393224 | tf_op jit(solution)/shard_map/ppermute | solution.py:25
  66.0 1.5 %collective-permute-start.9 = (bf16[512,128]{1,0:T(8,128)(2,1)S(1)}, bf16[512,128]{1,0:T(8,128)(2,1)S(1)}, u32[]{:S(2)}, u32[]{:S(2)}) collective-permute-start(bf16[512,128]{1,0:T(8,128)(2,1)S(1)} %get-tuple-element.55.st_ref.sc), channel_id=1, source_target_pairs={{4,0},{8,4},{12,8},{16,12},{20,16},{24,20},{28,24},{5,1},{9,5},{13... | collective-permute-start | bytes 393224 | tf_op jit(solution)/shard_map/ppermute | solution.py:25
  67.4 7.2 %query_kernel.2.rest_0_ = bf16[512,512]{1,0:T(8,128)(2,1)} custom-call(bf16[512,1024]{1,0:T(8,128)(2,1)S(1)} %queries_to_send.1.q_ref.g_ref.qc.gc, bf16[512,1024]{1,0:T(8,128)(2,1)S(1)} %queries_to_send.1.q_ref.g_ref.qc.gc, bf16[512,128]{1,0:T(8,128)(2,1)S(1)} %get-tuple-element.55.st_ref.sc, ...), custom_call_target="tpu_custom_call" | custom-call | bytes 24500000 | tf_op jit(solution)/shard_map/query_kernel/pallas_call | solution.py:287
  74.6 0.0 copy-done
  74.6 0.0 copy-done.2
  74.6 7.2 %query_kernel.3 = bf16[512,512]{1,0:T(8,128)(2,1)} custom-call(bf16[512,1024]{1,0:T(8,128)(2,1)S(1)} %queries_to_send.1.q_ref.g_ref.qc.gc, bf16[512,1024]{1,0:T(8,128)(2,1)S(1)} %queries_to_send.1.q_ref.g_ref.qc.gc, bf16[512,128]{1,0:T(8,128)(2,1)S(1)} %get-tuple-element.55.st_ref.sc, ...), custom_call_target="tpu_custom_call", output_to_operand_aliasing={{}: (15, {})} | custom-call | bytes 24500000 | tf_op jit(solution)/shard_map/query_kernel/pallas_call | solution.py:287
  81.8 0.0 collective-permute-done.10.se
  81.8 4.6 %collective-permute-done.9.sd = bf16[512,128]{1,0:T(8,128)(2,1)S(1)} collective-permute-done((bf16[512,128]{1,0:T(8,128)(2,1)S(1)}, bf16[512,128]{1,0:T(8,128)(2,1)S(1)}, u32[]{:S(2)}, u32[]{:S(2)}) %collective-permute-start.9) | collective-permute-done | bytes 131104 | tf_op jit(solution)/shard_map/ppermute | solution.py:25
  86.4 0.0 collective-permute-done.8.moved_ref
  86.4 2.4 %keep_term.1 = (bf16[4,64,512]{2,1,0:T(8,128)(2,1)S(1)}, f32[4,64,512]{2,1,0:T(8,128)S(1)}) custom-call(s32[3]{0:T(128)S(1)} %get-tuple-element.66.sel_ref, bf16[256,512]{1,0:T(8,128)(2,1)} %copy-done.3, bf16[256,512]{1,0:T(8,128)(2,1)} %copy-done.4, bf16[512,2048]{1,0:T(8,128)(2,1)} %bitcast.21, ...), custom_call_target="tpu_custom_call" | custom-call | bytes 10500000 | tf_op jit(solution)/shard_map/keep_term/pallas_call | solution.py:424
  88.8 0.0 copy-done.7
  88.8 0.1 collective-permute-start.11
  88.9 0.0 collective-permute-done.12.qd.gd
  88.9 8.3 %key_kernel.3 = (bf16[512,512]{1,0:T(8,128)(2,1)}, bf16[512,512]{1,0:T(8,128)(2,1)}) custom-call(bf16[528,512]{1,0:T(8,128)(2,1)S(1)} %pad_maximum_fusion.kc.vc.tc.k_ref.v_ref.t_ref, bf16[528,512]{1,0:T(8,128)(2,1)S(1)} %pad_maximum_fusion.kc.vc.tc.k_ref.v_ref.t_ref, bf16[528,512]{1,0:T(8,128)(2,1)S(1)} %pad_maximum_fusion.kc.vc.tc.k_ref.v_ref.t_ref, ...), custom_call_target="tpu_custom_call" | custom-call | bytes 29400000 | tf_op jit(solution)/shard_map/key_kernel/pallas_call | solution.py:287
  97.2 0.0 collective-permute-done.11.got_ref
  97.2 0.1 stage.2
  97.3 0.8 collective-permute-start.13
  98.0 5.0 %key_kernel.4 = (bf16[512,512]{1,0:T(8,128)(2,1)}, bf16[512,512]{1,0:T(8,128)(2,1)}) custom-call(bf16[528,512]{1,0:T(8,128)(2,1)S(1)} %pad_maximum_fusion.1.kc.vc.tc.k_ref.v_ref.t_ref, bf16[528,512]{1,0:T(8,128)(2,1)S(1)} %pad_maximum_fusion.1.kc.vc.tc.k_ref.v_ref.t_ref, ...), custom_call_target="tpu_custom_call", output_to_operand_aliasing={{0}: (12, {}), {1}: (13, {})} | custom-call | bytes 14700000 | tf_op jit(solution)/shard_map/key_kernel/pallas_call | solution.py:287
  103.0 0.0 collective-permute-done.13.got_ref
  103.1 3.4 %collective-permute-start.14 = (bf16[1,64,512]{2,1,0:T(8,128)(2,1)S(1)}, bf16[1,64,512]{2,1,0:T(8,128)(2,1)S(1)}, u32[]{:S(2)}, u32[]{:S(2)}) collective-permute-start(bf16[1,64,512]{2,1,0:T(8,128)(2,1)S(1)} %get-tuple-element.54), channel_id=1, source_target_pairs={{0,16},{4,20},{8,24},{12,28},{16,0},{20,4},{24,8},{28,12},{1,17},{... | collective-permute-start | bytes 196616 | tf_op jit(solution)/shard_map/ppermute | solution.py:441
  106.5 5.0 %key_kernel.5 = (bf16[512,512]{1,0:T(8,128)(2,1)}, bf16[512,512]{1,0:T(8,128)(2,1)}) custom-call(bf16[528,512]{1,0:T(8,128)(2,1)S(1)} %pad_maximum_fusion.1.kc.vc.tc.k_ref.v_ref.t_ref, bf16[528,512]{1,0:T(8,128)(2,1)S(1)} %pad_maximum_fusion.1.kc.vc.tc.k_ref.v_ref.t_ref, ...), custom_call_target="tpu_custom_call", output_to_operand_aliasing={{0}: (12, {}), {1}: (13, {})} | custom-call | bytes 14700000 | tf_op jit(solution)/shard_map/key_kernel/pallas_call | solution.py:287
  111.6 0.0 collective-permute-done.14
  111.6 0.7 last_sum.1
  (7 shorter events, 0.1 us)
Async XLA Ops:
  1.3 6.6 %copy-start.5 = (bf16[512,2048]{1,0:T(8,128)(2,1)S(1)}, bf16[512,2048]{1,0:T(8,128)(2,1)}, u32[]{:S(2)}) copy-start(bf16[512,2048]{1,0:T(8,128)(2,1)} %w_ref.1) | copy-start | bytes 6291460
  2.7 5.2 %copy-start.1 = (bf16[1,512,2048]{2,1,0:T(8,128)(2,1)S(1)}, bf16[1,512,2048]{2,1,0:T(8,128)(2,1)}, u32[]{:S(2)}) copy-start(bf16[1,512,2048]{2,1,0:T(8,128)(2,1)} %param.10) | copy-start | bytes 6291460
  2.8 18.2 %collective-permute-start.1 = (bf16[528,512]{1,0:T(8,128)(2,1)S(1)}, bf16[528,512]{1,0:T(8,128)(2,1)S(1)}, u32[]{:S(2)}, u32[]{:S(2)}) collective-permute-start(bf16[528,512]{1,0:T(8,128)(2,1)S(1)} %pad_maximum_fusion.kc.vc.tc.k_ref.v_ref.t_ref), channel_id=1, source_target_pairs={{0,8},{4,12},{8,16},{12,20},{16,24},{20,28},{1,9},{5,13},{9,17},{1... | collective-permute-start | bytes 1622024 | tf_op jit(solution)/shard_map/ppermute | solution.py:25
  8.0 1.0 copy-start.6
  10.8 63.8 %copy-start = (bf16[512,1024]{1,0:T(8,128)(2,1)}, bf16[512,1024]{1,0:T(8,128)(2,1)S(1)}, u32[]{:S(2)}) copy-start(bf16[512,1024]{1,0:T(8,128)(2,1)S(1)} %queries_to_send.1.q_ref.g_ref.qc.gc) | copy-start | bytes 3145732
  10.8 35.5 %collective-permute-start = (bf16[512,1024]{1,0:T(8,128)(2,1)S(1)}, bf16[512,1024]{1,0:T(8,128)(2,1)}, u32[]{:S(2)}, u32[]{:S(2)}) collective-permute-start(bf16[512,1024]{1,0:T(8,128)(2,1)S(1)} %queries_to_send.1.q_ref.g_ref.qc.gc), channel_id=1, source_target_pairs={{8,0},{12,4},{16,8},{20,12},{24,16},{28,20},{9,1},{13,5},{17,9},{2... | collective-permute-start | bytes 3145736 | tf_op jit(solution)/shard_map/ppermute | solution.py:25
  12.1 18.9 %collective-permute-start.4 = (bf16[528,512]{1,0:T(8,128)(2,1)S(1)}, bf16[528,512]{1,0:T(8,128)(2,1)S(1)}, u32[]{:S(2)}, u32[]{:S(2)}) collective-permute-start(bf16[528,512]{1,0:T(8,128)(2,1)S(1)} %pad_maximum_fusion.1.kc.vc.tc.k_ref.v_ref.t_ref), channel_id=1, source_target_pairs={{0,8},{4,12},{8,16},{12,20},{16,24},{20,28},{1,9},{5,13},{9,17},{1... | collective-permute-start | bytes 1622024 | tf_op jit(solution)/shard_map/ppermute | solution.py:25
  16.7 16.1 %collective-permute-start.2 = (bf16[528,512]{1,0:T(8,128)(2,1)S(1)}, bf16[528,512]{1,0:T(8,128)(2,1)}, u32[]{:S(2)}, u32[]{:S(2)}) collective-permute-start(bf16[528,512]{1,0:T(8,128)(2,1)S(1)} %pad_maximum_fusion.kc.vc.tc.k_ref.v_ref.t_ref), channel_id=1, source_target_pairs={{0,4},{8,12},{16,20},{24,28},{1,5},{9,13},{17,21},{25,29},{2,6},{1... | collective-permute-start | bytes 1622024 | tf_op jit(solution)/shard_map/ppermute | solution.py:446
  21.0 16.2 %collective-permute-start.3 = (bf16[528,512]{1,0:T(8,128)(2,1)S(1)}, bf16[528,512]{1,0:T(8,128)(2,1)}, u32[]{:S(2)}, u32[]{:S(2)}) collective-permute-start(bf16[528,512]{1,0:T(8,128)(2,1)S(1)} %collective-permute-done.1.ka.va.ta), channel_id=1, source_target_pairs={{4,0},{12,8},{20,16},{28,24},{5,1},{13,9},{21,17},{29,25},{6,2},{1... | collective-permute-start | bytes 1622024 | tf_op jit(solution)/shard_map/ppermute | solution.py:446
  22.3 26.3 %collective-permute-start.5 = (bf16[528,512]{1,0:T(8,128)(2,1)S(1)}, bf16[528,512]{1,0:T(8,128)(2,1)}, u32[]{:S(2)}, u32[]{:S(2)}) collective-permute-start(bf16[528,512]{1,0:T(8,128)(2,1)S(1)} %pad_maximum_fusion.1.kc.vc.tc.k_ref.v_ref.t_ref), channel_id=1, source_target_pairs={{0,4},{8,12},{16,20},{24,28},{1,5},{9,13},{17,21},{25,29},{2,6},{1... | collective-permute-start | bytes 1622024 | tf_op jit(solution)/shard_map/ppermute | solution.py:446
  31.0 17.6 %collective-permute-start.6 = (bf16[528,512]{1,0:T(8,128)(2,1)S(1)}, bf16[528,512]{1,0:T(8,128)(2,1)}, u32[]{:S(2)}, u32[]{:S(2)}) collective-permute-start(bf16[528,512]{1,0:T(8,128)(2,1)S(1)} %collective-permute-done.4.ka.va.ta), channel_id=1, source_target_pairs={{4,0},{12,8},{20,16},{28,24},{5,1},{13,9},{21,17},{29,25},{6,2},{1... | collective-permute-start | bytes 1622024 | tf_op jit(solution)/shard_map/ppermute | solution.py:446
  43.3 2.9 %copy-start.3 = (bf16[256,512]{1,0:T(8,128)(2,1)}, bf16[256,512]{1,0:T(8,128)(2,1)S(1)}, u32[]{:S(2)}) copy-start(bf16[256,512]{1,0:T(8,128)(2,1)S(1)} %get-tuple-element.35.o_ref.refs_0_.o0_ref) | copy-start | bytes 786436
  54.8 2.9 %copy-start.4 = (bf16[256,512]{1,0:T(8,128)(2,1)}, bf16[256,512]{1,0:T(8,128)(2,1)S(1)}, u32[]{:S(2)}) copy-start(bf16[256,512]{1,0:T(8,128)(2,1)S(1)} %get-tuple-element.40.o_ref.refs_1_.o1_ref) | copy-start | bytes 786436
  54.8 19.8 %copy-start.2 = (bf16[512,128]{1,0:T(8,128)(2,1)}, bf16[512,128]{1,0:T(8,128)(2,1)S(1)}, u32[]{:S(2)}) copy-start(bf16[512,128]{1,0:T(8,128)(2,1)S(1)} %get-tuple-element.55.st_ref.sc) | copy-start | bytes 393220
  57.8 3.0 %collective-permute-start.7 = (bf16[2,512,512]{2,1,0:T(8,128)(2,1)}, bf16[2,512,512]{2,1,0:T(8,128)(2,1)}, u32[]{:S(2)}, u32[]{:S(2)}) collective-permute-start(bf16[2,512,512]{2,1,0:T(8,128)(2,1)} %first_term.3), channel_id=1, source_target_pairs={{0,1},{1,0},{2,3},{3,2},{4,5},{5,4},{6,7},{7,6},{8,9},{9,8},{10,11... | collective-permute-start | bytes 3145736 | tf_op jit(solution)/shard_map/ppermute | solution.py:441
  57.8 31.1 %collective-permute-start.12 = (bf16[512,1024]{1,0:T(8,128)(2,1)}, bf16[512,1024]{1,0:T(8,128)(2,1)}, u32[]{:S(2)}, u32[]{:S(2)}) collective-permute-start(bf16[512,1024]{1,0:T(8,128)(2,1)} %broadcast_select_fusion), channel_id=1, source_target_pairs={{0,4},{4,0},{8,12},{12,8},{16,20},{20,16},{24,28},{28,24},{1,5},{5... | collective-permute-start | bytes 3145736 | tf_op jit(solution)/shard_map/ppermute | solution.py:441
  63.1 23.2 %collective-permute-start.8 = (bf16[1,512,512]{2,1,0:T(8,128)(2,1)S(1)}, bf16[1,512,512]{2,1,0:T(8,128)(2,1)S(1)}, u32[]{:S(2)}, u32[]{:S(2)}) collective-permute-start(bf16[1,512,512]{2,1,0:T(8,128)(2,1)S(1)} %weight_term.1), channel_id=1, source_target_pairs={{0,2},{1,3},{2,0},{3,1},{4,6},{5,7},{6,4},{7,5},{8,10},{9,11},{10,... | collective-permute-start | bytes 1572872 | tf_op jit(solution)/shard_map/ppermute | solution.py:441
  64.7 17.1 %collective-permute-start.10 = (bf16[512,128]{1,0:T(8,128)(2,1)S(1)}, bf16[512,128]{1,0:T(8,128)(2,1)S(1)}, u32[]{:S(2)}, u32[]{:S(2)}) collective-permute-start(bf16[512,128]{1,0:T(8,128)(2,1)S(1)} %get-tuple-element.55.st_ref.sc), channel_id=1, source_target_pairs={{8,0},{12,4},{16,8},{20,12},{24,16},{28,20},{9,1},{13,5},{17,9},{2... | collective-permute-start | bytes 393224 | tf_op jit(solution)/shard_map/ppermute | solution.py:25
  66.0 20.4 %collective-permute-start.9 = (bf16[512,128]{1,0:T(8,128)(2,1)S(1)}, bf16[512,128]{1,0:T(8,128)(2,1)S(1)}, u32[]{:S(2)}, u32[]{:S(2)}) collective-permute-start(bf16[512,128]{1,0:T(8,128)(2,1)S(1)} %get-tuple-element.55.st_ref.sc), channel_id=1, source_target_pairs={{4,0},{8,4},{12,8},{16,12},{20,16},{24,20},{28,24},{5,1},{9,5},{13... | collective-permute-start | bytes 393224 | tf_op jit(solution)/shard_map/ppermute | solution.py:25
  81.8 7.0 %copy-start.7 = (bf16[512,128]{1,0:T(8,128)(2,1)}, bf16[512,128]{1,0:T(8,128)(2,1)S(1)}, u32[]{:S(2)}) copy-start(bf16[512,128]{1,0:T(8,128)(2,1)S(1)} %collective-permute-done.10.se) | copy-start | bytes 393220
  86.4 2.4 %copy-start.8 = (bf16[512,128]{1,0:T(8,128)(2,1)}, bf16[512,128]{1,0:T(8,128)(2,1)S(1)}, u32[]{:S(2)}) copy-start(bf16[512,128]{1,0:T(8,128)(2,1)S(1)} %collective-permute-done.9.sd) | copy-start | bytes 393220
  88.8 8.4 %collective-permute-start.11 = (bf16[4,64,512]{2,1,0:T(8,128)(2,1)S(1)}, bf16[4,64,512]{2,1,0:T(8,128)(2,1)S(1)}, u32[]{:S(2)}, u32[]{:S(2)}) collective-permute-start(bf16[4,64,512]{2,1,0:T(8,128)(2,1)S(1)} %get-tuple-element.43), channel_id=1, source_target_pairs={{0,4},{4,0},{8,12},{12,8},{16,20},{20,16},{24,28},{28,24},{1,5},{5... | collective-permute-start | bytes 786440 | tf_op jit(solution)/shard_map/ppermute | solution.py:441
  97.3 5.8 %collective-permute-start.13 = (bf16[2,64,512]{2,1,0:T(8,128)(2,1)S(1)}, bf16[2,64,512]{2,1,0:T(8,128)(2,1)S(1)}, u32[]{:S(2)}, u32[]{:S(2)}) collective-permute-start(bf16[2,64,512]{2,1,0:T(8,128)(2,1)S(1)} %get-tuple-element.49), channel_id=1, source_target_pairs={{0,8},{4,12},{8,0},{12,4},{16,24},{20,28},{24,16},{28,20},{1,9},{5... | collective-permute-start | bytes 393224 | tf_op jit(solution)/shard_map/ppermute | solution.py:441
  103.1 8.5 %collective-permute-start.14 = (bf16[1,64,512]{2,1,0:T(8,128)(2,1)S(1)}, bf16[1,64,512]{2,1,0:T(8,128)(2,1)S(1)}, u32[]{:S(2)}, u32[]{:S(2)}) collective-permute-start(bf16[1,64,512]{2,1,0:T(8,128)(2,1)S(1)} %get-tuple-element.54), channel_id=1, source_target_pairs={{0,16},{4,20},{8,24},{12,28},{16,0},{20,4},{24,8},{28,12},{1,17},{... | collective-permute-start | bytes 196616 | tf_op jit(solution)/shard_map/ppermute | solution.py:441

commit v4 on v3

--- a/solution.py
+++ b/solution.py
@@ -311,7 +311,7 @@
     def key(self, held, sources, before):
         return self.call(
             key_kernel, self.held + (self.sent + [self.stat]) * 3,
-            [held] * 3 + [in_hbm(x) for q, st in sources for x in (q, q, st)],
+            [held] * 3 + [y for q, st in sources for y in (in_hbm(q), in_hbm(q), st)],
             [self.out] * 2, [(self.rows, self.width)] * 2, [self.extra] + [self.total] * 4,
             before, True, 4.2,
         )

time: 113 us -> 113 us (level)
  no operation moved by 1% of the time
where the time goes in v4:
time: 113 us; the launch traced here: 112 us
  Pallas kernels  57.8 us (51%)
  starting transfers between devices  32.5 us (29%)
  waiting for transfers between devices  14.8 us (13%)
  other arithmetic  3.24 us (3%)
  local copies, waits for them, and re-layouts  3.14 us (3%)
    pallas_call x7, Pallas kernels, call(): pl.pallas_call(functools.partial(kernel, self.first), grid=(self.count,),...  44.7 us
    ppermute x5, starting transfers between devices, shift(): return lax.ppermute(x, 'ctx', pairs)  13.7 us
    ppermute x4, starting transfers between devices, within_pair(): lax.ppermute(x, 'ctx', [(i, i + 1) if to_odd else (i + 1, i) for i in ran...  13.1 us
    ppermute x5, waiting for transfers between devices, shift(): return lax.ppermute(x, 'ctx', pairs)  7.09 us
    pallas_call x2, Pallas kernels, first_term(): pl.pallas_call(first_kernel, grid_spec=pltpu.PrefetchScalarGridSpec(num_s...  5.86 us
    ppermute x6, starting transfers between devices, swap(): lax.ppermute(x, axis, [(i, i ^ bit) for i in range(lax.axis_size(axis))])  5.77 us
    ppermute x4, waiting for transfers between devices, within_pair(): lax.ppermute(x, 'ctx', [(i, i + 1) if to_odd else (i + 1, i) for i in ran...  4.8 us
    ppermute x6, waiting for transfers between devices, swap(): lax.ppermute(x, axis, [(i, i ^ bit) for i in range(lax.axis_size(axis))])  2.91 us
  transfers between devices with their start and end apart: 15, of which 5 were waited for; matrix products, arithmetic and copies ran while one was open for 2% of the time, Pallas kernels for 43%

profile of v4, /device:TPU:0, one launch (start us, length us, event | category | flops | bytes accessed | tf_op | source)
XLA Modules:
  0.0 112.5 jit_solution(3745476785457184955)
XLA Ops:
  0.6 0.7 add_convert_fusion
  1.3 0.0 copy-start.4
  1.3 1.4 %fusion = (bf16[512,256]{1,0:T(8,128)(2,1)S(1)}, bf16[512,256]{1,0:T(8,128)(2,1)S(1)}, bf16[512,256]{1,0:T(8,128)(2,1)S(1)}, bf16[512,256]{1,0:T(8,128)(2,1)S(1)}) fusion(bf16[512,512]{1,0:T(8,128)(2,1)} %bitcast.29, bf16[512,512]{1,0:T(8,128)(2,1)} %bitcast.30), kind=kLoop, calls=%fused_computation.7 | loop fusion | bytes 2097152 | tf_op jit(solution)/shard_map/slice | solution.py:509
  2.7 0.0 copy-start.1
  2.8 5.1 %collective-permute-start.1 = (bf16[528,512]{1,0:T(8,128)(2,1)S(1)}, bf16[528,512]{1,0:T(8,128)(2,1)S(1)}, u32[]{:S(2)}, u32[]{:S(2)}) collective-permute-start(bf16[528,512]{1,0:T(8,128)(2,1)S(1)} %pad_maximum_fusion.kc.vc.tc.k_ref.v_ref.t_ref), channel_id=1, source_target_pairs={{0,8},{4,12},{8,16},{12,20},{16,24},{20,28},{1,9},{5,13},{9,17},{1... | collective-permute-start | bytes 1622024 | tf_op jit(solution)/shard_map/ppermute | solution.py:25
  8.0 0.0 copy-done.4
  8.0 0.0 copy-done.1
  8.0 0.0 copy-start.7
  8.0 1.0 copy-done.7
  9.0 1.8 %queries_to_send.1.q_ref.g_ref.qc.gc = bf16[512,1024]{1,0:T(8,128)(2,1)S(1)} custom-call(bf16[512,512]{1,0:T(8,128)(2,1)S(1)} %bitcast.23, bf16[512,2048]{1,0:T(8,128)(2,1)S(1)} %bitcast.22, bf16[512,2048]{1,0:T(8,128)(2,1)S(1)} %copy-done.4), custom_call_target="tpu_custom_call" | custom-call | bytes 17500000 | tf_op jit(solution)/shard_map/queries_to_send/pallas_call | solution.py:337
  10.8 0.0 copy-start
  10.8 1.3 %collective-permute-start = (bf16[512,1024]{1,0:T(8,128)(2,1)S(1)}, bf16[512,1024]{1,0:T(8,128)(2,1)}, u32[]{:S(2)}, u32[]{:S(2)}) collective-permute-start(bf16[512,1024]{1,0:T(8,128)(2,1)S(1)} %queries_to_send.1.q_ref.g_ref.qc.gc), channel_id=1, source_target_pairs={{8,0},{12,4},{16,8},{20,12},{24,16},{28,20},{9,1},{13,5},{17,9},{2... | collective-permute-start | bytes 3145736 | tf_op jit(solution)/shard_map/ppermute | solution.py:25
  12.1 4.6 %collective-permute-start.4 = (bf16[528,512]{1,0:T(8,128)(2,1)S(1)}, bf16[528,512]{1,0:T(8,128)(2,1)S(1)}, u32[]{:S(2)}, u32[]{:S(2)}) collective-permute-start(bf16[528,512]{1,0:T(8,128)(2,1)S(1)} %pad_maximum_fusion.1.kc.vc.tc.k_ref.v_ref.t_ref), channel_id=1, source_target_pairs={{0,8},{4,12},{8,16},{12,20},{16,24},{20,28},{1,9},{5,13},{9,17},{1... | collective-permute-start | bytes 1622024 | tf_op jit(solution)/shard_map/ppermute | solution.py:25
  16.7 4.3 %collective-permute-start.2 = (bf16[528,512]{1,0:T(8,128)(2,1)S(1)}, bf16[528,512]{1,0:T(8,128)(2,1)}, u32[]{:S(2)}, u32[]{:S(2)}) collective-permute-start(bf16[528,512]{1,0:T(8,128)(2,1)S(1)} %pad_maximum_fusion.kc.vc.tc.k_ref.v_ref.t_ref), channel_id=1, source_target_pairs={{0,4},{8,12},{16,20},{24,28},{1,5},{9,13},{17,21},{25,29},{2,6},{1... | collective-permute-start | bytes 1622024 | tf_op jit(solution)/shard_map/ppermute | solution.py:446
  21.0 0.0 collective-permute-done.1.ka.va.ta
  21.0 1.3 %collective-permute-start.3 = (bf16[528,512]{1,0:T(8,128)(2,1)S(1)}, bf16[528,512]{1,0:T(8,128)(2,1)}, u32[]{:S(2)}, u32[]{:S(2)}) collective-permute-start(bf16[528,512]{1,0:T(8,128)(2,1)S(1)} %collective-permute-done.1.ka.va.ta), channel_id=1, source_target_pairs={{4,0},{12,8},{20,16},{28,24},{5,1},{13,9},{21,17},{29,25},{6,2},{1... | collective-permute-start | bytes 1622024 | tf_op jit(solution)/shard_map/ppermute | solution.py:446
  22.3 6.2 %collective-permute-start.5 = (bf16[528,512]{1,0:T(8,128)(2,1)S(1)}, bf16[528,512]{1,0:T(8,128)(2,1)}, u32[]{:S(2)}, u32[]{:S(2)}) collective-permute-start(bf16[528,512]{1,0:T(8,128)(2,1)S(1)} %pad_maximum_fusion.1.kc.vc.tc.k_ref.v_ref.t_ref), channel_id=1, source_target_pairs={{0,4},{8,12},{16,20},{24,28},{1,5},{9,13},{17,21},{25,29},{2,6},{1... | collective-permute-start | bytes 1622024 | tf_op jit(solution)/shard_map/ppermute | solution.py:446
  28.5 2.5 %collective-permute-done.4.ka.va.ta = bf16[528,512]{1,0:T(8,128)(2,1)S(1)} collective-permute-done((bf16[528,512]{1,0:T(8,128)(2,1)S(1)}, bf16[528,512]{1,0:T(8,128)(2,1)S(1)}, u32[]{:S(2)}, u32[]{:S(2)}) %collective-permute-start.4) | collective-permute-done | bytes 540704 | tf_op jit(solution)/shard_map/ppermute | solution.py:25
  31.0 1.3 %collective-permute-start.6 = (bf16[528,512]{1,0:T(8,128)(2,1)S(1)}, bf16[528,512]{1,0:T(8,128)(2,1)}, u32[]{:S(2)}, u32[]{:S(2)}) collective-permute-start(bf16[528,512]{1,0:T(8,128)(2,1)S(1)} %collective-permute-done.4.ka.va.ta), channel_id=1, source_target_pairs={{4,0},{12,8},{20,16},{28,24},{5,1},{13,9},{21,17},{29,25},{6,2},{1... | collective-permute-start | bytes 1622024 | tf_op jit(solution)/shard_map/ppermute | solution.py:446
  32.3 0.1 add_add_fusion.sel_ref
  32.4 0.5 collective-permute-done.2.ke.ve.te
  32.8 4.3 %collective-permute-done.3.ko.vo.to = bf16[528,512]{1,0:T(8,128)(2,1)} collective-permute-done((bf16[528,512]{1,0:T(8,128)(2,1)S(1)}, bf16[528,512]{1,0:T(8,128)(2,1)}, u32[]{:S(2)}, u32[]{:S(2)}) %collective-permute-start.3) | collective-permute-done | bytes 540704 | tf_op jit(solution)/shard_map/ppermute | solution.py:446
  37.2 6.2 %forward_kernel.2 = (bf16[256,512]{1,0:T(8,128)(2,1)S(1)}, bf16[512,128]{1,0:T(8,128)(2,1)S(1)}) custom-call(bf16[512,1024]{1,0:T(8,128)(2,1)S(1)} %queries_to_send.1.q_ref.g_ref.qc.gc, bf16[512,1024]{1,0:T(8,128)(2,1)S(1)} %queries_to_send.1.q_ref.g_ref.qc.gc, bf16[528,512]{1,0:T(8,128)(2,1)S(1)} %pad_maximum_fusion.kc.vc.tc.k_ref.v_ref.t_ref, ...), custom_call_target="tpu_custom_call" | custom-call | bytes 24500000 | tf_op jit(solution)/shard_map/forward_kernel/pallas_call | solution.py:287
  43.4 0.0 copy-start.2
  43.4 2.9 %first_term.2.rest_0_ = bf16[2,512,512]{2,1,0:T(8,128)(2,1)} custom-call(s32[3]{0:T(128)S(1)} %add_add_fusion.sel_ref, bf16[256,512]{1,0:T(8,128)(2,1)S(1)} %get-tuple-element.35.o_ref.refs_0_.o0_ref, bf16[512,2048]{1,0:T(8,128)(2,1)} %bitcast.18), custom_call_target="tpu_custom_call" | custom-call | bytes 7000000 | tf_op jit(solution)/shard_map/first_term/pallas_call | solution.py:388
  46.3 0.0 copy-done.2
  46.3 0.0 collective-permute-done.qe.ge
  46.3 2.3 %broadcast_select_fusion = bf16[512,1024]{1,0:T(8,128)(2,1)} fusion(bf16[512,1024]{1,0:T(8,128)(2,1)S(1)} %queries_to_send.1.q_ref.g_ref.qc.gc, bf16[512,1024]{1,0:T(8,128)(2,1)} %collective-permute-done.qe.ge, pred[]{:T(512)S(6)} %eq.9), kind=kLoop, calls=%fused_computation | loop fusion | flops 524288 | bytes 3145729 | tf_op jit(solution)/shard_map/jit(_where)/select_n | solution.py:535
  48.6 0.0 collective-permute-done.5.ke.ve.te
  48.6 0.0 collective-permute-done.6.ko.vo.to
  48.6 6.2 %forward_kernel.3 = (bf16[256,512]{1,0:T(8,128)(2,1)S(1)}, bf16[512,128]{1,0:T(8,128)(2,1)S(1)}) custom-call(bf16[512,1024]{1,0:T(8,128)(2,1)S(1)} %queries_to_send.1.q_ref.g_ref.qc.gc, bf16[512,1024]{1,0:T(8,128)(2,1)S(1)} %queries_to_send.1.q_ref.g_ref.qc.gc, bf16[528,512]{1,0:T(8,128)(2,1)S(1)} %pad_maximum_fusion.1.kc.vc.tc.k_ref.v_ref.t_ref, ...), custom_call_target="tpu_custom_call" | custom-call | bytes 24500000 | tf_op jit(solution)/shard_map/forward_kernel/pallas_call | solution.py:287
  54.9 0.0 copy-start.3
  54.9 2.9 %first_term.3 = bf16[2,512,512]{2,1,0:T(8,128)(2,1)} custom-call(s32[3]{0:T(128)S(1)} %add_add_fusion.sel_ref, bf16[256,512]{1,0:T(8,128)(2,1)S(1)} %get-tuple-element.40.o_ref.refs_1_.o1_ref, bf16[512,2048]{1,0:T(8,128)(2,1)} %bitcast.19, bf16[2,512,512]{2,1,0:T(8,128)(2,1)} %first_term.2.rest_0_), custom_call_target="tpu_custom_call", output_to_operand_aliasing={{}: (3, {})} | custom-call | bytes 7000000 | tf_op jit(solution)/shard_map/first_term/pallas_call | solution.py:388
  57.8 0.0 copy-done.3
  57.8 0.0 collective-permute-start.7
  57.8 0.0 collective-permute-start.12
  57.8 0.1 add_add_fusion.1
  57.9 2.9 %collective-permute-done.7.refs_3_.got_ref = bf16[2,512,512]{2,1,0:T(8,128)(2,1)} collective-permute-done((bf16[2,512,512]{2,1,0:T(8,128)(2,1)}, bf16[2,512,512]{2,1,0:T(8,128)(2,1)}, u32[]{:S(2)}, u32[]{:S(2)}) %collective-permute-start.7) | collective-permute-done | bytes 1048608 | tf_op jit(solution)/shard_map/ppermute | solution.py:441
  60.8 2.3 %weight_term.1 = bf16[1,512,512]{2,1,0:T(8,128)(2,1)S(1)} custom-call(s32[3]{0:T(128)S(1)} %get-tuple-element.67.sel_ref, bf16[256,512]{1,0:T(8,128)(2,1)} %copy-done.2, bf16[256,512]{1,0:T(8,128)(2,1)} %copy-done.3, bf16[512,2048]{1,0:T(8,128)(2,1)} %bitcast.20, bf16[2,512,512]{2,1,0:T(8,128)(2,1)} %collective-permute-done.7.refs_3_.got_ref), custom_call_target="tpu_custom_call" | custom-call | bytes 10500000 | tf_op jit(solution)/shard_map/weight_term/pallas_call | solution.py:367
  63.2 1.6 %collective-permute-start.8 = (bf16[1,512,512]{2,1,0:T(8,128)(2,1)S(1)}, bf16[1,512,512]{2,1,0:T(8,128)(2,1)S(1)}, u32[]{:S(2)}, u32[]{:S(2)}) collective-permute-start(bf16[1,512,512]{2,1,0:T(8,128)(2,1)S(1)} %weight_term.1), channel_id=1, source_target_pairs={{0,2},{1,3},{2,0},{3,1},{4,6},{5,7},{6,4},{7,5},{8,10},{9,11},{10,... | collective-permute-start | bytes 1572872 | tf_op jit(solution)/shard_map/ppermute | solution.py:441
  64.7 1.3 %collective-permute-start.10 = (bf16[512,128]{1,0:T(8,128)(2,1)S(1)}, bf16[512,128]{1,0:T(8,128)(2,1)S(1)}, u32[]{:S(2)}, u32[]{:S(2)}) collective-permute-start(bf16[512,128]{1,0:T(8,128)(2,1)S(1)} %get-tuple-element.55.st_ref.sc), channel_id=1, source_target_pairs={{8,0},{12,4},{16,8},{20,12},{24,16},{28,20},{9,1},{13,5},{17,9},{2... | collective-permute-start | bytes 393224 | tf_op jit(solution)/shard_map/ppermute | solution.py:25
  66.0 1.5 %collective-permute-start.9 = (bf16[512,128]{1,0:T(8,128)(2,1)S(1)}, bf16[512,128]{1,0:T(8,128)(2,1)S(1)}, u32[]{:S(2)}, u32[]{:S(2)}) collective-permute-start(bf16[512,128]{1,0:T(8,128)(2,1)S(1)} %get-tuple-element.55.st_ref.sc), channel_id=1, source_target_pairs={{4,0},{8,4},{12,8},{16,12},{20,16},{24,20},{28,24},{5,1},{9,5},{13... | collective-permute-start | bytes 393224 | tf_op jit(solution)/shard_map/ppermute | solution.py:25
  67.5 7.2 %query_kernel.2.rest_0_ = bf16[512,512]{1,0:T(8,128)(2,1)} custom-call(bf16[512,1024]{1,0:T(8,128)(2,1)S(1)} %queries_to_send.1.q_ref.g_ref.qc.gc, bf16[512,1024]{1,0:T(8,128)(2,1)S(1)} %queries_to_send.1.q_ref.g_ref.qc.gc, bf16[512,128]{1,0:T(8,128)(2,1)S(1)} %get-tuple-element.55.st_ref.sc, ...), custom_call_target="tpu_custom_call" | custom-call | bytes 24500000 | tf_op jit(solution)/shard_map/query_kernel/pallas_call | solution.py:287
  74.6 0.0 copy-done
  74.7 7.1 %query_kernel.3 = bf16[512,512]{1,0:T(8,128)(2,1)} custom-call(bf16[512,1024]{1,0:T(8,128)(2,1)S(1)} %queries_to_send.1.q_ref.g_ref.qc.gc, bf16[512,1024]{1,0:T(8,128)(2,1)S(1)} %queries_to_send.1.q_ref.g_ref.qc.gc, bf16[512,128]{1,0:T(8,128)(2,1)S(1)} %get-tuple-element.55.st_ref.sc, ...), custom_call_target="tpu_custom_call", output_to_operand_aliasing={{}: (15, {})} | custom-call | bytes 24500000 | tf_op jit(solution)/shard_map/query_kernel/pallas_call | solution.py:287
  81.8 0.0 collective-permute-done.10.se
  81.8 4.6 %collective-permute-done.9.sd = bf16[512,128]{1,0:T(8,128)(2,1)S(1)} collective-permute-done((bf16[512,128]{1,0:T(8,128)(2,1)S(1)}, bf16[512,128]{1,0:T(8,128)(2,1)S(1)}, u32[]{:S(2)}, u32[]{:S(2)}) %collective-permute-start.9) | collective-permute-done | bytes 131104 | tf_op jit(solution)/shard_map/ppermute | solution.py:25
  86.4 0.0 copy-start.5
  86.4 0.7 copy-done.5
  87.1 0.0 collective-permute-done.8.moved_ref
  87.1 2.4 %keep_term.1 = (bf16[4,64,512]{2,1,0:T(8,128)(2,1)S(1)}, f32[4,64,512]{2,1,0:T(8,128)S(1)}) custom-call(s32[3]{0:T(128)S(1)} %get-tuple-element.66.sel_ref, bf16[256,512]{1,0:T(8,128)(2,1)} %copy-done.2, bf16[256,512]{1,0:T(8,128)(2,1)} %copy-done.3, bf16[512,2048]{1,0:T(8,128)(2,1)} %bitcast.21, ...), custom_call_target="tpu_custom_call" | custom-call | bytes 10500000 | tf_op jit(solution)/shard_map/keep_term/pallas_call | solution.py:424
  89.4 0.1 collective-permute-start.11
  89.6 0.0 collective-permute-done.12.qd.gd
  89.6 0.0 copy-done.6
  89.6 8.1 %key_kernel.3 = (bf16[512,512]{1,0:T(8,128)(2,1)}, bf16[512,512]{1,0:T(8,128)(2,1)}) custom-call(bf16[528,512]{1,0:T(8,128)(2,1)S(1)} %pad_maximum_fusion.kc.vc.tc.k_ref.v_ref.t_ref, bf16[528,512]{1,0:T(8,128)(2,1)S(1)} %pad_maximum_fusion.kc.vc.tc.k_ref.v_ref.t_ref, bf16[528,512]{1,0:T(8,128)(2,1)S(1)} %pad_maximum_fusion.kc.vc.tc.k_ref.v_ref.t_ref, ...), custom_call_target="tpu_custom_call" | custom-call | bytes 29400000 | tf_op jit(solution)/shard_map/key_kernel/pallas_call | solution.py:287
  97.7 0.0 collective-permute-done.11.got_ref
  97.7 0.1 stage.2
  97.8 0.7 collective-permute-start.13
  98.5 4.9 %key_kernel.4 = (bf16[512,512]{1,0:T(8,128)(2,1)}, bf16[512,512]{1,0:T(8,128)(2,1)}) custom-call(bf16[528,512]{1,0:T(8,128)(2,1)S(1)} %pad_maximum_fusion.1.kc.vc.tc.k_ref.v_ref.t_ref, bf16[528,512]{1,0:T(8,128)(2,1)S(1)} %pad_maximum_fusion.1.kc.vc.tc.k_ref.v_ref.t_ref, ...), custom_call_target="tpu_custom_call", output_to_operand_aliasing={{0}: (12, {}), {1}: (13, {})} | custom-call | bytes 14700000 | tf_op jit(solution)/shard_map/key_kernel/pallas_call | solution.py:287
  103.4 0.0 collective-permute-done.13.got_ref
  103.4 3.4 %collective-permute-start.14 = (bf16[1,64,512]{2,1,0:T(8,128)(2,1)S(1)}, bf16[1,64,512]{2,1,0:T(8,128)(2,1)S(1)}, u32[]{:S(2)}, u32[]{:S(2)}) collective-permute-start(bf16[1,64,512]{2,1,0:T(8,128)(2,1)S(1)} %get-tuple-element.54), channel_id=1, source_target_pairs={{0,16},{4,20},{8,24},{12,28},{16,0},{20,4},{24,8},{28,12},{1,17},{... | collective-permute-start | bytes 196616 | tf_op jit(solution)/shard_map/ppermute | solution.py:441
  106.9 4.9 %key_kernel.5 = (bf16[512,512]{1,0:T(8,128)(2,1)}, bf16[512,512]{1,0:T(8,128)(2,1)}) custom-call(bf16[528,512]{1,0:T(8,128)(2,1)S(1)} %pad_maximum_fusion.1.kc.vc.tc.k_ref.v_ref.t_ref, bf16[528,512]{1,0:T(8,128)(2,1)S(1)} %pad_maximum_fusion.1.kc.vc.tc.k_ref.v_ref.t_ref, ...), custom_call_target="tpu_custom_call", output_to_operand_aliasing={{0}: (12, {}), {1}: (13, {})} | custom-call | bytes 14700000 | tf_op jit(solution)/shard_map/key_kernel/pallas_call | solution.py:287
  111.8 0.0 collective-permute-done.14
  111.8 0.7 last_sum.1
  (5 shorter events, 0.1 us)
Async XLA Ops:
  1.3 6.6 %copy-start.4 = (bf16[512,2048]{1,0:T(8,128)(2,1)S(1)}, bf16[512,2048]{1,0:T(8,128)(2,1)}, u32[]{:S(2)}) copy-start(bf16[512,2048]{1,0:T(8,128)(2,1)} %w_ref.1) | copy-start | bytes 6291460
  2.7 5.2 %copy-start.1 = (bf16[1,512,2048]{2,1,0:T(8,128)(2,1)S(1)}, bf16[1,512,2048]{2,1,0:T(8,128)(2,1)}, u32[]{:S(2)}) copy-start(bf16[1,512,2048]{2,1,0:T(8,128)(2,1)} %param.10) | copy-start | bytes 6291460
  2.8 18.2 %collective-permute-start.1 = (bf16[528,512]{1,0:T(8,128)(2,1)S(1)}, bf16[528,512]{1,0:T(8,128)(2,1)S(1)}, u32[]{:S(2)}, u32[]{:S(2)}) collective-permute-start(bf16[528,512]{1,0:T(8,128)(2,1)S(1)} %pad_maximum_fusion.kc.vc.tc.k_ref.v_ref.t_ref), channel_id=1, source_target_pairs={{0,8},{4,12},{8,16},{12,20},{16,24},{20,28},{1,9},{5,13},{9,17},{1... | collective-permute-start | bytes 1622024 | tf_op jit(solution)/shard_map/ppermute | solution.py:25
  8.0 1.0 copy-start.7
  10.8 63.8 %copy-start = (bf16[512,1024]{1,0:T(8,128)(2,1)}, bf16[512,1024]{1,0:T(8,128)(2,1)S(1)}, u32[]{:S(2)}) copy-start(bf16[512,1024]{1,0:T(8,128)(2,1)S(1)} %queries_to_send.1.q_ref.g_ref.qc.gc) | copy-start | bytes 3145732
  10.8 35.5 %collective-permute-start = (bf16[512,1024]{1,0:T(8,128)(2,1)S(1)}, bf16[512,1024]{1,0:T(8,128)(2,1)}, u32[]{:S(2)}, u32[]{:S(2)}) collective-permute-start(bf16[512,1024]{1,0:T(8,128)(2,1)S(1)} %queries_to_send.1.q_ref.g_ref.qc.gc), channel_id=1, source_target_pairs={{8,0},{12,4},{16,8},{20,12},{24,16},{28,20},{9,1},{13,5},{17,9},{2... | collective-permute-start | bytes 3145736 | tf_op jit(solution)/shard_map/ppermute | solution.py:25
  12.1 18.9 %collective-permute-start.4 = (bf16[528,512]{1,0:T(8,128)(2,1)S(1)}, bf16[528,512]{1,0:T(8,128)(2,1)S(1)}, u32[]{:S(2)}, u32[]{:S(2)}) collective-permute-start(bf16[528,512]{1,0:T(8,128)(2,1)S(1)} %pad_maximum_fusion.1.kc.vc.tc.k_ref.v_ref.t_ref), channel_id=1, source_target_pairs={{0,8},{4,12},{8,16},{12,20},{16,24},{20,28},{1,9},{5,13},{9,17},{1... | collective-permute-start | bytes 1622024 | tf_op jit(solution)/shard_map/ppermute | solution.py:25
  16.7 16.1 %collective-permute-start.2 = (bf16[528,512]{1,0:T(8,128)(2,1)S(1)}, bf16[528,512]{1,0:T(8,128)(2,1)}, u32[]{:S(2)}, u32[]{:S(2)}) collective-permute-start(bf16[528,512]{1,0:T(8,128)(2,1)S(1)} %pad_maximum_fusion.kc.vc.tc.k_ref.v_ref.t_ref), channel_id=1, source_target_pairs={{0,4},{8,12},{16,20},{24,28},{1,5},{9,13},{17,21},{25,29},{2,6},{1... | collective-permute-start | bytes 1622024 | tf_op jit(solution)/shard_map/ppermute | solution.py:446
  21.0 16.2 %collective-permute-start.3 = (bf16[528,512]{1,0:T(8,128)(2,1)S(1)}, bf16[528,512]{1,0:T(8,128)(2,1)}, u32[]{:S(2)}, u32[]{:S(2)}) collective-permute-start(bf16[528,512]{1,0:T(8,128)(2,1)S(1)} %collective-permute-done.1.ka.va.ta), channel_id=1, source_target_pairs={{4,0},{12,8},{20,16},{28,24},{5,1},{13,9},{21,17},{29,25},{6,2},{1... | collective-permute-start | bytes 1622024 | tf_op jit(solution)/shard_map/ppermute | solution.py:446
  22.3 26.4 %collective-permute-start.5 = (bf16[528,512]{1,0:T(8,128)(2,1)S(1)}, bf16[528,512]{1,0:T(8,128)(2,1)}, u32[]{:S(2)}, u32[]{:S(2)}) collective-permute-start(bf16[528,512]{1,0:T(8,128)(2,1)S(1)} %pad_maximum_fusion.1.kc.vc.tc.k_ref.v_ref.t_ref), channel_id=1, source_target_pairs={{0,4},{8,12},{16,20},{24,28},{1,5},{9,13},{17,21},{25,29},{2,6},{1... | collective-permute-start | bytes 1622024 | tf_op jit(solution)/shard_map/ppermute | solution.py:446
  31.0 17.7 %collective-permute-start.6 = (bf16[528,512]{1,0:T(8,128)(2,1)S(1)}, bf16[528,512]{1,0:T(8,128)(2,1)}, u32[]{:S(2)}, u32[]{:S(2)}) collective-permute-start(bf16[528,512]{1,0:T(8,128)(2,1)S(1)} %collective-permute-done.4.ka.va.ta), channel_id=1, source_target_pairs={{4,0},{12,8},{20,16},{28,24},{5,1},{13,9},{21,17},{29,25},{6,2},{1... | collective-permute-start | bytes 1622024 | tf_op jit(solution)/shard_map/ppermute | solution.py:446
  43.4 3.0 %copy-start.2 = (bf16[256,512]{1,0:T(8,128)(2,1)}, bf16[256,512]{1,0:T(8,128)(2,1)S(1)}, u32[]{:S(2)}) copy-start(bf16[256,512]{1,0:T(8,128)(2,1)S(1)} %get-tuple-element.35.o_ref.refs_0_.o0_ref) | copy-start | bytes 786436
  54.9 2.9 %copy-start.3 = (bf16[256,512]{1,0:T(8,128)(2,1)}, bf16[256,512]{1,0:T(8,128)(2,1)S(1)}, u32[]{:S(2)}) copy-start(bf16[256,512]{1,0:T(8,128)(2,1)S(1)} %get-tuple-element.40.o_ref.refs_1_.o1_ref) | copy-start | bytes 786436
  57.8 3.0 %collective-permute-start.7 = (bf16[2,512,512]{2,1,0:T(8,128)(2,1)}, bf16[2,512,512]{2,1,0:T(8,128)(2,1)}, u32[]{:S(2)}, u32[]{:S(2)}) collective-permute-start(bf16[2,512,512]{2,1,0:T(8,128)(2,1)} %first_term.3), channel_id=1, source_target_pairs={{0,1},{1,0},{2,3},{3,2},{4,5},{5,4},{6,7},{7,6},{8,9},{9,8},{10,11... | collective-permute-start | bytes 3145736 | tf_op jit(solution)/shard_map/ppermute | solution.py:441
  57.8 31.8 %collective-permute-start.12 = (bf16[512,1024]{1,0:T(8,128)(2,1)}, bf16[512,1024]{1,0:T(8,128)(2,1)}, u32[]{:S(2)}, u32[]{:S(2)}) collective-permute-start(bf16[512,1024]{1,0:T(8,128)(2,1)} %broadcast_select_fusion), channel_id=1, source_target_pairs={{0,4},{4,0},{8,12},{12,8},{16,20},{20,16},{24,28},{28,24},{1,5},{5... | collective-permute-start | bytes 3145736 | tf_op jit(solution)/shard_map/ppermute | solution.py:441
  63.2 23.9 %collective-permute-start.8 = (bf16[1,512,512]{2,1,0:T(8,128)(2,1)S(1)}, bf16[1,512,512]{2,1,0:T(8,128)(2,1)S(1)}, u32[]{:S(2)}, u32[]{:S(2)}) collective-permute-start(bf16[1,512,512]{2,1,0:T(8,128)(2,1)S(1)} %weight_term.1), channel_id=1, source_target_pairs={{0,2},{1,3},{2,0},{3,1},{4,6},{5,7},{6,4},{7,5},{8,10},{9,11},{10,... | collective-permute-start | bytes 1572872 | tf_op jit(solution)/shard_map/ppermute | solution.py:441
  64.7 17.1 %collective-permute-start.10 = (bf16[512,128]{1,0:T(8,128)(2,1)S(1)}, bf16[512,128]{1,0:T(8,128)(2,1)S(1)}, u32[]{:S(2)}, u32[]{:S(2)}) collective-permute-start(bf16[512,128]{1,0:T(8,128)(2,1)S(1)} %get-tuple-element.55.st_ref.sc), channel_id=1, source_target_pairs={{8,0},{12,4},{16,8},{20,12},{24,16},{28,20},{9,1},{13,5},{17,9},{2... | collective-permute-start | bytes 393224 | tf_op jit(solution)/shard_map/ppermute | solution.py:25
  66.0 20.4 %collective-permute-start.9 = (bf16[512,128]{1,0:T(8,128)(2,1)S(1)}, bf16[512,128]{1,0:T(8,128)(2,1)S(1)}, u32[]{:S(2)}, u32[]{:S(2)}) collective-permute-start(bf16[512,128]{1,0:T(8,128)(2,1)S(1)} %get-tuple-element.55.st_ref.sc), channel_id=1, source_target_pairs={{4,0},{8,4},{12,8},{16,12},{20,16},{24,20},{28,24},{5,1},{9,5},{13... | collective-permute-start | bytes 393224 | tf_op jit(solution)/shard_map/ppermute | solution.py:25
  86.4 0.7 copy-start.5
  87.1 2.5 %copy-start.6 = (bf16[512,128]{1,0:T(8,128)(2,1)S(1)}, bf16[512,128]{1,0:T(8,128)(2,1)}, u32[]{:S(2)}) copy-start(bf16[512,128]{1,0:T(8,128)(2,1)} %copy-done.5) | copy-start | bytes 393220
  89.4 8.2 %collective-permute-start.11 = (bf16[4,64,512]{2,1,0:T(8,128)(2,1)S(1)}, bf16[4,64,512]{2,1,0:T(8,128)(2,1)S(1)}, u32[]{:S(2)}, u32[]{:S(2)}) collective-permute-start(bf16[4,64,512]{2,1,0:T(8,128)(2,1)S(1)} %get-tuple-element.43), channel_id=1, source_target_pairs={{0,4},{4,0},{8,12},{12,8},{16,20},{20,16},{24,28},{28,24},{1,5},{5... | collective-permute-start | bytes 786440 | tf_op jit(solution)/shard_map/ppermute | solution.py:441
  97.8 5.6 %collective-permute-start.13 = (bf16[2,64,512]{2,1,0:T(8,128)(2,1)S(1)}, bf16[2,64,512]{2,1,0:T(8,128)(2,1)S(1)}, u32[]{:S(2)}, u32[]{:S(2)}) collective-permute-start(bf16[2,64,512]{2,1,0:T(8,128)(2,1)S(1)} %get-tuple-element.49), channel_id=1, source_target_pairs={{0,8},{4,12},{8,0},{12,4},{16,24},{20,28},{24,16},{28,20},{1,9},{5... | collective-permute-start | bytes 393224 | tf_op jit(solution)/shard_map/ppermute | solution.py:441
  103.4 8.4 %collective-permute-start.14 = (bf16[1,64,512]{2,1,0:T(8,128)(2,1)S(1)}, bf16[1,64,512]{2,1,0:T(8,128)(2,1)S(1)}, u32[]{:S(2)}, u32[]{:S(2)}) collective-permute-start(bf16[1,64,512]{2,1,0:T(8,128)(2,1)S(1)} %get-tuple-element.54), channel_id=1, source_target_pairs={{0,16},{4,20},{8,24},{12,28},{16,0},{20,4},{24,8},{28,12},{1,17},{... | collective-permute-start | bytes 196616 | tf_op jit(solution)/shard_map/ppermute | solution.py:441
